TPU v7x, 32 devices: a whole 2x2x4 slice. The times are simulated.
32 devices in a mesh: gx: 8 (over z, x), gy: 4 (over y, core).
Axes of the slice: x: 2, y: 2, z: 4, core: 2. Of those that a mesh axis runs over, the one named last changes fastest.
Arguments:
- populations: float32 [19, 256, 2048], P(None, 'gx', 'gy'), may hold values from 0 to 0.7, as said below
- positions: float32 [768, 3, 642], P(('gx', 'gy')), may hold values from -3 to 31, as said below
- stiffness: float32 [768], P(('gx', 'gy')), may hold values from 0.002 to 0.02
- membrane_shape: float32 [3, 642], replicated, may hold values from -6 to 6
- neighbours: int32 [642, 6], replicated, may hold values from 0 to 641, as said below
- home_tile: int32 [768], P(('gx', 'gy')), may hold values from 0 to 31, as said below
Outputs:
- populations_out: float32 [19, 256, 2048], P(None, 'gx', 'gy')
- displacement: float32 [768, 3, 642], P(('gx', 'gy'))
- force_density: float32 [3, 256, 2048], P(None, 'gx', 'gy')
Inputs may be any that keep to these rules, and one draw needn't show every extreme that they name: `populations`: every entry is positive. `positions`: the first coordinate lies within [1, 31], the second within [1, 31]; the third is taken modulo 16. `neighbours`: row v never names v. `home_tile`: cells are owned in blocks of 24 in gx+gy order; the home tile of a cell owned at gx index a has gx index a - 1, a or a + 1 (cyclically) and any gy index, numbered gx index times the number of gy devices plus gy index; at most 4 cells of one device share a home tile, and in every device some home tile has exactly 4 of them.
All inputs are finite; a program needn't handle non-finite values.
Results may differ from a plain program's by a relative error of at most 0.0022.
Values sent between devices are 32-bit elements; how exact they have to be, the bound alone decides.
No kernel may reach another device: no remote copies, remote signals or barrier semaphores. Data moves between devices by JAX's collectives and lax.ppermute only.
A program may use at most 64 MiB of HBM per device.

v0:
```python
import functools

import jax
import jax.numpy as jnp
from jax import lax
from jax.experimental import pallas as pl
from jax.experimental.pallas import tpu as pltpu
from jax.sharding import PartitionSpec as P

CZ = 16
CAP = 4
STEPS = 2

LATTICE_VELOCITY = [
    [0, 0, 0],
    [1, 0, 0],
    [-1, 0, 0],
    [0, 1, 0],
    [0, -1, 0],
    [0, 0, 1],
    [0, 0, -1],
    [1, 1, 0],
    [-1, -1, 0],
    [1, -1, 0],
    [-1, 1, 0],
    [1, 0, 1],
    [-1, 0, -1],
    [1, 0, -1],
    [-1, 0, 1],
    [0, 1, 1],
    [0, -1, -1],
    [0, 1, -1],
    [0, -1, 1],
]
LATTICE_WEIGHT = [1.0 / 3.0] + [1.0 / 18.0] * 6 + [1.0 / 36.0] * 12
RIGHT_MOVERS = [1, 7, 9, 11, 13]
LEFT_MOVERS = [2, 8, 10, 12, 14]
UPWARD_MOVERS = [3, 7, 10, 15, 17]
DOWNWARD_MOVERS = [4, 8, 9, 16, 18]
RELAX_RATE = 1.25
PUSH_SCALE = 0.05
TETHER_GAIN = 2.0
LANES = 128
F32 = jnp.float32
BF16 = jnp.bfloat16
SMEM = pltpu.SMEM
VMEM = pltpu.VMEM


def spec(space):
    return pl.BlockSpec(memory_space=space)


def call(kernel, outs, ins, scratch=(), cost=None, limit=None):
    return pl.pallas_call(
        kernel,
        out_shape=[jax.ShapeDtypeStruct(s, d) for s, d, _ in outs],
        in_specs=[spec(m) for m in ins],
        out_specs=[spec(m) for _, _, m in outs],
        scratch_shapes=list(scratch),
        compiler_params=pltpu.CompilerParams(vmem_limit_bytes=limit or (24 << 20)),
        cost_estimate=cost,
    )


def lane_index(shape):
    return lax.broadcasted_iota(jnp.int32, shape, len(shape) - 1)


def row_index(shape):
    return lax.broadcasted_iota(jnp.int32, shape, len(shape) - 2)


class Sizes:
    def __init__(self, cells, vertices, width_x, plane, devices_x, devices_y):
        self.cells = cells
        self.vertices = vertices
        self.width_x = width_x
        self.plane = plane
        self.devices_x = devices_x
        self.devices_y = devices_y
        self.main = vertices - vertices % LANES
        self.tail = vertices - self.main
        self.full = self.main + LANES
        self.message = 3 * self.main + LANES
        self.center = devices_y * CAP
        self.slots = 3 * devices_y * CAP
        self.width_y = plane // CZ


def cell_places(z, home_ref, count_ref):
    own_x = lax.axis_index("gx")
    own_y = lax.axis_index("gy")
    for g in range(3 * z.devices_y):
        count_ref[g] = 0
    found = []
    for n in range(z.cells):
        home = home_ref[n]
        target_x = lax.div(home, z.devices_y)
        target_y = lax.rem(home, z.devices_y)
        side = lax.rem(target_x - own_x + 1 + z.devices_x, z.devices_x)
        turn = lax.rem(target_y - own_y + z.devices_y, z.devices_y)
        group = side * z.devices_y + turn
        rank = count_ref[group]
        count_ref[group] = rank + 1
        found.append((group, rank))
    return found


def pack_kernel(z, home_ref, stiff_ref, places_ref, *rest):
    left_ref, right_ref = rest[:2]
    center_refs = rest[2 : 2 + z.devices_y]
    table_ref, count_ref = rest[2 + z.devices_y :]
    table_ref[...] = jnp.zeros_like(table_ref)
    lane = lane_index((1, LANES))
    zeros = jnp.zeros((1, LANES - z.tail), F32)
    for n, (group, rank) in enumerate(cell_places(z, home_ref, count_ref)):
        ends = jnp.where(lane == 3 * z.tail, stiff_ref[n], 0.0)
        parts = []
        for c in range(3):
            line = places_ref[n, c : c + 1, :]
            parts.append(line[:, : z.main])
            end = jnp.concatenate([line[:, z.main :], zeros], axis=1)
            ends = ends + (end if c == 0 else pltpu.roll(end, c * z.tail, 1))
        table_ref[group, pl.ds(rank, 1), :] = jnp.concatenate(parts + [ends], axis=1)
    d = z.devices_y
    left_ref[...] = table_ref[0:d]
    right_ref[...] = table_ref[2 * d : 3 * d]
    for r in range(d):
        center_refs[r][...] = table_ref[d + r]


def unpack_kernel(z, home_ref, places_ref, left_ref, right_ref, *rest):
    center_refs = rest[: z.devices_y]
    out_ref, table_ref, count_ref = rest[z.devices_y :]
    d = z.devices_y
    table_ref[0:d] = left_ref[...]
    table_ref[2 * d : 3 * d] = right_ref[...]
    for r in range(d):
        table_ref[d + r] = center_refs[r][...]
    for n, (group, rank) in enumerate(cell_places(z, home_ref, count_ref)):
        line = table_ref[group, pl.ds(rank, 1), :]
        ends = line[:, 3 * z.main :]
        for c in range(3):
            end = ends if c == 0 else pltpu.roll(ends, LANES - c * z.tail, 1)
            whole = jnp.concatenate([line[:, c * z.main : (c + 1) * z.main], end], axis=1)
            out_ref[n, c : c + 1, :] = whole[:, : z.vertices] - places_ref[n, c : c + 1, :]


def matrix_kernel(z, near_ref, near_t_ref, link_ref, degree_ref):
    near = near_ref[...]
    near_t = near_t_ref[...]
    count = near.shape[1]
    lane = lane_index((z.full, LANES))
    row = row_index((z.full, LANES))
    for t in range(z.full // LANES):
        total = jnp.zeros((z.full, LANES), F32)
        for b in range(count):
            total += jnp.where(near[:, b : b + 1] == lane + t * LANES, 1.0, 0.0)
            total += jnp.where(near_t[b : b + 1, t * LANES : (t + 1) * LANES] == row, 1.0, 0.0)
        link_ref[:, t * LANES : (t + 1) * LANES] = total.astype(BF16)
        degree_ref[:, t * LANES : (t + 1) * LANES] = (
            jnp.sum(total, axis=0, keepdims=True) + TETHER_GAIN
        )


def list_active(flags, first, last, ids_ref, start, count_at):
    def step(s, state):
        count, empty = state
        filled = flags(s) > 0.0

        @pl.when(filled)
        def _():
            ids_ref[start + count] = s

        return (
            jnp.where(filled, count + 1, count),
            jnp.where(filled, empty, s),
        )

    count, empty = lax.fori_loop(first, last, step, (jnp.int32(0), jnp.int32(first)))

    @pl.when(lax.rem(count, 2) == 1)
    def _():
        ids_ref[start + count] = empty

    ids_ref[count_at] = lax.div(count + 1, 2)


def split_message(z, line_ref, at, places_ref, ends_ref, slot):
    value = line_ref[...] if at is None else line_ref[at]
    for c in range(3):
        places_ref[c, slot : slot + CAP, : z.main] = value[:, c * z.main : (c + 1) * z.main]
    ends_ref[slot : slot + CAP, :] = value[:, 3 * z.main :]


def place_tails(z, ends_ref, places_ref, stiff_ref):
    ends = ends_ref[...]
    lane = lane_index(ends.shape)
    for c in range(3):
        end = ends if c == 0 else pltpu.roll(ends, LANES - c * z.tail, 1)
        places_ref[c, :, z.main :] = jnp.where(lane < z.tail, end, 0.0)
    stiff_ref[...] = jnp.broadcast_to(ends[:, 3 * z.tail : 3 * z.tail + 1], ends.shape)


def forces(z, places_ref, stiff_ref, shape_ref, link_ref, degree_ref, force_ref):
    rows = places_ref.shape[1]
    lane = lane_index((rows, z.full))
    inside = lane < z.vertices
    parts = []
    for c in range(3):
        x = places_ref[c]
        mean = jnp.sum(x, axis=1, keepdims=True) * (1.0 / z.vertices)
        parts.append(jnp.where(inside, x - mean - shape_ref[c : c + 1, :], 0.0))
    strain = jnp.concatenate(parts, axis=0)
    high = strain.astype(BF16)
    rest = strain - high.astype(F32)
    low = rest.astype(BF16)
    link = link_ref[...]
    linked = jnp.dot(high, link, preferred_element_type=F32) + jnp.dot(
        low, link, preferred_element_type=F32
    )
    pulled = degree_ref[...] * (high.astype(F32) + low.astype(F32)) - linked
    stiff = stiff_ref[:, 0:1]
    for c in range(3):
        force_ref[c] = -stiff * pulled[c * rows : (c + 1) * rows]


def tails_to_lanes(z, ref, c):
    ends = ref[c, :, z.main :]
    lane = lane_index(ends.shape)
    row = row_index(ends.shape)
    picked = jnp.zeros_like(ends)
    for t in range(z.tail):
        picked = jnp.where(lane == row * z.tail + t, ends[:, t : t + 1], picked)
    return jnp.sum(picked, axis=0, keepdims=True)


def hat_tables(z, x, y, depth, plane_ref, at):
    width = x.shape[1]
    steps_x = row_index((z.width_x, width)).astype(F32)
    steps_y = steps_x if z.width_y == z.width_x else row_index((z.width_y, width)).astype(F32)
    steps_z = row_index((CZ, width)).astype(F32)
    hat_x = jnp.maximum(0.0, 1.0 - jnp.abs(x - steps_x))
    hat_y = jnp.maximum(0.0, 1.0 - jnp.abs(y - steps_y))
    wrapped = depth - CZ * jnp.floor(depth * (1.0 / CZ))
    gap = jnp.abs(wrapped - steps_z)
    hat_z = jnp.maximum(0.0, 1.0 - jnp.minimum(gap, CZ - gap))
    for j in range(z.width_y):
        plane_ref[j * CZ : (j + 1) * CZ, at : at + width] = (hat_y[j : j + 1] * hat_z).astype(BF16)
    return hat_x


def spread(z, places_ref, force_ref, ids_ref, start, pairs, grid_ref, plane_ref, lift_ref, tails):
    def contract(width):
        return lax.dot_general(
            lift_ref[:, :width],
            plane_ref[:, :width],
            (((1,), (1,)), ((), ())),
            preferred_element_type=F32,
        )

    def fill(line, pull, at):
        hat_x = hat_tables(z, *line, plane_ref, at)
        width = line[0].shape[1]
        for c in range(3):
            lift_ref[c * z.width_x : (c + 1) * z.width_x, at : at + width] = (
                pull[c] * hat_x
            ).astype(BF16)

    def step(p, carry):
        for h in range(2):
            s = ids_ref[start + 2 * p + h]
            line = [places_ref[c, pl.ds(s, 1), : z.main] for c in range(3)]
            pull = [force_ref[c, pl.ds(s, 1), : z.main] for c in range(3)]
            fill(line, pull, h * z.main)
        grid_ref[...] += contract(2 * z.main)
        return carry

    lax.fori_loop(0, pairs, step, 0)
    if tails:
        line = [tails_to_lanes(z, places_ref, c) for c in range(3)]
        pull = [tails_to_lanes(z, force_ref, c) for c in range(3)]
        fill(line, pull, 0)
        grid_ref[...] += contract(LANES)


def sample(z, places_ref, flow_ref, ids_ref, start, pairs, plane_ref):
    def step(p, carry):
        hats = []
        slots = [ids_ref[start + 2 * p + h] for h in range(2)]
        lines = [[places_ref[c, pl.ds(s, 1), : z.main] for c in range(3)] for s in slots]
        for h in range(2):
            hats.append(hat_tables(z, *lines[h], plane_ref, h * z.main))
        picked = jnp.dot(
            flow_ref[...], plane_ref[:, : 2 * z.main], preferred_element_type=F32
        )
        for h in range(2):
            for c in range(3):
                part = picked[
                    c * z.width_x : (c + 1) * z.width_x, h * z.main : (h + 1) * z.main
                ]
                drift = jnp.sum(part * hats[h], axis=0, keepdims=True)
                places_ref[c, pl.ds(slots[h], 1), : z.main] = lines[h][c] + drift
        return carry

    lax.fori_loop(0, pairs, step, 0)


def sample_tails(z, places_ref, flow_ref, plane_ref):
    line = [tails_to_lanes(z, places_ref, c) for c in range(3)]
    hat_x = hat_tables(z, *line, plane_ref, 0)
    picked = jnp.dot(flow_ref[...], plane_ref[:, :LANES], preferred_element_type=F32)
    rows = places_ref.shape[1]
    lane = lane_index((rows, LANES))
    row = row_index((rows, LANES))
    for c in range(3):
        drift = jnp.sum(picked[c * z.width_x : (c + 1) * z.width_x] * hat_x, axis=0, keepdims=True)
        ends = places_ref[c, :, z.main :]
        for t in range(z.tail):
            moved = jnp.sum(
                jnp.where(lane == row * z.tail + t, drift, 0.0), axis=1, keepdims=True
            )
            ends = jnp.where(lane == t, ends + moved, ends)
        places_ref[c, :, z.main :] = ends


def collide(z, flow_ref, grid_ref, post_ref):
    def block(r, carry):
        rows = pl.ds(pl.multiple_of(r * 8, 8), 8)
        for t in range(z.plane // LANES):
            lanes = slice(t * LANES, (t + 1) * LANES)
            f = [flow_ref[q, rows, lanes] for q in range(19)]
            push = [
                PUSH_SCALE
                * grid_ref[pl.ds(pl.multiple_of(c * z.width_x + r * 8, 8), 8), lanes]
                for c in range(3)
            ]
            density = f[0]
            for q in range(1, 19):
                density = density + f[q]
            inverse = 1.0 / density
            u = []
            for c in range(3):
                m = 0.5 * push[c]
                for q in range(1, 19):
                    v = LATTICE_VELOCITY[q][c]
                    if v == 1:
                        m = m + f[q]
                    elif v == -1:
                        m = m - f[q]
                u.append(m * inverse)
            square = u[0] * u[0] + u[1] * u[1] + u[2] * u[2]
            work = u[0] * push[0] + u[1] * push[1] + u[2] * push[2]
            gain = 1.0 - 0.5 * RELAX_RATE
            heavy = RELAX_RATE * density
            base = heavy * (1.0 - 1.5 * square) - (3.0 * gain) * work
            post_ref[0, rows, lanes] = (1.0 - RELAX_RATE) * f[0] + LATTICE_WEIGHT[0] * base
            for q in range(1, 19, 2):
                along = None
                pull = None
                for c in range(3):
                    v = LATTICE_VELOCITY[q][c]
                    if v:
                        along = v * u[c] if along is None else along + v * u[c]
                        pull = v * push[c] if pull is None else pull + v * push[c]
                w = LATTICE_WEIGHT[q]
                lifted = heavy * along
                even = w * (base + along * (4.5 * lifted + (9.0 * gain) * pull))
                odd = (3.0 * w) * (lifted + gain * pull)
                post_ref[q, rows, lanes] = (1.0 - RELAX_RATE) * f[q] + (even + odd)
                post_ref[q + 1, rows, lanes] = (1.0 - RELAX_RATE) * f[q + 1] + (even - odd)
        return carry

    lax.fori_loop(0, z.width_x // 8, block, 0)


def write_edges(z, post_ref, right_ref, left_ref, up_ref, down_ref):
    for number, q in enumerate(RIGHT_MOVERS):
        right_ref[number : number + 1, :] = post_ref[q, z.width_x - 1 : z.width_x, :]
    for number, q in enumerate(LEFT_MOVERS):
        left_ref[number : number + 1, :] = post_ref[q, 0:1, :]
    right_ref[5:8, :] = jnp.zeros((3, z.plane), F32)
    left_ref[5:8, :] = jnp.zeros((3, z.plane), F32)
    lane = lane_index((z.width_x, LANES))
    up = jnp.zeros((z.width_x, LANES), F32)
    down = jnp.zeros((z.width_x, LANES), F32)
    for number, q in enumerate(UPWARD_MOVERS):
        here = (lane >= number * CZ) & (lane < (number + 1) * CZ)
        value = post_ref[q, :, z.plane - LANES :]
        up = jnp.where(here, pltpu.roll(value, (number + 1) * CZ, 1), up)
    for number, q in enumerate(DOWNWARD_MOVERS):
        here = (lane >= number * CZ) & (lane < (number + 1) * CZ)
        value = post_ref[q, :, :LANES]
        down = jnp.where(here, value if number == 0 else pltpu.roll(value, number * CZ, 1), down)
    up_ref[...] = up
    down_ref[...] = down


def stream(z, post_ref, from_left_ref, from_right_ref, below_ref, above_ref, out_ref, grid_ref, flow_ref):
    shape = (z.width_x, z.plane)
    lane = lane_index(shape)
    row = row_index(shape)
    edge_row = row_index((z.width_x, LANES))
    layer = lax.rem(lane, CZ)
    last_row = z.width_x - 1
    sums = [None] * 4
    for q in range(19):
        cx, cy, cz = LATTICE_VELOCITY[q]
        value = post_ref[q]
        if cx == 1:
            k = RIGHT_MOVERS.index(q)
            value = jnp.where(row == 0, from_left_ref[k : k + 1, :], pltpu.roll(value, 1, 0))
        elif cx == -1:
            k = LEFT_MOVERS.index(q)
            value = jnp.where(
                row == last_row, from_right_ref[k : k + 1, :], pltpu.roll(value, last_row, 0)
            )
        if cy:
            edges = below_ref if cy == 1 else above_ref
            k = (UPWARD_MOVERS if cy == 1 else DOWNWARD_MOVERS).index(q)
            edge = edges[: z.width_x, :]
            shift = (LANES - k * CZ if cy == 1 else 2 * LANES - (k + 1) * CZ) % LANES
            edge = edge if shift == 0 else pltpu.roll(edge, shift, 1)
            if cx:
                movers = RIGHT_MOVERS if cx == 1 else LEFT_MOVERS
                at = z.width_x + (0 if cx == 1 else 8) + movers.index(q)
                corner = edges[at : at + 1, :]
                turn = CZ if cy == 1 else LANES - CZ
                corner = pltpu.roll(corner, turn, 1)
                if cx == 1:
                    edge = jnp.where(edge_row == 0, corner, pltpu.roll(edge, 1, 0))
                else:
                    edge = jnp.where(edge_row == last_row, corner, pltpu.roll(edge, last_row, 0))
            rest = jnp.zeros((z.width_x, z.plane - LANES), F32)
            if cy == 1:
                wide = jnp.concatenate([edge, rest], axis=1)
                value = jnp.where(lane < CZ, wide, pltpu.roll(value, CZ, 1))
            else:
                wide = jnp.concatenate([rest, edge], axis=1)
                value = jnp.where(lane >= z.plane - CZ, wide, pltpu.roll(value, z.plane - CZ, 1))
        if cz == 1:
            value = jnp.where(
                layer == 0, pltpu.roll(value, z.plane - (CZ - 1), 1), pltpu.roll(value, 1, 1)
            )
        elif cz == -1:
            value = jnp.where(
                layer == CZ - 1, pltpu.roll(value, CZ - 1, 1), pltpu.roll(value, z.plane - 1, 1)
            )
        out_ref[q] = value
    for r in range(z.width_x // 8):
        rows = slice(r * 8, (r + 1) * 8)
        for t in range(z.plane // LANES):
            lanes = slice(t * LANES, (t + 1) * LANES)
            f = [out_ref[q, rows, lanes] for q in range(19)]
            density = f[0]
            for q in range(1, 19):
                density = density + f[q]
            inverse = 1.0 / density
            for c in range(3):
                m = (0.5 * PUSH_SCALE) * grid_ref[
                    c * z.width_x + r * 8 : c * z.width_x + (r + 1) * 8, lanes
                ]
                for q in range(1, 19):
                    v = LATTICE_VELOCITY[q][c]
                    if v == 1:
                        m = m + f[q]
                    elif v == -1:
                        m = m - f[q]
                sums[c] = m * inverse
            for c in range(3):
                flow_ref[c * z.width_x + r * 8 : c * z.width_x + (r + 1) * 8, lanes] = sums[c]


IDS = 128


def layout(z):
    return (0, 2), (1, 2 + z.center)


def read_flags(z, refs, flags_ref, sem):
    copies = []
    for g, (ref, at) in enumerate(refs):
        view = ref if at is None else ref.at[at]
        copies.append(
            pltpu.make_async_copy(
                view.at[:, pl.ds(3 * z.main, LANES)], flags_ref.at[g], sem.at[g]
            )
        )
    return copies


def center_kernel(z, *refs):
    d = z.devices_y
    center = refs[:d]
    shape_ref, link_ref, degree_ref, grid_ref = refs[d : d + 4]
    places, ends, stiff, force, plane, lift, flags, ids, sem = refs[d + 4 :]
    copies = read_flags(z, [(r, None) for r in center], flags, sem)
    for copy in copies:
        copy.start()
    for e in range(d):
        split_message(z, center[e], None, places, ends, e * CAP)
    place_tails(z, ends, places, stiff)
    forces(z, places, stiff, shape_ref, link_ref, degree_ref, force)
    grid_ref[...] = jnp.zeros_like(grid_ref)
    for copy in copies:
        copy.wait()
    (count_at, start), _ = layout(z)
    list_active(
        lambda s: flags[lax.div(s, CAP), lax.rem(s, CAP), 3 * z.tail], 0, z.center, ids, start, count_at
    )
    spread(z, places, force, ids, start, ids[count_at], grid_ref, plane, lift, True)


def sides_kernel(z, *refs):
    d = z.devices_y
    center, sides = refs[:d], refs[d : 2 * d]
    shape_ref, link_ref, degree_ref, part_ref, flow_ref = refs[2 * d : 2 * d + 5]
    (
        grid_ref,
        post_ref,
        right_ref,
        left_ref,
        up_ref,
        down_ref,
        places_ref,
        stiff_ref,
        ids_ref,
    ) = refs[2 * d + 5 : 2 * d + 14]
    ends, side_places, side_ends, side_stiff, force, plane, lift, flags, sem = refs[2 * d + 14 :]
    sources = [(r, None) for r in center]
    for e in range(d):
        sources += [(sides[e], 0), (sides[e], 1)]
    copies = read_flags(z, sources, flags, sem)
    for copy in copies:
        copy.start()
    for g, (ref, at) in enumerate(sources):
        split_message(z, ref, at, places_ref, ends, g * CAP)
        if g >= d:
            split_message(z, ref, at, side_places, side_ends, (g - d) * CAP)
    place_tails(z, ends, places_ref, stiff_ref)
    place_tails(z, side_ends, side_places, side_stiff)
    forces(z, side_places, side_stiff, shape_ref, link_ref, degree_ref, force)
    grid_ref[...] = part_ref[...]
    for copy in copies:
        copy.wait()
    flag = lambda s: flags[lax.div(s, CAP), lax.rem(s, CAP), 3 * z.tail]
    (center_count, center_start), (side_count, side_start) = layout(z)
    list_active(flag, 0, z.center, ids_ref, center_start, center_count)
    list_active(
        lambda s: flag(s + z.center), 0, z.slots - z.center, ids_ref, side_start, side_count
    )
    spread(z, side_places, force, ids_ref, side_start, ids_ref[side_count], grid_ref, plane, lift, True)
    collide(z, flow_ref, grid_ref, post_ref)
    write_edges(z, post_ref, right_ref, left_ref, up_ref, down_ref)


def copy_ids(z, ids_ref, out_ref):
    (center_count, center_start), (side_count, side_start) = layout(z)
    out_ref[center_count] = ids_ref[center_count]
    out_ref[side_count] = ids_ref[side_count]

    def one(i, carry):
        out_ref[center_start + i] = ids_ref[center_start + i]
        return carry

    def other(i, carry):
        out_ref[side_start + i] = ids_ref[side_start + i] + z.center
        return carry

    lax.fori_loop(0, 2 * ids_ref[center_count], one, 0)
    lax.fori_loop(0, 2 * ids_ref[side_count], other, 0)


def middle_kernel(z, *refs):
    (
        post_ref,
        from_left,
        from_right,
        below,
        above,
        old_grid,
        old_places,
        stiff_ref,
        ids_ref,
        shape_ref,
        link_ref,
        degree_ref,
    ) = refs[:12]
    grid_ref, next_ref, right_ref, left_ref, up_ref, down_ref, places_ref = refs[12:19]
    moved, flow32, flow, force, plane, lift, ids = refs[19:]
    copy_ids(z, ids_ref, ids)
    places_ref[...] = old_places[...]
    stream(z, post_ref, from_left, from_right, below, above, moved, old_grid, flow32)
    flow[...] = flow32[...].astype(BF16)
    grid_ref[...] = jnp.zeros_like(grid_ref)
    lists = layout(z)
    sample_tails(z, places_ref, flow, plane)
    for count_at, start in lists:
        sample(z, places_ref, flow, ids, start, ids[count_at], plane)
    forces(z, places_ref, stiff_ref, shape_ref, link_ref, degree_ref, force)
    for number, (count_at, start) in enumerate(lists):
        spread(
            z, places_ref, force, ids, start, ids[count_at], grid_ref, plane, lift, number == 0
        )
    collide(z, moved, grid_ref, next_ref)
    write_edges(z, next_ref, right_ref, left_ref, up_ref, down_ref)


def join_message(z, places_ref, slot, out_ref, at):
    lane = lane_index((CAP, LANES))
    ends = jnp.zeros((CAP, LANES), F32)
    for c in range(3):
        line = places_ref[c, slot : slot + CAP, :]
        lanes = slice(c * z.main, (c + 1) * z.main)
        if at is None:
            out_ref[:, lanes] = line[:, : z.main]
        else:
            out_ref[at, :, lanes] = line[:, : z.main]
        end = jnp.where(lane < z.tail, line[:, z.main :], 0.0)
        ends = ends + (end if c == 0 else pltpu.roll(end, c * z.tail, 1))
    if at is None:
        out_ref[:, 3 * z.main :] = ends
    else:
        out_ref[at, :, 3 * z.main :] = ends


def last_sides_kernel(z, *refs):
    d = z.devices_y
    (post_ref, from_left, from_right, below, above, grid_ref, old_places, ids_ref) = refs[:8]
    moved_ref, flow_ref, tail_places_ref = refs[8:11]
    side_refs = refs[11 : 11 + d]
    flow32, places, plane, ids = refs[11 + d :]
    copy_ids(z, ids_ref, ids)
    places[...] = old_places[...]
    stream(z, post_ref, from_left, from_right, below, above, moved_ref, grid_ref, flow32)
    flow_ref[...] = flow32[...].astype(BF16)
    sample_tails(z, places, flow_ref, plane)
    _, (count_at, start) = layout(z)
    sample(z, places, flow_ref, ids, start, ids[count_at], plane)
    for e in range(d):
        for h in range(2):
            join_message(z, places, z.center + (2 * e + h) * CAP, side_refs[e], h)
    tail_places_ref[...] = places[:, : z.center, :]


def last_center_kernel(z, *refs):
    d = z.devices_y
    flow_ref, old_places, ids_ref = refs[:3]
    center_refs = refs[3 : 3 + d]
    places, plane = refs[3 + d :]
    places[...] = old_places[...]
    (count_at, start), _ = layout(z)
    sample(z, places, flow_ref, ids_ref, start, ids_ref[count_at], plane)
    for e in range(d):
        join_message(z, places, e * CAP, center_refs[e], None)


def shift(value, axis, step):
    count = lax.axis_size(axis)
    return lax.ppermute(value, axis, [(i, (i + step) % count) for i in range(count)])


def trade_edges(z, right, left, up, down):
    from_left = shift(right, "gx", 1)
    from_right = shift(left, "gx", -1)
    far, near = slice(z.plane - LANES, z.plane), slice(0, LANES)
    up = jnp.concatenate([up, from_left[:, far], from_right[:, far]], axis=0)
    down = jnp.concatenate([down, from_left[:, near], from_right[:, near]], axis=0)
    return from_left, from_right, shift(up, "gy", 1), shift(down, "gy", -1)


def local(populations, positions, stiffness, membrane_shape, neighbours, home_tile):
    z = Sizes(
        positions.shape[0],
        positions.shape[2],
        populations.shape[1],
        populations.shape[2],
        lax.axis_size("gx"),
        lax.axis_size("gy"),
    )
    d = z.devices_y
    run = functools.partial
    line = (CAP, z.message)
    table = VMEM((3 * d,) + line, F32)
    counts = SMEM((3 * d,), jnp.int32)
    packed = call(
        run(pack_kernel, z),
        [((d,) + line, F32, VMEM)] * 2 + [(line, F32, VMEM)] * d,
        [SMEM, SMEM, VMEM],
        [table, counts],
    )(home_tile, stiffness, positions)
    to_left, to_right, center = packed[0], packed[1], packed[2:]
    from_left = shift(to_right, "gx", 1)
    from_right = shift(to_left, "gx", -1)
    center = [center[0]] + [shift(center[e], "gy", e) for e in range(1, d)]
    pad = z.full - z.vertices
    near = jnp.pad(neighbours, ((0, pad), (0, 0)), constant_values=-1)
    shape = jnp.pad(membrane_shape, ((0, 0), (0, pad)))
    link, degree = call(
        run(matrix_kernel, z),
        [((z.full, z.full), BF16, VMEM), ((1, z.full), F32, VMEM)],
        [VMEM, VMEM],
    )(near, near.T)
    sides = [jnp.stack([from_left[e], from_right[e]]) for e in range(d)]
    sides = [sides[0]] + [shift(sides[e], "gy", e) for e in range(1, d)]

    grid_type = ((3 * z.width_x, z.plane), F32, VMEM)
    post_type = ((19, z.width_x, z.plane), F32, VMEM)
    plane_scratch = VMEM((z.plane, 2 * z.main), BF16)
    lift_scratch = VMEM((3 * z.width_x, 2 * z.main), BF16)
    edge_types = [((8, z.plane), F32, VMEM)] * 2 + [((z.width_x, LANES), F32, VMEM)] * 2

    def rows(n):
        return VMEM((3, n, z.full), F32)

    def ends(n):
        return VMEM((n, LANES), F32)

    (part,) = call(
        run(center_kernel, z),
        [grid_type],
        [VMEM] * (d + 3),
        [
            rows(z.center),
            ends(z.center),
            ends(z.center),
            rows(z.center),
            plane_scratch,
            lift_scratch,
            SMEM((d, CAP, LANES), F32),
            SMEM((IDS,), jnp.int32),
            pltpu.SemaphoreType.DMA((d,)),
        ],
        pl.CostEstimate(flops=2_000_000_000, bytes_accessed=4_000_000, transcendentals=0),
    )(*center, shape, link, degree)
    n_sides = z.slots - z.center
    places_type = ((3, z.slots, z.full), F32, VMEM)
    grid, post, right, left, up, down, places, stiff, ids = call(
        run(sides_kernel, z),
        [grid_type, post_type]
        + edge_types
        + [places_type, ((z.slots, LANES), F32, VMEM), ((IDS,), jnp.int32, SMEM)],
        [VMEM] * (2 * d + 5),
        [
            ends(z.slots),
            rows(n_sides),
            ends(n_sides),
            ends(n_sides),
            rows(n_sides),
            plane_scratch,
            lift_scratch,
            SMEM((3 * d, CAP, LANES), F32),
            pltpu.SemaphoreType.DMA((3 * d,)),
        ],
    )(*center, *sides, shape, link, degree, part, populations)
    for _ in range(STEPS - 1):
        edges = trade_edges(z, right, left, up, down)
        grid, post, right, left, up, down, places = call(
            run(middle_kernel, z),
            [grid_type, post_type] + edge_types + [places_type],
            [VMEM] * 8 + [SMEM] + [VMEM] * 3,
            [
                VMEM(post_type[0], F32),
                VMEM(grid_type[0], F32),
                VMEM(grid_type[0], BF16),
                rows(z.slots),
                plane_scratch,
                lift_scratch,
                SMEM((IDS,), jnp.int32),
            ],
        )(post, *edges, grid, places, stiff, ids, shape, link, degree)
    edges = trade_edges(z, right, left, up, down)
    last = call(
        run(last_sides_kernel, z),
        [post_type, (grid_type[0], BF16, VMEM), ((3, z.center, z.full), F32, VMEM)]
        + [((2,) + line, F32, VMEM)] * d,
        [VMEM] * 7 + [SMEM],
        [VMEM(grid_type[0], F32), rows(z.slots), plane_scratch, SMEM((IDS,), jnp.int32)],
    )(post, *edges, grid, places, ids)
    moved, flow, center_places, sides = last[0], last[1], last[2], last[3:]
    sides = [sides[0]] + [shift(sides[e], "gy", -e) for e in range(1, d)]
    center = call(
        run(last_center_kernel, z),
        [(line, F32, VMEM)] * d,
        [VMEM, VMEM, SMEM],
        [rows(z.center), plane_scratch],
        pl.CostEstimate(flops=2_000_000_000, bytes_accessed=4_000_000, transcendentals=0),
    )(flow, center_places, ids)
    center = [center[0]] + [shift(center[e], "gy", -e) for e in range(1, d)]
    to_left = jnp.stack([sides[e][0] for e in range(d)])
    to_right = jnp.stack([sides[e][1] for e in range(d)])
    right_part = shift(to_left, "gx", -1)
    left_part = shift(to_right, "gx", 1)
    (displacement,) = call(
        run(unpack_kernel, z),
        [(positions.shape, F32, VMEM)],
        [SMEM] + [VMEM] * (3 + d),
        [table, counts],
    )(home_tile, positions, left_part, right_part, *center)
    return moved, displacement, grid.reshape(3, z.width_x, z.plane)


def solution(mesh):
    placed = (
        P(None, "gx", "gy"),
        P(("gx", "gy"), None, None),
        P(("gx", "gy")),
        P(),
        P(),
        P(("gx", "gy")),
    )
    return jax.shard_map(
        local,
        mesh=mesh,
        in_specs=placed,
        out_specs=(P(None, "gx", "gy"), P(("gx", "gy"), None, None), P(None, "gx", "gy")),
        check_vma=False,
    )
```

profile of v0, /device:TPU:0, one launch (start us, length us, event | category | flops | bytes accessed | tf_op | source)
XLA Modules:
  0.0 106.5 jit_solution(1322179169079620923)
XLA Ops:
  0.6 1.1 copy.9.places_ref
  1.7 0.0 copy-start.2
  1.7 0.6 copy-done.2
  2.3 0.7 copy-done.4
  3.0 0.9 shard_map.85
  3.9 0.5 collective-permute-start
  4.5 2.6 %collective-permute-start.1 = (f32[4,2048]{1,0:T(4,128)S(1)}, f32[4,2048]{1,0:T(4,128)S(1)}, u32[]{:S(2)}, u32[]{:S(2)}) collective-permute-start(f32[4,2048]{1,0:T(4,128)S(1)} %get-tuple-element.40), channel_id=1, source_target_pairs={{0,2},{1,3},{2,0},{3,1},{4,6},{5,7},{6,4},{7,5},{8,10},{9,11},{10,... | collective-permute-start | bytes 98312 | tf_op jit(solution)/shard_map/ppermute | solution.py:662
  7.0 1.4 %collective-permute-start.2 = (f32[4,2048]{1,0:T(4,128)S(1)}, f32[4,2048]{1,0:T(4,128)S(1)}, u32[]{:S(2)}, u32[]{:S(2)}) collective-permute-start(f32[4,2048]{1,0:T(4,128)S(1)} %get-tuple-element.41), channel_id=1, source_target_pairs={{0,3},{1,0},{2,1},{3,2},{4,7},{5,4},{6,5},{7,6},{8,11},{9,8},{10,9... | collective-permute-start | bytes 98312 | tf_op jit(solution)/shard_map/ppermute | solution.py:662
  8.4 1.5 %collective-permute-start.3 = (f32[4,4,2048]{2,1,0:T(4,128)S(1)}, f32[4,4,2048]{2,1,0:T(4,128)S(1)}, u32[]{:S(2)}, u32[]{:S(2)}) collective-permute-start(f32[4,4,2048]{2,1,0:T(4,128)S(1)} %get-tuple-element.42), channel_id=1, source_target_pairs={{0,4},{4,8},{8,12},{12,16},{16,20},{20,24},{24,28},{28,0},{1,5},{5... | collective-permute-start | bytes 393224 | tf_op jit(solution)/shard_map/ppermute | solution.py:662
  9.9 3.2 %collective-permute-start.4 = (f32[4,4,2048]{2,1,0:T(4,128)S(1)}, f32[4,4,2048]{2,1,0:T(4,128)S(1)}, u32[]{:S(2)}, u32[]{:S(2)}) collective-permute-start(f32[4,4,2048]{2,1,0:T(4,128)S(1)} %get-tuple-element.43), channel_id=1, source_target_pairs={{0,28},{4,0},{8,4},{12,8},{16,12},{20,16},{24,20},{28,24},{1,29},{... | collective-permute-start | bytes 393224 | tf_op jit(solution)/shard_map/ppermute | solution.py:662
  13.2 0.7 pad_bitcast_fusion.near_t_ref
  13.9 0.9 copy.13
  14.8 0.7 pad.8.refs_4_.refs_8_.refs_9_
  15.6 3.7 %shard_map.86 = (bf16[768,768]{1,0:T(8,128)(2,1)S(1)}, f32[1,768]{1,0:T(1,128)S(1)}) custom-call(s32[768,6]{1,0:T(8,128)S(1)} %pad.9.clone.near_ref, s32[6,768]{1,0:T(8,128)S(1)} %pad_bitcast_fusion.near_t_ref), custom_call_target="tpu_custom_call" | custom-call | tf_op jit(solution)/shard_map/pallas_call | solution.py:701
  19.2 0.0 collective-permute-done.refs_1_
  19.2 0.0 collective-permute-done.1.refs_2_
  19.2 0.0 collective-permute-done.2.refs_3_
  19.3 0.0 copy-start
  19.3 3.0 %shard_map.87.refs_11_ = f32[96,512]{1,0:T(8,128)S(1)} custom-call(f32[4,2048]{1,0:T(4,128)S(1)} %get-tuple-element.38.refs_0_, f32[4,2048]{1,0:T(4,128)S(1)} %collective-permute-done.refs_1_, f32[4,2048]{1,0:T(4,128)S(1)} %collective-permute-done.1.refs_2_, f32[4,2048]{1,0:T(4,128)S(1)} %collective-permute-done.2.refs_3_, ...), custom_call_target="tpu_custom_call" | custom-call | flops 2000000000 | bytes 4000000 | tf_op jit(solution)/shard_map/pallas_call | solution.py:721
  22.3 0.0 collective-permute-done.3
  22.3 0.0 collective-permute-done.4
  22.3 0.1 collective-permute-start.5
  22.4 1.7 %collective-permute-start.6 = (f32[2,4,2048]{2,1,0:T(4,128)S(1)}, f32[2,4,2048]{2,1,0:T(4,128)S(1)}, u32[]{:S(2)}, u32[]{:S(2)}) collective-permute-start(f32[2,4,2048]{2,1,0:T(4,128)S(1)} %pad_maximum_fusion.4), channel_id=1, source_target_pairs={{0,2},{1,3},{2,0},{3,1},{4,6},{5,7},{6,4},{7,5},{8,10},{9,11},{10,... | collective-permute-start | bytes 196616 | tf_op jit(solution)/shard_map/ppermute | solution.py:662
  24.1 1.3 %collective-permute-start.7 = (f32[2,4,2048]{2,1,0:T(4,128)S(1)}, f32[2,4,2048]{2,1,0:T(4,128)S(1)}, u32[]{:S(2)}, u32[]{:S(2)}) collective-permute-start(f32[2,4,2048]{2,1,0:T(4,128)S(1)} %pad_maximum_fusion.5), channel_id=1, source_target_pairs={{0,3},{1,0},{2,1},{3,2},{4,7},{5,4},{6,5},{7,6},{8,11},{9,8},{10,9... | collective-permute-start | bytes 196616 | tf_op jit(solution)/shard_map/ppermute | solution.py:662
  25.5 0.6 collective-permute-done.5.refs_5_
  26.1 0.8 collective-permute-done.6.refs_6_
  26.9 0.5 collective-permute-done.7.refs_7_
  27.4 7.0 %shard_map.88 = (f32[96,512]{1,0:T(8,128)S(1)}, f32[19,32,512]{2,1,0:T(8,128)S(1)}, f32[8,512]{1,0:T(8,128)S(1)}, f32[8,512]{1,0:T(8,128)S(1)}, f32[32,128]{1,0:...) custom-call(f32[4,2048]{1,0:T(4,128)S(1)} %get-tuple-element.38.refs_0, ...), custom_call_target="tpu_custom_call" | custom-call | tf_op jit(solution)/shard_map/pallas_call | solution.py:740
  34.4 0.1 collective-permute-start.8
  34.5 4.7 %collective-permute-start.9 = (f32[8,512]{1,0:T(8,128)S(1)}, f32[8,512]{1,0:T(8,128)S(1)}, u32[]{:S(2)}, u32[]{:S(2)}) collective-permute-start(f32[8,512]{1,0:T(8,128)S(1)} %get-tuple-element.48), channel_id=1, source_target_pairs={{0,28},{4,0},{8,4},{12,8},{16,12},{20,16},{24,20},{28,24},{1,29},{... | collective-permute-start | bytes 49160 | tf_op jit(solution)/shard_map/ppermute | solution.py:662
  39.2 1.8 %collective-permute-done.8.refs_1_ = f32[8,512]{1,0:T(8,128)S(1)} collective-permute-done((f32[8,512]{1,0:T(8,128)S(1)}, f32[8,512]{1,0:T(8,128)S(1)}, u32[]{:S(2)}, u32[]{:S(2)}) %collective-permute-start.8) | collective-permute-done | bytes 16416 | tf_op jit(solution)/shard_map/ppermute | solution.py:662
  41.0 2.4 %collective-permute-start.10 = (f32[48,128]{1,0:T(8,128)S(1)}, f32[48,128]{1,0:T(8,128)S(1)}, u32[]{:S(2)}, u32[]{:S(2)}) collective-permute-start(f32[48,128]{1,0:T(8,128)S(1)} %pad_maximum_fusion.6), channel_id=1, source_target_pairs={{0,1},{1,2},{2,3},{3,0},{4,5},{5,6},{6,7},{7,4},{8,9},{9,10},{10,1... | collective-permute-start | bytes 73736 | tf_op jit(solution)/shard_map/ppermute | solution.py:662
  43.4 0.0 collective-permute-start.11
  43.4 0.9 collective-permute-done.10.refs_3_
  44.4 0.6 collective-permute-done.11.refs_4_
  45.0 13.7 %shard_map.89 = (f32[96,512]{1,0:T(8,128)}, f32[19,32,512]{2,1,0:T(8,128)S(1)}, f32[8,512]{1,0:T(8,128)S(1)}, f32[8,512]{1,0:T(8,128)S(1)}, f32[32,128]{1,0:T(8,...) custom-call(f32[19,32,512]{2,1,0:T(8,128)S(1)} %get-tuple-element.46.refs_0_, ...), custom_call_target="tpu_custom_call" | custom-call | tf_op jit(solution)/shard_map/pallas_call | solution.py:760
  58.7 0.5 collective-permute-start.12
  59.2 5.0 %collective-permute-start.13 = (f32[8,512]{1,0:T(8,128)S(1)}, f32[8,512]{1,0:T(8,128)S(1)}, u32[]{:S(2)}, u32[]{:S(2)}) collective-permute-start(f32[8,512]{1,0:T(8,128)S(1)} %get-tuple-element.57), channel_id=1, source_target_pairs={{0,28},{4,0},{8,4},{12,8},{16,12},{20,16},{24,20},{28,24},{1,29},{... | collective-permute-start | bytes 49160 | tf_op jit(solution)/shard_map/ppermute | solution.py:662
  64.1 1.7 %collective-permute-done.12.refs_1_ = f32[8,512]{1,0:T(8,128)S(1)} collective-permute-done((f32[8,512]{1,0:T(8,128)S(1)}, f32[8,512]{1,0:T(8,128)S(1)}, u32[]{:S(2)}, u32[]{:S(2)}) %collective-permute-start.12) | collective-permute-done | bytes 16416 | tf_op jit(solution)/shard_map/ppermute | solution.py:662
  65.9 0.0 collective-permute-done.13.refs_2_
  65.9 6.5 %collective-permute-start.14 = (f32[48,128]{1,0:T(8,128)S(1)}, f32[48,128]{1,0:T(8,128)S(1)}, u32[]{:S(2)}, u32[]{:S(2)}) collective-permute-start(f32[48,128]{1,0:T(8,128)S(1)} %pad_maximum_fusion.8), channel_id=1, source_target_pairs={{0,1},{1,2},{2,3},{3,0},{4,5},{5,6},{6,7},{7,4},{8,9},{9,10},{10,1... | collective-permute-start | bytes 73736 | tf_op jit(solution)/shard_map/ppermute | solution.py:662
  72.4 0.0 collective-permute-start.15
  72.4 0.8 collective-permute-done.14.refs_3_
  73.3 1.8 %collective-permute-done.15.refs_4_ = f32[48,128]{1,0:T(8,128)S(1)} collective-permute-done((f32[48,128]{1,0:T(8,128)S(1)}, f32[48,128]{1,0:T(8,128)S(1)}, u32[]{:S(2)}, u32[]{:S(2)}) %collective-permute-start.15) | collective-permute-done | bytes 24608 | tf_op jit(solution)/shard_map/ppermute | solution.py:662
  75.1 0.9 copy-done.1
  76.0 5.9 %shard_map.90 = (f32[19,32,512]{2,1,0:T(8,128)}, bf16[96,512]{1,0:T(8,128)(2,1)S(1)}, f32[3,16,768]{2,1,0:T(8,128)S(1)}, f32[2,4,2048]{2,1,0:T(4,128)S(1)}, f32[...) custom-call(f32[19,32,512]{2,1,0:T(8,128)S(1)} %get-tuple-element.55.refs_0_, ...), custom_call_target="tpu_custom_call" | custom-call | tf_op jit(solution)/shard_map/pallas_call | solution.py:775
  81.9 1.2 %collective-permute-start.16 = (f32[2,4,2048]{2,1,0:T(4,128)S(1)}, f32[2,4,2048]{2,1,0:T(4,128)S(1)}, u32[]{:S(2)}, u32[]{:S(2)}) collective-permute-start(f32[2,4,2048]{2,1,0:T(4,128)S(1)} %get-tuple-element.64), channel_id=1, source_target_pairs={{0,3},{1,0},{2,1},{3,2},{4,7},{5,4},{6,5},{7,6},{8,11},{9,8},{10,9... | collective-permute-start | bytes 196616 | tf_op jit(solution)/shard_map/ppermute | solution.py:662
  83.1 5.7 %collective-permute-start.17 = (f32[2,4,2048]{2,1,0:T(4,128)S(1)}, f32[2,4,2048]{2,1,0:T(4,128)S(1)}, u32[]{:S(2)}, u32[]{:S(2)}) collective-permute-start(f32[2,4,2048]{2,1,0:T(4,128)S(1)} %get-tuple-element.65), channel_id=1, source_target_pairs={{0,2},{1,3},{2,0},{3,1},{4,6},{5,7},{6,4},{7,5},{8,10},{9,11},{10,... | collective-permute-start | bytes 196616 | tf_op jit(solution)/shard_map/ppermute | solution.py:662
  88.8 0.0 collective-permute-start.18
  88.8 3.3 %collective-permute-done.17 = f32[2,4,2048]{2,1,0:T(4,128)S(1)} collective-permute-done((f32[2,4,2048]{2,1,0:T(4,128)S(1)}, f32[2,4,2048]{2,1,0:T(4,128)S(1)}, u32[]{:S(2)}, u32[]{:S(2)}) %collective-permute-start.17) | collective-permute-done | bytes 65568 | tf_op jit(solution)/shard_map/ppermute | solution.py:662
  92.1 0.5 collective-permute-done.18
  92.7 0.1 collective-permute-start.19
  92.8 4.8 %collective-permute-start.20 = (f32[4,4,2048]{2,1,0:T(4,128)S(1)}, f32[4,4,2048]{2,1,0:T(4,128)S(1)}, u32[]{:S(2)}, u32[]{:S(2)}) collective-permute-start(f32[4,4,2048]{2,1,0:T(4,128)S(1)} %pad_maximum_fusion.1), channel_id=1, source_target_pairs={{0,28},{4,0},{8,4},{12,8},{16,12},{20,16},{24,20},{28,24},{1,29},{... | collective-permute-start | bytes 393224 | tf_op jit(solution)/shard_map/ppermute | solution.py:662
  97.6 2.2 %shard_map.91 = (f32[4,2048]{1,0:T(4,128)S(1)}, f32[4,2048]{1,0:T(4,128)S(1)}, f32[4,2048]{1,0:T(4,128)S(1)}, f32[4,2048]{1,0:T(4,128)S(1)}) custom-call(bf16[96,512]{1,0:T(8,128)(2,1)S(1)} %get-tuple-element.67.refs_0_, f32[3,16,768]{2,1,0:T(8,128)S(1)} %get-tuple-element.68.refs_1_, s32[128]{0:T(128)S(1)} %get-tuple-element.54.refs_8_.refs_7_.refs_2_), custom_call_target="tpu_custom_call" | custom-call | flops 2000000000 | bytes 4000000 | tf_op jit(solution)/shard_map/pallas_call | solution.py:784
  99.8 0.5 collective-permute-start.21
  100.3 1.3 %collective-permute-start.22 = (f32[4,2048]{1,0:T(4,128)S(1)}, f32[4,2048]{1,0:T(4,128)S(1)}, u32[]{:S(2)}, u32[]{:S(2)}) collective-permute-start(f32[4,2048]{1,0:T(4,128)S(1)} %get-tuple-element.71), channel_id=1, source_target_pairs={{0,2},{1,3},{2,0},{3,1},{4,6},{5,7},{6,4},{7,5},{8,10},{9,11},{10,... | collective-permute-start | bytes 98312 | tf_op jit(solution)/shard_map/ppermute | solution.py:662
  101.6 0.2 collective-permute-start.23
  101.7 0.2 collective-permute-done.21.rest_1_
  101.9 2.3 %collective-permute-done.22.rest_2_ = f32[4,2048]{1,0:T(4,128)S(1)} collective-permute-done((f32[4,2048]{1,0:T(4,128)S(1)}, f32[4,2048]{1,0:T(4,128)S(1)}, u32[]{:S(2)}, u32[]{:S(2)}) %collective-permute-start.22) | collective-permute-done | bytes 32800 | tf_op jit(solution)/shard_map/ppermute | solution.py:662
  104.2 0.7 collective-permute-done.23.rest_3_
  104.9 0.0 collective-permute-done.19.left_ref
  104.9 0.0 collective-permute-done.20.right_ref
  104.9 0.9 shard_map.92
  105.8 0.7 copy.12
  (28 shorter events, 0.2 us)
Async XLA Ops:
  1.7 0.7 copy-start.2
  2.3 0.7 copy-start.4
  3.9 15.3 %collective-permute-start = (f32[4,2048]{1,0:T(4,128)S(1)}, f32[4,2048]{1,0:T(4,128)S(1)}, u32[]{:S(2)}, u32[]{:S(2)}) collective-permute-start(f32[4,2048]{1,0:T(4,128)S(1)} %get-tuple-element.39), channel_id=1, source_target_pairs={{0,1},{1,2},{2,3},{3,0},{4,5},{5,6},{6,7},{7,4},{8,9},{9,10},{10,1... | collective-permute-start | bytes 98312 | tf_op jit(solution)/shard_map/ppermute | solution.py:662
  4.5 14.8 %collective-permute-start.1 = (f32[4,2048]{1,0:T(4,128)S(1)}, f32[4,2048]{1,0:T(4,128)S(1)}, u32[]{:S(2)}, u32[]{:S(2)}) collective-permute-start(f32[4,2048]{1,0:T(4,128)S(1)} %get-tuple-element.40), channel_id=1, source_target_pairs={{0,2},{1,3},{2,0},{3,1},{4,6},{5,7},{6,4},{7,5},{8,10},{9,11},{10,... | collective-permute-start | bytes 98312 | tf_op jit(solution)/shard_map/ppermute | solution.py:662
  7.0 12.2 %collective-permute-start.2 = (f32[4,2048]{1,0:T(4,128)S(1)}, f32[4,2048]{1,0:T(4,128)S(1)}, u32[]{:S(2)}, u32[]{:S(2)}) collective-permute-start(f32[4,2048]{1,0:T(4,128)S(1)} %get-tuple-element.41), channel_id=1, source_target_pairs={{0,3},{1,0},{2,1},{3,2},{4,7},{5,4},{6,5},{7,6},{8,11},{9,8},{10,9... | collective-permute-start | bytes 98312 | tf_op jit(solution)/shard_map/ppermute | solution.py:662
  8.4 13.8 %collective-permute-start.3 = (f32[4,4,2048]{2,1,0:T(4,128)S(1)}, f32[4,4,2048]{2,1,0:T(4,128)S(1)}, u32[]{:S(2)}, u32[]{:S(2)}) collective-permute-start(f32[4,4,2048]{2,1,0:T(4,128)S(1)} %get-tuple-element.42), channel_id=1, source_target_pairs={{0,4},{4,8},{8,12},{12,16},{16,20},{20,24},{24,28},{28,0},{1,5},{5... | collective-permute-start | bytes 393224 | tf_op jit(solution)/shard_map/ppermute | solution.py:662
  9.9 12.4 %collective-permute-start.4 = (f32[4,4,2048]{2,1,0:T(4,128)S(1)}, f32[4,4,2048]{2,1,0:T(4,128)S(1)}, u32[]{:S(2)}, u32[]{:S(2)}) collective-permute-start(f32[4,4,2048]{2,1,0:T(4,128)S(1)} %get-tuple-element.43), channel_id=1, source_target_pairs={{0,28},{4,0},{8,4},{12,8},{16,12},{20,16},{24,20},{28,24},{1,29},{... | collective-permute-start | bytes 393224 | tf_op jit(solution)/shard_map/ppermute | solution.py:662
  19.3 8.1 %copy-start = (f32[19,32,512]{2,1,0:T(8,128)S(1)}, f32[19,32,512]{2,1,0:T(8,128)}, u32[]{:S(2)}) copy-start(f32[19,32,512]{2,1,0:T(8,128)} %refs_12_.1) | copy-start | bytes 3735556
  22.3 3.8 %collective-permute-start.5 = (f32[2,4,2048]{2,1,0:T(4,128)S(1)}, f32[2,4,2048]{2,1,0:T(4,128)S(1)}, u32[]{:S(2)}, u32[]{:S(2)}) collective-permute-start(f32[2,4,2048]{2,1,0:T(4,128)S(1)} %pad_maximum_fusion.3), channel_id=1, source_target_pairs={{0,1},{1,2},{2,3},{3,0},{4,5},{5,6},{6,7},{7,4},{8,9},{9,10},{10,1... | collective-permute-start | bytes 196616 | tf_op jit(solution)/shard_map/ppermute | solution.py:662
  22.4 4.5 %collective-permute-start.6 = (f32[2,4,2048]{2,1,0:T(4,128)S(1)}, f32[2,4,2048]{2,1,0:T(4,128)S(1)}, u32[]{:S(2)}, u32[]{:S(2)}) collective-permute-start(f32[2,4,2048]{2,1,0:T(4,128)S(1)} %pad_maximum_fusion.4), channel_id=1, source_target_pairs={{0,2},{1,3},{2,0},{3,1},{4,6},{5,7},{6,4},{7,5},{8,10},{9,11},{10,... | collective-permute-start | bytes 196616 | tf_op jit(solution)/shard_map/ppermute | solution.py:662
  24.1 3.2 %collective-permute-start.7 = (f32[2,4,2048]{2,1,0:T(4,128)S(1)}, f32[2,4,2048]{2,1,0:T(4,128)S(1)}, u32[]{:S(2)}, u32[]{:S(2)}) collective-permute-start(f32[2,4,2048]{2,1,0:T(4,128)S(1)} %pad_maximum_fusion.5), channel_id=1, source_target_pairs={{0,3},{1,0},{2,1},{3,2},{4,7},{5,4},{6,5},{7,6},{8,11},{9,8},{10,9... | collective-permute-start | bytes 196616 | tf_op jit(solution)/shard_map/ppermute | solution.py:662
  34.4 6.6 %collective-permute-start.8 = (f32[8,512]{1,0:T(8,128)S(1)}, f32[8,512]{1,0:T(8,128)S(1)}, u32[]{:S(2)}, u32[]{:S(2)}) collective-permute-start(f32[8,512]{1,0:T(8,128)S(1)} %get-tuple-element.47), channel_id=1, source_target_pairs={{0,4},{4,8},{8,12},{12,16},{16,20},{20,24},{24,28},{28,0},{1,5},{5... | collective-permute-start | bytes 49160 | tf_op jit(solution)/shard_map/ppermute | solution.py:662
  34.5 6.5 %collective-permute-start.9 = (f32[8,512]{1,0:T(8,128)S(1)}, f32[8,512]{1,0:T(8,128)S(1)}, u32[]{:S(2)}, u32[]{:S(2)}) collective-permute-start(f32[8,512]{1,0:T(8,128)S(1)} %get-tuple-element.48), channel_id=1, source_target_pairs={{0,28},{4,0},{8,4},{12,8},{16,12},{20,16},{24,20},{28,24},{1,29},{... | collective-permute-start | bytes 49160 | tf_op jit(solution)/shard_map/ppermute | solution.py:662
  41.0 3.3 %collective-permute-start.10 = (f32[48,128]{1,0:T(8,128)S(1)}, f32[48,128]{1,0:T(8,128)S(1)}, u32[]{:S(2)}, u32[]{:S(2)}) collective-permute-start(f32[48,128]{1,0:T(8,128)S(1)} %pad_maximum_fusion.6), channel_id=1, source_target_pairs={{0,1},{1,2},{2,3},{3,0},{4,5},{5,6},{6,7},{7,4},{8,9},{9,10},{10,1... | collective-permute-start | bytes 73736 | tf_op jit(solution)/shard_map/ppermute | solution.py:662
  43.4 1.5 %collective-permute-start.11 = (f32[48,128]{1,0:T(8,128)S(1)}, f32[48,128]{1,0:T(8,128)S(1)}, u32[]{:S(2)}, u32[]{:S(2)}) collective-permute-start(f32[48,128]{1,0:T(8,128)S(1)} %pad_maximum_fusion.7), channel_id=1, source_target_pairs={{0,3},{1,0},{2,1},{3,2},{4,7},{5,4},{6,5},{7,6},{8,11},{9,8},{10,9... | collective-permute-start | bytes 73736 | tf_op jit(solution)/shard_map/ppermute | solution.py:662
  58.7 7.2 %collective-permute-start.12 = (f32[8,512]{1,0:T(8,128)S(1)}, f32[8,512]{1,0:T(8,128)S(1)}, u32[]{:S(2)}, u32[]{:S(2)}) collective-permute-start(f32[8,512]{1,0:T(8,128)S(1)} %get-tuple-element.56), channel_id=1, source_target_pairs={{0,4},{4,8},{8,12},{12,16},{16,20},{20,24},{24,28},{28,0},{1,5},{5... | collective-permute-start | bytes 49160 | tf_op jit(solution)/shard_map/ppermute | solution.py:662
  59.2 6.7 %collective-permute-start.13 = (f32[8,512]{1,0:T(8,128)S(1)}, f32[8,512]{1,0:T(8,128)S(1)}, u32[]{:S(2)}, u32[]{:S(2)}) collective-permute-start(f32[8,512]{1,0:T(8,128)S(1)} %get-tuple-element.57), channel_id=1, source_target_pairs={{0,28},{4,0},{8,4},{12,8},{16,12},{20,16},{24,20},{28,24},{1,29},{... | collective-permute-start | bytes 49160 | tf_op jit(solution)/shard_map/ppermute | solution.py:662
  65.9 7.4 %collective-permute-start.14 = (f32[48,128]{1,0:T(8,128)S(1)}, f32[48,128]{1,0:T(8,128)S(1)}, u32[]{:S(2)}, u32[]{:S(2)}) collective-permute-start(f32[48,128]{1,0:T(8,128)S(1)} %pad_maximum_fusion.8), channel_id=1, source_target_pairs={{0,1},{1,2},{2,3},{3,0},{4,5},{5,6},{6,7},{7,4},{8,9},{9,10},{10,1... | collective-permute-start | bytes 73736 | tf_op jit(solution)/shard_map/ppermute | solution.py:662
  72.4 2.7 %collective-permute-start.15 = (f32[48,128]{1,0:T(8,128)S(1)}, f32[48,128]{1,0:T(8,128)S(1)}, u32[]{:S(2)}, u32[]{:S(2)}) collective-permute-start(f32[48,128]{1,0:T(8,128)S(1)} %pad_maximum_fusion.9), channel_id=1, source_target_pairs={{0,3},{1,0},{2,1},{3,2},{4,7},{5,4},{6,5},{7,6},{8,11},{9,8},{10,9... | collective-permute-start | bytes 73736 | tf_op jit(solution)/shard_map/ppermute | solution.py:662
  75.1 0.9 copy-start.1
  81.9 6.9 %collective-permute-start.16 = (f32[2,4,2048]{2,1,0:T(4,128)S(1)}, f32[2,4,2048]{2,1,0:T(4,128)S(1)}, u32[]{:S(2)}, u32[]{:S(2)}) collective-permute-start(f32[2,4,2048]{2,1,0:T(4,128)S(1)} %get-tuple-element.64), channel_id=1, source_target_pairs={{0,3},{1,0},{2,1},{3,2},{4,7},{5,4},{6,5},{7,6},{8,11},{9,8},{10,9... | collective-permute-start | bytes 196616 | tf_op jit(solution)/shard_map/ppermute | solution.py:662
  83.1 9.0 %collective-permute-start.17 = (f32[2,4,2048]{2,1,0:T(4,128)S(1)}, f32[2,4,2048]{2,1,0:T(4,128)S(1)}, u32[]{:S(2)}, u32[]{:S(2)}) collective-permute-start(f32[2,4,2048]{2,1,0:T(4,128)S(1)} %get-tuple-element.65), channel_id=1, source_target_pairs={{0,2},{1,3},{2,0},{3,1},{4,6},{5,7},{6,4},{7,5},{8,10},{9,11},{10,... | collective-permute-start | bytes 196616 | tf_op jit(solution)/shard_map/ppermute | solution.py:662
  88.8 3.8 %collective-permute-start.18 = (f32[2,4,2048]{2,1,0:T(4,128)S(1)}, f32[2,4,2048]{2,1,0:T(4,128)S(1)}, u32[]{:S(2)}, u32[]{:S(2)}) collective-permute-start(f32[2,4,2048]{2,1,0:T(4,128)S(1)} %get-tuple-element.66), channel_id=1, source_target_pairs={{0,1},{1,2},{2,3},{3,0},{4,5},{5,6},{6,7},{7,4},{8,9},{9,10},{10,1... | collective-permute-start | bytes 196616 | tf_op jit(solution)/shard_map/ppermute | solution.py:662
  92.7 12.2 %collective-permute-start.19 = (f32[4,4,2048]{2,1,0:T(4,128)S(1)}, f32[4,4,2048]{2,1,0:T(4,128)S(1)}, u32[]{:S(2)}, u32[]{:S(2)}) collective-permute-start(f32[4,4,2048]{2,1,0:T(4,128)S(1)} %pad_maximum_fusion), channel_id=1, source_target_pairs={{0,4},{4,8},{8,12},{12,16},{16,20},{20,24},{24,28},{28,0},{1,5},{5... | collective-permute-start | bytes 393224 | tf_op jit(solution)/shard_map/ppermute | solution.py:662
  92.8 12.1 %collective-permute-start.20 = (f32[4,4,2048]{2,1,0:T(4,128)S(1)}, f32[4,4,2048]{2,1,0:T(4,128)S(1)}, u32[]{:S(2)}, u32[]{:S(2)}) collective-permute-start(f32[4,4,2048]{2,1,0:T(4,128)S(1)} %pad_maximum_fusion.1), channel_id=1, source_target_pairs={{0,28},{4,0},{8,4},{12,8},{16,12},{20,16},{24,20},{28,24},{1,29},{... | collective-permute-start | bytes 393224 | tf_op jit(solution)/shard_map/ppermute | solution.py:662
  97.6 7.3 %copy-start.3 = (s32[24]{0:T(128)S(1)}, s32[24]{0:T(128)}, u32[]{:S(2)}) copy-start(s32[24]{0:T(128)} %home_ref.3) | copy-start | bytes 292
  99.8 2.1 %collective-permute-start.21 = (f32[4,2048]{1,0:T(4,128)S(1)}, f32[4,2048]{1,0:T(4,128)S(1)}, u32[]{:S(2)}, u32[]{:S(2)}) collective-permute-start(f32[4,2048]{1,0:T(4,128)S(1)} %get-tuple-element.70), channel_id=1, source_target_pairs={{0,3},{1,0},{2,1},{3,2},{4,7},{5,4},{6,5},{7,6},{8,11},{9,8},{10,9... | collective-permute-start | bytes 98312 | tf_op jit(solution)/shard_map/ppermute | solution.py:662
  100.3 3.9 %collective-permute-start.22 = (f32[4,2048]{1,0:T(4,128)S(1)}, f32[4,2048]{1,0:T(4,128)S(1)}, u32[]{:S(2)}, u32[]{:S(2)}) collective-permute-start(f32[4,2048]{1,0:T(4,128)S(1)} %get-tuple-element.71), channel_id=1, source_target_pairs={{0,2},{1,3},{2,0},{3,1},{4,6},{5,7},{6,4},{7,5},{8,10},{9,11},{10,... | collective-permute-start | bytes 98312 | tf_op jit(solution)/shard_map/ppermute | solution.py:662
  101.6 3.3 %collective-permute-start.23 = (f32[4,2048]{1,0:T(4,128)S(1)}, f32[4,2048]{1,0:T(4,128)S(1)}, u32[]{:S(2)}, u32[]{:S(2)}) collective-permute-start(f32[4,2048]{1,0:T(4,128)S(1)} %get-tuple-element.72), channel_id=1, source_target_pairs={{0,1},{1,2},{2,3},{3,0},{4,5},{5,6},{6,7},{7,4},{8,9},{9,10},{10,1... | collective-permute-start | bytes 98312 | tf_op jit(solution)/shard_map/ppermute | solution.py:662
where the time goes:
time: 105 us; the launch traced here: 107 us
  starting transfers between devices  45.1 us (43%)
  Pallas kernels  37.3 us (36%)
  waiting for transfers between devices  16.6 us (16%)
  local copies, waits for them, and re-layouts  6.46 us (6%)
    ppermute x24, starting transfers between devices, shift(): lax.ppermute(value, axis, [(i, (i + step) % count) for i in range(count)])  45.1 us
    ppermute x24, waiting for transfers between devices, shift(): lax.ppermute(value, axis, [(i, (i + step) % count) for i in range(count)])  16.6 us
    pallas_call x1, Pallas kernels, local(): call(run(middle_kernel, z), [grid_type, post_type] + edge_types + [places...  13.7 us
    pallas_call x1, Pallas kernels, local(): call(run(sides_kernel, z), [grid_type, post_type] + edge_types + [places_...  7.04 us
    pallas_call x1, Pallas kernels, local(): call(run(last_sides_kernel, z), [post_type, (grid_type[0], BF16, VMEM), (...  5.93 us
    unnamed x13, local copies, waits for them, and re-layouts  4.92 us
    pallas_call x1, Pallas kernels, local(): call(run(matrix_kernel, z), [((z.full, z.full), BF16, VMEM), ((1, z.full)...  3.66 us
    pallas_call x1, Pallas kernels, local(): call(run(center_kernel, z), [grid_type], [VMEM] * (d + 3), [rows(z.center...  2.99 us
  transfers between devices with their start and end apart: 24, of which 14 were waited for; matrix products, arithmetic and copies ran while one was open for 2% of the time, Pallas kernels for 8%

commit v1 on v0

v1 whole, which is shorter than its diff:
```python
import functools

import jax
import jax.numpy as jnp
from jax import lax
from jax.experimental import pallas as pl
from jax.experimental.pallas import tpu as pltpu
from jax.sharding import PartitionSpec as P

CZ = 16
CAP = 4
STEPS = 2

LATTICE_VELOCITY = [
    [0, 0, 0],
    [1, 0, 0],
    [-1, 0, 0],
    [0, 1, 0],
    [0, -1, 0],
    [0, 0, 1],
    [0, 0, -1],
    [1, 1, 0],
    [-1, -1, 0],
    [1, -1, 0],
    [-1, 1, 0],
    [1, 0, 1],
    [-1, 0, -1],
    [1, 0, -1],
    [-1, 0, 1],
    [0, 1, 1],
    [0, -1, -1],
    [0, 1, -1],
    [0, -1, 1],
]
LATTICE_WEIGHT = [1.0 / 3.0] + [1.0 / 18.0] * 6 + [1.0 / 36.0] * 12
RIGHT_MOVERS = [1, 7, 9, 11, 13]
LEFT_MOVERS = [2, 8, 10, 12, 14]
UPWARD_MOVERS = [3, 7, 10, 15, 17]
DOWNWARD_MOVERS = [4, 8, 9, 16, 18]
RELAX_RATE = 1.25
PUSH_SCALE = 0.05
TETHER_GAIN = 2.0
LANES = 128
WINDOW = 16
SLOW = 15
FAST_AT = 2
SLOW_AT = 64
CODE_AT = 128
LISTS = 256
F32 = jnp.float32
BF16 = jnp.bfloat16
SMEM = pltpu.SMEM
VMEM = pltpu.VMEM


def spec(space):
    return pl.BlockSpec(memory_space=space)


def call(kernel, outs, ins, scratch=(), cost=None, limit=None):
    return pl.pallas_call(
        kernel,
        out_shape=[jax.ShapeDtypeStruct(s, d) for s, d, _ in outs],
        in_specs=[spec(m) for m in ins],
        out_specs=[spec(m) for _, _, m in outs],
        scratch_shapes=list(scratch),
        compiler_params=pltpu.CompilerParams(vmem_limit_bytes=limit or (24 << 20)),
        cost_estimate=cost,
    )


def lane_index(shape):
    return lax.broadcasted_iota(jnp.int32, shape, len(shape) - 1)


def row_index(shape):
    return lax.broadcasted_iota(jnp.int32, shape, len(shape) - 2)


class Sizes:
    def __init__(self, cells, vertices, width_x, plane, devices_x, devices_y):
        self.cells = cells
        self.vertices = vertices
        self.width_x = width_x
        self.plane = plane
        self.devices_x = devices_x
        self.devices_y = devices_y
        self.main = vertices - vertices % LANES
        self.tail = vertices - self.main
        self.full = self.main + LANES
        self.message = 3 * self.main + LANES
        self.groups = 3 * devices_y
        self.slots = 3 * devices_y * CAP
        self.width_y = plane // CZ


def cell_places(z, home_ref, count_ref):
    own_x = lax.axis_index("gx")
    own_y = lax.axis_index("gy")
    for g in range(z.groups):
        count_ref[g] = 0
    found = []
    for n in range(z.cells):
        home = home_ref[n]
        target_x = lax.div(home, z.devices_y)
        target_y = lax.rem(home, z.devices_y)
        side = lax.rem(target_x - own_x + 1 + z.devices_x, z.devices_x)
        turn = lax.rem(target_y - own_y + z.devices_y, z.devices_y)
        group = side * z.devices_y + turn
        rank = count_ref[group]
        count_ref[group] = rank + 1
        found.append((group, rank))
    return found


def pack_kernel(z, home_ref, stiff_ref, places_ref, left_ref, center_ref, right_ref, table_ref, count_ref):
    table_ref[...] = jnp.zeros_like(table_ref)
    lane = lane_index((1, LANES))
    zeros = jnp.zeros((1, LANES - z.tail), F32)
    for n, (group, rank) in enumerate(cell_places(z, home_ref, count_ref)):
        ends = jnp.where(lane == 3 * z.tail, stiff_ref[n], 0.0)
        parts = []
        for c in range(3):
            line = places_ref[c, n : n + 1, :]
            parts.append(line[:, : z.main])
            end = jnp.concatenate([line[:, z.main :], zeros], axis=1)
            ends = ends + (end if c == 0 else pltpu.roll(end, c * z.tail, 1))
        table_ref[group, pl.ds(rank, 1), :] = jnp.concatenate(parts + [ends], axis=1)
    d = z.devices_y
    left_ref[...] = table_ref[0:d]
    center_ref[...] = table_ref[d : 2 * d]
    right_ref[...] = table_ref[2 * d : 3 * d]


def unpack_kernel(z, home_ref, places_ref, left_ref, right_ref, *rest):
    center_refs = rest[: z.devices_y]
    out_ref, table_ref, count_ref = rest[z.devices_y :]
    d = z.devices_y
    table_ref[0:d] = left_ref[...]
    table_ref[2 * d : 3 * d] = right_ref[...]
    for r in range(d):
        table_ref[d + r] = center_refs[r][0]
    for n, (group, rank) in enumerate(cell_places(z, home_ref, count_ref)):
        line = table_ref[group, pl.ds(rank, 1), :]
        ends = line[:, 3 * z.main :]
        for c in range(3):
            end = ends if c == 0 else pltpu.roll(ends, LANES - c * z.tail, 1)
            whole = jnp.concatenate([line[:, c * z.main : (c + 1) * z.main], end], axis=1)
            out_ref[c, n : n + 1, :] = whole[:, : z.vertices] - places_ref[c, n : n + 1, :]


def matrix_kernel(z, near_ref, shape_ref, link_ref, degree_ref, rest_ref, half_ref):
    near = near_ref[...]
    shape = shape_ref[...]
    rest_ref[...] = jnp.concatenate(
        [shape, jnp.zeros((3, z.full - z.vertices), F32)], axis=1
    )
    entries = near.shape[0]
    tiles = z.full // LANES
    missing = jnp.full((entries, z.full - z.vertices), -1, jnp.int32)
    near = jnp.concatenate([near, missing], axis=1)
    row = row_index((LANES, LANES))
    for t in range(tiles):
        lines = near[:, t * LANES : (t + 1) * LANES]
        for r in range(tiles):
            total = jnp.zeros((LANES, LANES), F32)
            for b in range(entries):
                total += jnp.where(lines[b : b + 1] == row + r * LANES, 1.0, 0.0)
            half_ref[r * LANES : (r + 1) * LANES, t * LANES : (t + 1) * LANES] = total
    for t in range(tiles):
        lanes = slice(t * LANES, (t + 1) * LANES)
        degree = jnp.zeros((1, LANES), F32) + TETHER_GAIN
        for r in range(tiles):
            rows = slice(r * LANES, (r + 1) * LANES)
            total = half_ref[rows, lanes] + half_ref[lanes, rows].T
            link_ref[rows, lanes] = total.astype(BF16)
            degree += jnp.sum(total, axis=0, keepdims=True)
        degree_ref[:, lanes] = degree


def split_message(z, value, places_ref, ends_ref, slot):
    for c in range(3):
        places_ref[c, slot : slot + CAP, : z.main] = value[:, c * z.main : (c + 1) * z.main]
    ends_ref[slot : slot + CAP, :] = value[:, 3 * z.main :]


def place_tails(z, ends_ref, places_ref, stiff_ref):
    ends = ends_ref[...]
    lane = lane_index(ends.shape)
    for c in range(3):
        end = ends if c == 0 else pltpu.roll(ends, LANES - c * z.tail, 1)
        places_ref[c, :, z.main :] = jnp.where(lane < z.tail, end, 0.0)
    stiff_ref[...] = jnp.broadcast_to(ends[:, 3 * z.tail : 3 * z.tail + 1], ends.shape)


def forces(z, places_ref, stiff_ref, shape_ref, link_ref, degree_ref, force_ref):
    rows = places_ref.shape[1]
    lane = lane_index((rows, z.full))
    inside = lane < z.vertices
    parts = []
    for c in range(3):
        x = places_ref[c]
        mean = jnp.sum(x, axis=1, keepdims=True) * (1.0 / z.vertices)
        parts.append(jnp.where(inside, x - mean - shape_ref[c : c + 1, :], 0.0))
    strain = jnp.concatenate(parts, axis=0)
    high = strain.astype(BF16)
    rest = strain - high.astype(F32)
    low = rest.astype(BF16)
    link = link_ref[...]
    linked = jnp.dot(high, link, preferred_element_type=F32) + jnp.dot(
        low, link, preferred_element_type=F32
    )
    pulled = degree_ref[...] * (high.astype(F32) + low.astype(F32)) - linked
    stiff = stiff_ref[:, 0:1]
    for c in range(3):
        force_ref[c] = -stiff * pulled[c * rows : (c + 1) * rows]


def list_slots(z, places_ref, stiff_ref, lists_ref):
    codes = None
    fits = None
    for c, width in ((0, z.width_x), (1, z.width_y)):
        x = places_ref[c, :, : z.main]
        low = jnp.maximum(jnp.floor(jnp.min(x, axis=1, keepdims=True)), 0.0)
        high = jnp.minimum(jnp.floor(jnp.max(x, axis=1, keepdims=True)) + 1.0, width - 1.0)
        block = jnp.minimum(jnp.floor(low * 0.125), (width - WINDOW) // 8 * 1.0)
        fit = high - 8.0 * block <= WINDOW - 1.0
        codes = block if codes is None else codes + 4.0 * block
        fits = fit if fits is None else fits & fit
    codes = jnp.where(fits, codes, SLOW * 1.0)
    codes = jnp.where(stiff_ref[:, 0:1] > 0.0, codes, -1.0).astype(jnp.int32)
    for s in range(z.slots):
        lists_ref[CODE_AT + s] = codes[s, 0]

    def step(s, state):
        fast, slow, empty = state
        code = lists_ref[CODE_AT + s]
        is_slow = code == SLOW
        is_fast = (code >= 0) & (code < SLOW)

        @pl.when(is_fast)
        def _():
            lists_ref[FAST_AT + fast] = s

        @pl.when(is_slow)
        def _():
            lists_ref[SLOW_AT + slow] = s

        @pl.when(code < 0)
        def _():
            lists_ref[CODE_AT + s] = 0

        return (
            jnp.where(is_fast, fast + 1, fast),
            jnp.where(is_slow, slow + 1, slow),
            jnp.where(code < 0, s, empty),
        )

    zero = jnp.int32(0)
    fast, slow, empty = lax.fori_loop(0, z.slots, step, (zero, zero, zero))

    @pl.when(lax.rem(fast, 2) == 1)
    def _():
        lists_ref[FAST_AT + fast] = empty

    @pl.when(lax.rem(slow, 2) == 1)
    def _():
        lists_ref[SLOW_AT + slow] = empty

    lists_ref[0] = lax.div(fast + 1, 2)
    lists_ref[1] = lax.div(slow + 1, 2)


def window_of(lists_ref, s):
    code = lists_ref[CODE_AT + s]
    return 8 * lax.rem(code, 4), 8 * lax.div(code, 4)


def tails_to_lanes(z, ref, c):
    ends = ref[c, :, z.main :]
    lane = lane_index(ends.shape)
    row = row_index(ends.shape)
    picked = jnp.zeros_like(ends)
    for t in range(z.tail):
        picked = jnp.where(lane == row * z.tail + t, ends[:, t : t + 1], picked)
    return jnp.sum(picked, axis=0, keepdims=True)


def hat_tables(x, y, depth, first_x, count_x, first_y, count_y, plane_ref, rows_at, at):
    width = x.shape[1]
    steps_x = row_index((count_x, width)).astype(F32)
    steps_y = row_index((count_y, width)).astype(F32)
    if first_x is not None:
        steps_x = steps_x + first_x
        steps_y = steps_y + first_y
    steps_z = row_index((CZ, width)).astype(F32)
    hat_x = jnp.maximum(0.0, 1.0 - jnp.abs(x - steps_x))
    hat_y = jnp.maximum(0.0, 1.0 - jnp.abs(y - steps_y))
    wrapped = depth - CZ * jnp.floor(depth * (1.0 / CZ))
    gap = jnp.abs(wrapped - steps_z)
    hat_z = jnp.maximum(0.0, 1.0 - jnp.minimum(gap, CZ - gap))
    for j in range(count_y):
        rows = slice(rows_at + j * CZ, rows_at + (j + 1) * CZ)
        plane_ref[rows, at : at + width] = (hat_y[j : j + 1] * hat_z).astype(BF16)
    return hat_x


def contract(lift, plane):
    return lax.dot_general(lift, plane, (((1,), (1,)), ((), ())), preferred_element_type=F32)


def spread(z, places_ref, force_ref, lists_ref, grid_ref, plane_ref, lift_ref):
    grid_ref[...] = jnp.zeros_like(grid_ref)

    def fill(line, pull, firsts, counts, at, plane_row, lift_row):
        hat_x = hat_tables(*line, firsts[0], counts[0], firsts[1], counts[1], plane_ref, plane_row, at)
        width = line[0].shape[1]
        for c in range(3):
            row = lift_row + c * counts[0]
            lift_ref[row : row + counts[0], at : at + width] = (pull[c] * hat_x).astype(BF16)

    def load(s):
        line = [places_ref[c, pl.ds(s, 1), : z.main] for c in range(3)]
        pull = [force_ref[c, pl.ds(s, 1), : z.main] for c in range(3)]
        return line, pull

    whole = (z.width_x, z.width_y)
    window = (WINDOW, WINDOW)
    plane_rows = WINDOW * CZ
    lift_rows = 3 * WINDOW

    def fast(p, carry):
        firsts = []
        for h in range(2):
            s = lists_ref[FAST_AT + 2 * p + h]
            first = window_of(lists_ref, s)
            firsts.append(first)
            line, pull = load(s)
            fill(
                line, pull, [f.astype(F32) for f in first], window, 0, h * plane_rows, h * lift_rows
            )
        for h in range(2):
            part = contract(
                lift_ref[h * lift_rows : (h + 1) * lift_rows, : z.main],
                plane_ref[h * plane_rows : (h + 1) * plane_rows, : z.main],
            )
            lanes = pl.ds(pl.multiple_of(firsts[h][1] * CZ, LANES), plane_rows)
            for c in range(3):
                rows = pl.ds(pl.multiple_of(c * z.width_x + firsts[h][0], 8), WINDOW)
                grid_ref[rows, lanes] += part[c * WINDOW : (c + 1) * WINDOW]
        return carry

    def slow(p, carry):
        for h in range(2):
            line, pull = load(lists_ref[SLOW_AT + 2 * p + h])
            fill(line, pull, (None, None), whole, h * z.main, 0, 0)
        grid_ref[...] += contract(lift_ref[...], plane_ref[...])
        return carry

    line = [tails_to_lanes(z, places_ref, c) for c in range(3)]
    pull = [tails_to_lanes(z, force_ref, c) for c in range(3)]
    fill(line, pull, (None, None), whole, 0, 0, 0)
    grid_ref[...] = contract(lift_ref[:, :LANES], plane_ref[:, :LANES])
    lax.fori_loop(0, lists_ref[0], fast, 0)
    lax.fori_loop(0, lists_ref[1], slow, 0)


def sample(z, places_ref, flow_ref, lists_ref, plane_ref):
    plane_rows = WINDOW * CZ

    def load(s):
        return [places_ref[c, pl.ds(s, 1), : z.main] for c in range(3)]

    def move(s, line, picked, hat_x, count_x):
        for c in range(3):
            drift = jnp.sum(picked[c * count_x : (c + 1) * count_x] * hat_x, axis=0, keepdims=True)
            places_ref[c, pl.ds(s, 1), : z.main] = line[c] + drift

    def fast(p, carry):
        slots = [lists_ref[FAST_AT + 2 * p + h] for h in range(2)]
        firsts = [window_of(lists_ref, s) for s in slots]
        lines = [load(s) for s in slots]
        hats = [
            hat_tables(
                *lines[h],
                firsts[h][0].astype(F32),
                WINDOW,
                firsts[h][1].astype(F32),
                WINDOW,
                plane_ref,
                h * plane_rows,
                0,
            )
            for h in range(2)
        ]
        picked = []
        for h in range(2):
            lanes = pl.ds(pl.multiple_of(firsts[h][1] * CZ, LANES), plane_rows)
            flow = jnp.concatenate(
                [
                    flow_ref[
                        pl.ds(pl.multiple_of(c * z.width_x + firsts[h][0], 8), WINDOW), lanes
                    ]
                    for c in range(3)
                ],
                axis=0,
            ).astype(BF16)
            plane = plane_ref[h * plane_rows : (h + 1) * plane_rows, : z.main]
            picked.append(jnp.dot(flow, plane, preferred_element_type=F32))
        for h in range(2):
            move(slots[h], lines[h], picked[h], hats[h], WINDOW)
        return carry

    def slow(p, carry):
        slots = [lists_ref[SLOW_AT + 2 * p + h] for h in range(2)]
        lines = [load(s) for s in slots]
        hats = [
            hat_tables(
                *lines[h], None, z.width_x, None, z.width_y, plane_ref, 0, h * z.main
            )
            for h in range(2)
        ]
        picked = jnp.dot(
            flow_ref[...].astype(BF16), plane_ref[...], preferred_element_type=F32
        )
        for h in range(2):
            move(
                slots[h], lines[h], picked[:, h * z.main : (h + 1) * z.main], hats[h], z.width_x
            )
        return carry

    line = [tails_to_lanes(z, places_ref, c) for c in range(3)]
    hat_x = hat_tables(*line, None, z.width_x, None, z.width_y, plane_ref, 0, 0)
    picked = jnp.dot(
        flow_ref[...].astype(BF16), plane_ref[:, :LANES], preferred_element_type=F32
    )
    rows = places_ref.shape[1]
    lane = lane_index((rows, LANES))
    row = row_index((rows, LANES))
    for c in range(3):
        drift = jnp.sum(picked[c * z.width_x : (c + 1) * z.width_x] * hat_x, axis=0, keepdims=True)
        ends = places_ref[c, :, z.main :]
        for t in range(z.tail):
            moved = jnp.sum(
                jnp.where(lane == row * z.tail + t, drift, 0.0), axis=1, keepdims=True
            )
            ends = jnp.where(lane == t, ends + moved, ends)
        places_ref[c, :, z.main :] = ends
    lax.fori_loop(0, lists_ref[0], fast, 0)
    lax.fori_loop(0, lists_ref[1], slow, 0)


def collide(z, flow_ref, grid_ref, post_ref):
    def block(r, carry):
        rows = pl.ds(pl.multiple_of(r * 8, 8), 8)
        for t in range(z.plane // LANES):
            lanes = slice(t * LANES, (t + 1) * LANES)
            f = [flow_ref[q, rows, lanes] for q in range(19)]
            push = [
                PUSH_SCALE
                * grid_ref[pl.ds(pl.multiple_of(c * z.width_x + r * 8, 8), 8), lanes]
                for c in range(3)
            ]
            density = f[0]
            for q in range(1, 19):
                density = density + f[q]
            inverse = 1.0 / density
            u = []
            for c in range(3):
                m = 0.5 * push[c]
                for q in range(1, 19):
                    v = LATTICE_VELOCITY[q][c]
                    if v == 1:
                        m = m + f[q]
                    elif v == -1:
                        m = m - f[q]
                u.append(m * inverse)
            square = u[0] * u[0] + u[1] * u[1] + u[2] * u[2]
            work = u[0] * push[0] + u[1] * push[1] + u[2] * push[2]
            gain = 1.0 - 0.5 * RELAX_RATE
            heavy = RELAX_RATE * density
            base = heavy * (1.0 - 1.5 * square) - (3.0 * gain) * work
            post_ref[0, rows, lanes] = (1.0 - RELAX_RATE) * f[0] + LATTICE_WEIGHT[0] * base
            for q in range(1, 19, 2):
                along = None
                pull = None
                for c in range(3):
                    v = LATTICE_VELOCITY[q][c]
                    if v:
                        along = v * u[c] if along is None else along + v * u[c]
                        pull = v * push[c] if pull is None else pull + v * push[c]
                w = LATTICE_WEIGHT[q]
                lifted = heavy * along
                even = w * (base + along * (4.5 * lifted + (9.0 * gain) * pull))
                odd = (3.0 * w) * (lifted + gain * pull)
                post_ref[q, rows, lanes] = (1.0 - RELAX_RATE) * f[q] + (even + odd)
                post_ref[q + 1, rows, lanes] = (1.0 - RELAX_RATE) * f[q + 1] + (even - odd)
        return carry

    lax.fori_loop(0, z.width_x // 8, block, 0)


def write_edges(z, post_ref, right_ref, left_ref, up_ref, down_ref):
    for number, q in enumerate(RIGHT_MOVERS):
        right_ref[number : number + 1, :] = post_ref[q, z.width_x - 1 : z.width_x, :]
    for number, q in enumerate(LEFT_MOVERS):
        left_ref[number : number + 1, :] = post_ref[q, 0:1, :]
    right_ref[5:8, :] = jnp.zeros((3, z.plane), F32)
    left_ref[5:8, :] = jnp.zeros((3, z.plane), F32)
    lane = lane_index((z.width_x, LANES))
    up = jnp.zeros((z.width_x, LANES), F32)
    down = jnp.zeros((z.width_x, LANES), F32)
    for number, q in enumerate(UPWARD_MOVERS):
        here = (lane >= number * CZ) & (lane < (number + 1) * CZ)
        value = post_ref[q, :, z.plane - LANES :]
        up = jnp.where(here, pltpu.roll(value, (number + 1) * CZ, 1), up)
    for number, q in enumerate(DOWNWARD_MOVERS):
        here = (lane >= number * CZ) & (lane < (number + 1) * CZ)
        value = post_ref[q, :, :LANES]
        down = jnp.where(here, value if number == 0 else pltpu.roll(value, number * CZ, 1), down)
    up_ref[...] = up
    down_ref[...] = down


def stream(z, post_ref, from_left_ref, from_right_ref, below_ref, above_ref, out_ref, grid_ref, flow_ref):
    shape = (z.width_x, z.plane)
    lane = lane_index(shape)
    row = row_index(shape)
    edge_row = row_index((z.width_x, LANES))
    layer = lax.rem(lane, CZ)
    last_row = z.width_x - 1
    sums = [None] * 4
    for q in range(19):
        cx, cy, cz = LATTICE_VELOCITY[q]
        value = post_ref[q]
        if cx == 1:
            k = RIGHT_MOVERS.index(q)
            value = jnp.where(row == 0, from_left_ref[k : k + 1, :], pltpu.roll(value, 1, 0))
        elif cx == -1:
            k = LEFT_MOVERS.index(q)
            value = jnp.where(
                row == last_row, from_right_ref[k : k + 1, :], pltpu.roll(value, last_row, 0)
            )
        if cy:
            edges = below_ref if cy == 1 else above_ref
            k = (UPWARD_MOVERS if cy == 1 else DOWNWARD_MOVERS).index(q)
            edge = edges[: z.width_x, :]
            shift = (LANES - k * CZ if cy == 1 else 2 * LANES - (k + 1) * CZ) % LANES
            edge = edge if shift == 0 else pltpu.roll(edge, shift, 1)
            if cx:
                movers = RIGHT_MOVERS if cx == 1 else LEFT_MOVERS
                at = z.width_x + (0 if cx == 1 else 8) + movers.index(q)
                corner = edges[at : at + 1, :]
                turn = CZ if cy == 1 else LANES - CZ
                corner = pltpu.roll(corner, turn, 1)
                if cx == 1:
                    edge = jnp.where(edge_row == 0, corner, pltpu.roll(edge, 1, 0))
                else:
                    edge = jnp.where(edge_row == last_row, corner, pltpu.roll(edge, last_row, 0))
            rest = jnp.zeros((z.width_x, z.plane - LANES), F32)
            if cy == 1:
                wide = jnp.concatenate([edge, rest], axis=1)
                value = jnp.where(lane < CZ, wide, pltpu.roll(value, CZ, 1))
            else:
                wide = jnp.concatenate([rest, edge], axis=1)
                value = jnp.where(lane >= z.plane - CZ, wide, pltpu.roll(value, z.plane - CZ, 1))
        if cz == 1:
            value = jnp.where(
                layer == 0, pltpu.roll(value, z.plane - (CZ - 1), 1), pltpu.roll(value, 1, 1)
            )
        elif cz == -1:
            value = jnp.where(
                layer == CZ - 1, pltpu.roll(value, CZ - 1, 1), pltpu.roll(value, z.plane - 1, 1)
            )
        out_ref[q] = value
    for r in range(z.width_x // 8):
        rows = slice(r * 8, (r + 1) * 8)
        for t in range(z.plane // LANES):
            lanes = slice(t * LANES, (t + 1) * LANES)
            f = [out_ref[q, rows, lanes] for q in range(19)]
            density = f[0]
            for q in range(1, 19):
                density = density + f[q]
            inverse = 1.0 / density
            for c in range(3):
                m = (0.5 * PUSH_SCALE) * grid_ref[
                    c * z.width_x + r * 8 : c * z.width_x + (r + 1) * 8, lanes
                ]
                for q in range(1, 19):
                    v = LATTICE_VELOCITY[q][c]
                    if v == 1:
                        m = m + f[q]
                    elif v == -1:
                        m = m - f[q]
                sums[c] = m * inverse
            for c in range(3):
                flow_ref[c * z.width_x + r * 8 : c * z.width_x + (r + 1) * 8, lanes] = sums[c]


def first_kernel(z, *refs):
    d = z.devices_y
    messages = refs[:d]
    shape_ref, link_ref, degree_ref, flow_ref = refs[d : d + 4]
    grid_ref, post_ref, right_ref, left_ref, up_ref, down_ref = refs[d + 4 : d + 10]
    places_ref, stiff_ref, lists_ref = refs[d + 10 : d + 13]
    ends, force, plane, lift = refs[d + 13 :]
    for e in range(d):
        for h in range(3):
            split_message(z, messages[e][h], places_ref, ends, (3 * e + h) * CAP)
    place_tails(z, ends, places_ref, stiff_ref)
    list_slots(z, places_ref, stiff_ref, lists_ref)
    forces(z, places_ref, stiff_ref, shape_ref, link_ref, degree_ref, force)
    spread(z, places_ref, force, lists_ref, grid_ref, plane, lift)
    collide(z, flow_ref, grid_ref, post_ref)
    write_edges(z, post_ref, right_ref, left_ref, up_ref, down_ref)


def middle_kernel(z, *refs):
    post_ref, from_left, from_right, below, above = refs[:5]
    old_grid, old_places, stiff_ref, old_lists, shape_ref, link_ref, degree_ref = refs[5:12]
    grid_ref, next_ref, right_ref, left_ref, up_ref, down_ref, places_ref, lists_ref = refs[12:20]
    moved, flow, force, plane, lift = refs[20:]
    places_ref[...] = old_places[...]
    stream(z, post_ref, from_left, from_right, below, above, moved, old_grid, flow)
    sample(z, places_ref, flow, old_lists, plane)
    list_slots(z, places_ref, stiff_ref, lists_ref)
    forces(z, places_ref, stiff_ref, shape_ref, link_ref, degree_ref, force)
    spread(z, places_ref, force, lists_ref, grid_ref, plane, lift)
    collide(z, moved, grid_ref, next_ref)
    write_edges(z, next_ref, right_ref, left_ref, up_ref, down_ref)


def join_message(z, places_ref, slot, out_ref, at):
    lane = lane_index((CAP, LANES))
    ends = jnp.zeros((CAP, LANES), F32)
    for c in range(3):
        line = places_ref[c, slot : slot + CAP, :]
        out_ref[at, :, c * z.main : (c + 1) * z.main] = line[:, : z.main]
        end = jnp.where(lane < z.tail, line[:, z.main :], 0.0)
        ends = ends + (end if c == 0 else pltpu.roll(end, c * z.tail, 1))
    out_ref[at, :, 3 * z.main :] = ends


def last_kernel(z, *refs):
    d = z.devices_y
    post_ref, from_left, from_right, below, above, grid_ref, old_places, lists_ref = refs[:8]
    moved_ref = refs[8]
    message_refs = refs[9 : 9 + d]
    flow, places, plane = refs[9 + d :]
    places[...] = old_places[...]
    stream(z, post_ref, from_left, from_right, below, above, moved_ref, grid_ref, flow)
    sample(z, places, flow, lists_ref, plane)
    for e in range(d):
        for h in range(3):
            join_message(z, places, (3 * e + h) * CAP, message_refs[e], h)


def shift(value, axis, step):
    count = lax.axis_size(axis)
    return lax.ppermute(value, axis, [(i, (i + step) % count) for i in range(count)])


def trade_edges(z, right, left, up, down):
    from_left = shift(right, "gx", 1)
    from_right = shift(left, "gx", -1)
    far, near = slice(z.plane - LANES, z.plane), slice(0, LANES)
    up = jnp.concatenate([up, from_left[:, far], from_right[:, far]], axis=0)
    down = jnp.concatenate([down, from_left[:, near], from_right[:, near]], axis=0)
    return from_left, from_right, shift(up, "gy", 1), shift(down, "gy", -1)


def local(populations, positions, stiffness, membrane_shape, neighbours, home_tile):
    z = Sizes(
        positions.shape[0],
        positions.shape[2],
        populations.shape[1],
        populations.shape[2],
        lax.axis_size("gx"),
        lax.axis_size("gy"),
    )
    d = z.devices_y
    run = functools.partial
    line = (CAP, z.message)
    table = VMEM((z.groups,) + line, F32)
    counts = SMEM((z.groups,), jnp.int32)
    places_in = positions.transpose(1, 0, 2)
    to_left, center, to_right = call(
        run(pack_kernel, z),
        [((d,) + line, F32, VMEM)] * 3,
        [SMEM, SMEM, VMEM],
        [table, counts],
    )(home_tile, stiffness, places_in)
    from_left = shift(to_right, "gx", 1)
    from_right = shift(to_left, "gx", -1)
    messages = [jnp.stack([center[e], from_left[e], from_right[e]]) for e in range(d)]
    messages = [messages[0]] + [shift(messages[e], "gy", e) for e in range(1, d)]
    link, degree, shape = call(
        run(matrix_kernel, z),
        [
            ((z.full, z.full), BF16, VMEM),
            ((1, z.full), F32, VMEM),
            ((3, z.full), F32, VMEM),
        ],
        [VMEM, VMEM],
        [VMEM((z.full, z.full), F32)],
        pl.CostEstimate(flops=2_000_000_000, bytes_accessed=4_000_000, transcendentals=0),
    )(neighbours.T, membrane_shape)

    grid_type = ((3 * z.width_x, z.plane), F32, VMEM)
    post_type = ((19, z.width_x, z.plane), F32, VMEM)
    plane_scratch = VMEM((z.plane, 2 * z.main), BF16)
    lift_scratch = VMEM((3 * z.width_x, 2 * z.main), BF16)
    edge_types = [((8, z.plane), F32, VMEM)] * 2 + [((z.width_x, LANES), F32, VMEM)] * 2
    places_type = ((3, z.slots, z.full), F32, VMEM)
    lists_type = ((LISTS,), jnp.int32, SMEM)
    rows = VMEM(places_type[0], F32)

    grid, post, right, left, up, down, places, stiff, lists = call(
        run(first_kernel, z),
        [grid_type, post_type]
        + edge_types
        + [places_type, ((z.slots, LANES), F32, VMEM), lists_type],
        [VMEM] * (d + 4),
        [VMEM((z.slots, LANES), F32), rows, plane_scratch, lift_scratch],
    )(*messages, shape, link, degree, populations)
    for _ in range(STEPS - 1):
        edges = trade_edges(z, right, left, up, down)
        grid, post, right, left, up, down, places, lists = call(
            run(middle_kernel, z),
            [grid_type, post_type] + edge_types + [places_type, lists_type],
            [VMEM] * 8 + [SMEM] + [VMEM] * 3,
            [VMEM(post_type[0], F32), VMEM(grid_type[0], F32), rows, plane_scratch, lift_scratch],
        )(post, *edges, grid, places, stiff, lists, shape, link, degree)
    edges = trade_edges(z, right, left, up, down)
    moved, *messages = call(
        run(last_kernel, z),
        [post_type] + [((3,) + line, F32, VMEM)] * d,
        [VMEM] * 7 + [SMEM],
        [VMEM(grid_type[0], F32), rows, plane_scratch],
    )(post, *edges, grid, places, lists)
    messages = [messages[0]] + [shift(messages[e], "gy", -e) for e in range(1, d)]
    right_part = shift(jnp.stack([m[1] for m in messages]), "gx", -1)
    left_part = shift(jnp.stack([m[2] for m in messages]), "gx", 1)
    (displacement,) = call(
        run(unpack_kernel, z),
        [(places_in.shape, F32, VMEM)],
        [SMEM] + [VMEM] * (3 + d),
        [table, counts],
    )(home_tile, places_in, left_part, right_part, *messages)
    return moved, displacement.transpose(1, 0, 2), grid.reshape(3, z.width_x, z.plane)


def solution(mesh):
    placed = (
        P(None, "gx", "gy"),
        P(("gx", "gy"), None, None),
        P(("gx", "gy")),
        P(),
        P(),
        P(("gx", "gy")),
    )
    return jax.shard_map(
        local,
        mesh=mesh,
        in_specs=placed,
        out_specs=(P(None, "gx", "gy"), P(("gx", "gy"), None, None), P(None, "gx", "gy")),
        check_vma=False,
    )
```

time: 105 us -> 87.8 us (0.84)
  starting transfers between devices: 45.1 us -> 28.9 us
  waiting for transfers between devices: 16.6 us -> 22.3 us
  Pallas kernels: 37.3 us -> 31.7 us
  local copies, waits for them, and re-layouts: 6.46 us -> 4.68 us
    ppermute x24 -> x18, starting transfers between devices: 45.1 us -> 28.9 us  [shift(): lax.ppermute(value, axis, [(i, (i + step) % count) for i in range(count)])]
    ppermute x24 -> x18, waiting for transfers between devices: 16.6 us -> 22.3 us  [shift(): lax.ppermute(value, axis, [(i, (i + step) % count) for i in range(count)])]
    pallas_call x6 -> x4, Pallas kernels: 20 us -> 16.7 us  [the longest x1 7.45 us: local(): call(run(first_kernel, z), [grid_type, post_type] + edge_types + [places_...]
    pallas_call x1, Pallas kernels: 3.66 us -> 1.7 us  [local(): call(run(matrix_kernel, z), [((z.full, z.full), BF16, VMEM), ((1, z.full)...]
    unnamed x13 -> x18, local copies, waits for them, and re-layouts: 4.92 us -> 4.62 us
  transfers between devices with their start and end apart: 24 -> 18, of which waited for: 14 -> 14; matrix products, arithmetic and copies ran while one was open for 2% -> 0% of each run, Pallas kernels for 8% -> 2%
where the time goes in v1:
time: 87.8 us; the launch traced here: 88.5 us
  Pallas kernels  31.7 us (36%)
  starting transfers between devices  28.9 us (33%)
  waiting for transfers between devices  22.3 us (25%)
  local copies, waits for them, and re-layouts  4.68 us (5%)
    ppermute x18, starting transfers between devices, shift(): lax.ppermute(value, axis, [(i, (i + step) % count) for i in range(count)])  28.9 us
    ppermute x18, waiting for transfers between devices, shift(): lax.ppermute(value, axis, [(i, (i + step) % count) for i in range(count)])  22.3 us
    pallas_call x1, Pallas kernels, local(): call(run(middle_kernel, z), [grid_type, post_type] + edge_types + [places...  13.2 us
    pallas_call x1, Pallas kernels, local(): call(run(first_kernel, z), [grid_type, post_type] + edge_types + [places_...  7.45 us
    pallas_call x1, Pallas kernels, local(): call(run(last_kernel, z), [post_type] + [((3,) + line, F32, VMEM)] * d, [...  6.7 us
    unnamed x18, local copies, waits for them, and re-layouts  4.62 us
  transfers between devices with their start and end apart: 18, of which 14 were waited for; matrix products, arithmetic and copies ran while one was open for 0% of the time, Pallas kernels for 2%

profile of v1, /device:TPU:0, one launch (start us, length us, event | category | flops | bytes accessed | tf_op | source)
XLA Modules:
  0.0 88.5 jit_solution(3587168889496577263)
XLA Ops:
  0.6 0.0 copy-start.1
  0.6 0.9 %copy-done.1 = f32[24,3,642]{2,0,1:T(8,128)S(1)} copy-done((f32[24,3,642]{2,0,1:T(8,128)S(1)}, f32[24,3,642]{2,0,1:T(8,128)}, u32[]{:S(2)}) %copy-start.1) | copy-done | bytes 184920
  1.6 0.0 copy-start.4
  1.6 0.7 copy-done.4
  2.2 0.0 copy-start.6
  2.2 0.7 copy-done.6
  2.9 1.0 %shard_map.85 = (f32[4,4,2048]{2,1,0:T(4,128)S(1)}, f32[4,4,2048]{2,1,0:T(4,128)S(1)}, f32[4,4,2048]{2,1,0:T(4,128)S(1)}) custom-call(s32[24]{0:T(128)S(1)} %copy-done.4, f32[24]{0:T(128)S(1)} %copy-done.6, f32[3,24,642]{2,1,0:T(8,128)S(1)} %bitcast.4), custom_call_target="tpu_custom_call" | custom-call | tf_op jit(solution)/shard_map/pallas_call | solution.py:687
  3.8 3.0 %collective-permute-start = (f32[4,4,2048]{2,1,0:T(4,128)S(1)}, f32[4,4,2048]{2,1,0:T(4,128)S(1)}, u32[]{:S(2)}, u32[]{:S(2)}) collective-permute-start(f32[4,4,2048]{2,1,0:T(4,128)S(1)} %get-tuple-element.32), channel_id=1, source_target_pairs={{0,4},{4,8},{8,12},{12,16},{16,20},{20,24},{24,28},{28,0},{1,5},{5... | collective-permute-start | bytes 393224 | tf_op jit(solution)/shard_map/ppermute | solution.py:660
  6.9 3.1 %collective-permute-start.1 = (f32[4,4,2048]{2,1,0:T(4,128)S(1)}, f32[4,4,2048]{2,1,0:T(4,128)S(1)}, u32[]{:S(2)}, u32[]{:S(2)}) collective-permute-start(f32[4,4,2048]{2,1,0:T(4,128)S(1)} %get-tuple-element.33), channel_id=1, source_target_pairs={{0,28},{4,0},{8,4},{12,8},{16,12},{20,16},{24,20},{28,24},{1,29},{... | collective-permute-start | bytes 393224 | tf_op jit(solution)/shard_map/ppermute | solution.py:660
  10.0 0.0 copy-start.7
  10.0 0.7 copy-done.7
  10.7 0.0 copy-start.8
  10.7 0.7 copy-done.8
  11.4 1.7 %shard_map.86 = (bf16[768,768]{1,0:T(8,128)(2,1)S(1)}, f32[1,768]{1,0:T(1,128)S(1)}, f32[3,768]{1,0:T(4,128)S(1)}) custom-call(s32[6,642]{1,0:T(8,128)S(1)} %bitcast.7, f32[3,642]{1,0:T(4,128)S(1)} %copy-done.8), custom_call_target="tpu_custom_call" | custom-call | flops 2000000000 | bytes 4000000 | tf_op jit(solution)/shard_map/pallas_call | solution.py:697
  13.1 0.0 copy-start
  13.1 0.4 collective-permute-done
  13.5 1.1 %collective-permute-done.1 = f32[4,4,2048]{2,1,0:T(4,128)S(1)} collective-permute-done((f32[4,4,2048]{2,1,0:T(4,128)S(1)}, f32[4,4,2048]{2,1,0:T(4,128)S(1)}, u32[]{:S(2)}, u32[]{:S(2)}) %collective-permute-start.1) | collective-permute-done | bytes 131104 | tf_op jit(solution)/shard_map/ppermute | solution.py:660
  14.7 0.1 collective-permute-start.2
  14.8 1.6 %collective-permute-start.3 = (f32[3,4,2048]{2,1,0:T(4,128)S(1)}, f32[3,4,2048]{2,1,0:T(4,128)S(1)}, u32[]{:S(2)}, u32[]{:S(2)}) collective-permute-start(f32[3,4,2048]{2,1,0:T(4,128)S(1)} %pad_maximum_fusion.4), channel_id=1, source_target_pairs={{0,2},{1,3},{2,0},{3,1},{4,6},{5,7},{6,4},{7,5},{8,10},{9,11},{10,... | collective-permute-start | bytes 294920 | tf_op jit(solution)/shard_map/ppermute | solution.py:660
  16.4 1.5 %collective-permute-start.4 = (f32[3,4,2048]{2,1,0:T(4,128)S(1)}, f32[3,4,2048]{2,1,0:T(4,128)S(1)}, u32[]{:S(2)}, u32[]{:S(2)}) collective-permute-start(f32[3,4,2048]{2,1,0:T(4,128)S(1)} %pad_maximum_fusion.5), channel_id=1, source_target_pairs={{0,3},{1,0},{2,1},{3,2},{4,7},{5,4},{6,5},{7,6},{8,11},{9,8},{10,9... | collective-permute-start | bytes 294920 | tf_op jit(solution)/shard_map/ppermute | solution.py:660
  17.9 1.2 %collective-permute-done.2.refs_1_ = f32[3,4,2048]{2,1,0:T(4,128)S(1)} collective-permute-done((f32[3,4,2048]{2,1,0:T(4,128)S(1)}, f32[3,4,2048]{2,1,0:T(4,128)S(1)}, u32[]{:S(2)}, u32[]{:S(2)}) %collective-permute-start.2) | collective-permute-done | bytes 98336 | tf_op jit(solution)/shard_map/ppermute | solution.py:660
  19.1 1.4 %collective-permute-done.3.refs_2_ = f32[3,4,2048]{2,1,0:T(4,128)S(1)} collective-permute-done((f32[3,4,2048]{2,1,0:T(4,128)S(1)}, f32[3,4,2048]{2,1,0:T(4,128)S(1)}, u32[]{:S(2)}, u32[]{:S(2)}) %collective-permute-start.3) | collective-permute-done | bytes 98336 | tf_op jit(solution)/shard_map/ppermute | solution.py:660
  20.5 0.5 collective-permute-done.4.refs_3_
  21.0 0.0 copy-done
  21.0 7.4 %shard_map.87 = (f32[96,512]{1,0:T(8,128)S(1)}, f32[19,32,512]{2,1,0:T(8,128)S(1)}, f32[8,512]{1,0:T(8,128)S(1)}, f32[8,512]{1,0:T(8,128)S(1)}, f32[32,128]{1,0:...) custom-call(f32[3,4,2048]{2,1,0:T(4,128)S(1)} %pad_maximum_fusion.2.re, ...), custom_call_target="tpu_custom_call" | custom-call | tf_op jit(solution)/shard_map/pallas_call | solution.py:718
  28.4 2.5 %collective-permute-start.5 = (f32[8,512]{1,0:T(8,128)S(1)}, f32[8,512]{1,0:T(8,128)S(1)}, u32[]{:S(2)}, u32[]{:S(2)}) collective-permute-start(f32[8,512]{1,0:T(8,128)S(1)} %get-tuple-element.38), channel_id=1, source_target_pairs={{0,4},{4,8},{8,12},{12,16},{16,20},{20,24},{24,28},{28,0},{1,5},{5... | collective-permute-start | bytes 49160 | tf_op jit(solution)/shard_map/ppermute | solution.py:660
  30.9 2.3 %collective-permute-start.6 = (f32[8,512]{1,0:T(8,128)S(1)}, f32[8,512]{1,0:T(8,128)S(1)}, u32[]{:S(2)}, u32[]{:S(2)}) collective-permute-start(f32[8,512]{1,0:T(8,128)S(1)} %get-tuple-element.39), channel_id=1, source_target_pairs={{0,28},{4,0},{8,4},{12,8},{16,12},{20,16},{24,20},{28,24},{1,29},{... | collective-permute-start | bytes 49160 | tf_op jit(solution)/shard_map/ppermute | solution.py:660
  33.2 1.8 %collective-permute-done.5.refs_1_ = f32[8,512]{1,0:T(8,128)S(1)} collective-permute-done((f32[8,512]{1,0:T(8,128)S(1)}, f32[8,512]{1,0:T(8,128)S(1)}, u32[]{:S(2)}, u32[]{:S(2)}) %collective-permute-start.5) | collective-permute-done | bytes 16416 | tf_op jit(solution)/shard_map/ppermute | solution.py:660
  35.0 0.0 collective-permute-done.6.refs_2_
  35.0 0.1 collective-permute-start.7
  35.1 1.7 %collective-permute-start.8 = (f32[48,128]{1,0:T(8,128)S(1)}, f32[48,128]{1,0:T(8,128)S(1)}, u32[]{:S(2)}, u32[]{:S(2)}) collective-permute-start(f32[48,128]{1,0:T(8,128)S(1)} %pad_maximum_fusion.7), channel_id=1, source_target_pairs={{0,3},{1,0},{2,1},{3,2},{4,7},{5,4},{6,5},{7,6},{8,11},{9,8},{10,9... | collective-permute-start | bytes 73736 | tf_op jit(solution)/shard_map/ppermute | solution.py:660
  36.8 1.5 %collective-permute-done.7.refs_3_ = f32[48,128]{1,0:T(8,128)S(1)} collective-permute-done((f32[48,128]{1,0:T(8,128)S(1)}, f32[48,128]{1,0:T(8,128)S(1)}, u32[]{:S(2)}, u32[]{:S(2)}) %collective-permute-start.7) | collective-permute-done | bytes 24608 | tf_op jit(solution)/shard_map/ppermute | solution.py:660
  38.3 0.0 collective-permute-done.8.refs_4_
  38.4 13.2 %shard_map.88 = (f32[96,512]{1,0:T(8,128)}, f32[19,32,512]{2,1,0:T(8,128)S(1)}, f32[8,512]{1,0:T(8,128)S(1)}, f32[8,512]{1,0:T(8,128)S(1)}, f32[32,128]{1,0:T(8,...) custom-call(f32[19,32,512]{2,1,0:T(8,128)S(1)} %get-tuple-element.37.refs_0_, ...), custom_call_target="tpu_custom_call" | custom-call | tf_op jit(solution)/shard_map/pallas_call | solution.py:728
  51.6 4.6 %collective-permute-start.9 = (f32[8,512]{1,0:T(8,128)S(1)}, f32[8,512]{1,0:T(8,128)S(1)}, u32[]{:S(2)}, u32[]{:S(2)}) collective-permute-start(f32[8,512]{1,0:T(8,128)S(1)} %get-tuple-element.47), channel_id=1, source_target_pairs={{0,4},{4,8},{8,12},{12,16},{16,20},{20,24},{24,28},{28,0},{1,5},{5... | collective-permute-start | bytes 49160 | tf_op jit(solution)/shard_map/ppermute | solution.py:660
  56.2 0.2 collective-permute-start.10
  56.4 1.8 %collective-permute-done.9.refs_1_ = f32[8,512]{1,0:T(8,128)S(1)} collective-permute-done((f32[8,512]{1,0:T(8,128)S(1)}, f32[8,512]{1,0:T(8,128)S(1)}, u32[]{:S(2)}, u32[]{:S(2)}) %collective-permute-start.9) | collective-permute-done | bytes 16416 | tf_op jit(solution)/shard_map/ppermute | solution.py:660
  58.2 1.8 %collective-permute-done.10.refs_2_ = f32[8,512]{1,0:T(8,128)S(1)} collective-permute-done((f32[8,512]{1,0:T(8,128)S(1)}, f32[8,512]{1,0:T(8,128)S(1)}, u32[]{:S(2)}, u32[]{:S(2)}) %collective-permute-start.10) | collective-permute-done | bytes 16416 | tf_op jit(solution)/shard_map/ppermute | solution.py:660
  60.0 0.0 collective-permute-start.11
  60.0 1.7 %collective-permute-start.12 = (f32[48,128]{1,0:T(8,128)S(1)}, f32[48,128]{1,0:T(8,128)S(1)}, u32[]{:S(2)}, u32[]{:S(2)}) collective-permute-start(f32[48,128]{1,0:T(8,128)S(1)} %pad_maximum_fusion.9), channel_id=1, source_target_pairs={{0,3},{1,0},{2,1},{3,2},{4,7},{5,4},{6,5},{7,6},{8,11},{9,8},{10,9... | collective-permute-start | bytes 73736 | tf_op jit(solution)/shard_map/ppermute | solution.py:660
  61.7 1.7 %collective-permute-done.11.refs_3_ = f32[48,128]{1,0:T(8,128)S(1)} collective-permute-done((f32[48,128]{1,0:T(8,128)S(1)}, f32[48,128]{1,0:T(8,128)S(1)}, u32[]{:S(2)}, u32[]{:S(2)}) %collective-permute-start.11) | collective-permute-done | bytes 24608 | tf_op jit(solution)/shard_map/ppermute | solution.py:660
  63.4 0.0 collective-permute-done.12.refs_4_
  63.4 0.0 copy-start.3
  63.4 0.9 %copy-done.3 = f32[96,512]{1,0:T(8,128)S(1)} copy-done((f32[96,512]{1,0:T(8,128)S(1)}, f32[96,512]{1,0:T(8,128)}, u32[]{:S(2)}) %copy-start.3) | copy-done | bytes 196632
  64.3 0.0 copy-start.2
  64.3 0.0 copy-start.5
  64.3 6.7 %shard_map.89 = (f32[19,32,512]{2,1,0:T(8,128)}, f32[3,4,2048]{2,1,0:T(4,128)S(1)}, f32[3,4,2048]{2,1,0:T(4,128)S(1)}, f32[3,4,2048]{2,1,0:T(4,128)S(1)}, f32[3,4,2048]{2,1,0:T(4,128)S(1)}) custom-call(f32[19,32,512]{2,1,0:T(8,128)S(1)} %get-tuple-element.46.refs_0_, f32[8,512]{1,0:T(8,128)S(1)} %collective-permute-done.9.refs_1_, ...), custom_call_target="tpu_custom_call" | custom-call | tf_op jit(solution)/shard_map/pallas_call | solution.py:735
  71.0 0.7 collective-permute-start.13
  71.7 1.1 %collective-permute-start.14 = (f32[3,4,2048]{2,1,0:T(4,128)S(1)}, f32[3,4,2048]{2,1,0:T(4,128)S(1)}, u32[]{:S(2)}, u32[]{:S(2)}) collective-permute-start(f32[3,4,2048]{2,1,0:T(4,128)S(1)} %get-tuple-element.57), channel_id=1, source_target_pairs={{0,2},{1,3},{2,0},{3,1},{4,6},{5,7},{6,4},{7,5},{8,10},{9,11},{10,... | collective-permute-start | bytes 294920 | tf_op jit(solution)/shard_map/ppermute | solution.py:660
  72.7 0.0 collective-permute-start.15
  72.7 1.7 %collective-permute-done.13.rest_1_ = f32[3,4,2048]{2,1,0:T(4,128)S(1)} collective-permute-done((f32[3,4,2048]{2,1,0:T(4,128)S(1)}, f32[3,4,2048]{2,1,0:T(4,128)S(1)}, u32[]{:S(2)}, u32[]{:S(2)}) %collective-permute-start.13) | collective-permute-done | bytes 98336 | tf_op jit(solution)/shard_map/ppermute | solution.py:660
  74.5 3.8 %collective-permute-done.14.rest_2_ = f32[3,4,2048]{2,1,0:T(4,128)S(1)} collective-permute-done((f32[3,4,2048]{2,1,0:T(4,128)S(1)}, f32[3,4,2048]{2,1,0:T(4,128)S(1)}, u32[]{:S(2)}, u32[]{:S(2)}) %collective-permute-start.14) | collective-permute-done | bytes 98336 | tf_op jit(solution)/shard_map/ppermute | solution.py:660
  78.3 0.0 collective-permute-done.15.rest_3_
  78.4 1.7 %collective-permute-start.16 = (f32[4,4,2048]{2,1,0:T(4,128)S(1)}, f32[4,4,2048]{2,1,0:T(4,128)S(1)}, u32[]{:S(2)}, u32[]{:S(2)}) collective-permute-start(f32[4,4,2048]{2,1,0:T(4,128)S(1)} %pad_maximum_fusion), channel_id=1, source_target_pairs={{0,4},{4,8},{8,12},{12,16},{16,20},{20,24},{24,28},{28,0},{1,5},{5... | collective-permute-start | bytes 393224 | tf_op jit(solution)/shard_map/ppermute | solution.py:660
  80.1 3.2 %collective-permute-start.17 = (f32[4,4,2048]{2,1,0:T(4,128)S(1)}, f32[4,4,2048]{2,1,0:T(4,128)S(1)}, u32[]{:S(2)}, u32[]{:S(2)}) collective-permute-start(f32[4,4,2048]{2,1,0:T(4,128)S(1)} %pad_maximum_fusion.1), channel_id=1, source_target_pairs={{0,28},{4,0},{8,4},{12,8},{16,12},{20,16},{24,20},{28,24},{1,29},{... | collective-permute-start | bytes 393224 | tf_op jit(solution)/shard_map/ppermute | solution.py:660
  83.2 3.0 %collective-permute-done.16.left_ref = f32[4,4,2048]{2,1,0:T(4,128)S(1)} collective-permute-done((f32[4,4,2048]{2,1,0:T(4,128)S(1)}, f32[4,4,2048]{2,1,0:T(4,128)S(1)}, u32[]{:S(2)}, u32[]{:S(2)}) %collective-permute-start.16) | collective-permute-done | bytes 131104 | tf_op jit(solution)/shard_map/ppermute | solution.py:660
  86.2 0.7 collective-permute-done.17.right_ref
  86.9 0.0 copy-done.2
  86.9 0.0 copy-done.5
  86.9 1.6 %shard_map.90 = f32[3,24,642]{2,1,0:T(8,128)} custom-call(s32[24]{0:T(128)S(1)} %copy-done.5, f32[3,24,642]{2,1,0:T(8,128)S(1)} %bitcast.5, f32[4,4,2048]{2,1,0:T(4,128)S(1)} %collective-permute-done.16.left_ref, f32[4,4,2048]{2,1,0:T(4,128)S(1)} %collective-permute-done.17.right_ref, f32[3,4,2048]{2,1,0:T(4,128)S(1)} %get-tuple-element.55.rest_0_, ...), custom_call_target="tpu_custom_call" | custom-call | tf_op jit(solution)/shard_map/pallas_call | solution.py:744
  (21 shorter events, 0.2 us)
Async XLA Ops:
  0.6 0.9 %copy-start.1 = (f32[24,3,642]{2,0,1:T(8,128)S(1)}, f32[24,3,642]{2,0,1:T(8,128)}, u32[]{:S(2)}) copy-start(f32[24,3,642]{2,0,1:T(8,128)} %param.7) | copy-start | bytes 554692
  1.6 0.7 copy-start.4
  2.2 0.7 copy-start.6
  3.8 9.7 %collective-permute-start = (f32[4,4,2048]{2,1,0:T(4,128)S(1)}, f32[4,4,2048]{2,1,0:T(4,128)S(1)}, u32[]{:S(2)}, u32[]{:S(2)}) collective-permute-start(f32[4,4,2048]{2,1,0:T(4,128)S(1)} %get-tuple-element.32), channel_id=1, source_target_pairs={{0,4},{4,8},{8,12},{12,16},{16,20},{20,24},{24,28},{28,0},{1,5},{5... | collective-permute-start | bytes 393224 | tf_op jit(solution)/shard_map/ppermute | solution.py:660
  6.9 7.8 %collective-permute-start.1 = (f32[4,4,2048]{2,1,0:T(4,128)S(1)}, f32[4,4,2048]{2,1,0:T(4,128)S(1)}, u32[]{:S(2)}, u32[]{:S(2)}) collective-permute-start(f32[4,4,2048]{2,1,0:T(4,128)S(1)} %get-tuple-element.33), channel_id=1, source_target_pairs={{0,28},{4,0},{8,4},{12,8},{16,12},{20,16},{24,20},{28,24},{1,29},{... | collective-permute-start | bytes 393224 | tf_op jit(solution)/shard_map/ppermute | solution.py:660
  10.0 0.7 copy-start.7
  10.7 0.7 copy-start.8
  13.1 7.9 %copy-start = (f32[19,32,512]{2,1,0:T(8,128)S(1)}, f32[19,32,512]{2,1,0:T(8,128)}, u32[]{:S(2)}) copy-start(f32[19,32,512]{2,1,0:T(8,128)} %refs_7_.1) | copy-start | bytes 3735556
  14.7 4.5 %collective-permute-start.2 = (f32[3,4,2048]{2,1,0:T(4,128)S(1)}, f32[3,4,2048]{2,1,0:T(4,128)S(1)}, u32[]{:S(2)}, u32[]{:S(2)}) collective-permute-start(f32[3,4,2048]{2,1,0:T(4,128)S(1)} %pad_maximum_fusion.3), channel_id=1, source_target_pairs={{0,1},{1,2},{2,3},{3,0},{4,5},{5,6},{6,7},{7,4},{8,9},{9,10},{10,1... | collective-permute-start | bytes 294920 | tf_op jit(solution)/shard_map/ppermute | solution.py:660
  14.8 5.7 %collective-permute-start.3 = (f32[3,4,2048]{2,1,0:T(4,128)S(1)}, f32[3,4,2048]{2,1,0:T(4,128)S(1)}, u32[]{:S(2)}, u32[]{:S(2)}) collective-permute-start(f32[3,4,2048]{2,1,0:T(4,128)S(1)} %pad_maximum_fusion.4), channel_id=1, source_target_pairs={{0,2},{1,3},{2,0},{3,1},{4,6},{5,7},{6,4},{7,5},{8,10},{9,11},{10,... | collective-permute-start | bytes 294920 | tf_op jit(solution)/shard_map/ppermute | solution.py:660
  16.4 4.6 %collective-permute-start.4 = (f32[3,4,2048]{2,1,0:T(4,128)S(1)}, f32[3,4,2048]{2,1,0:T(4,128)S(1)}, u32[]{:S(2)}, u32[]{:S(2)}) collective-permute-start(f32[3,4,2048]{2,1,0:T(4,128)S(1)} %pad_maximum_fusion.5), channel_id=1, source_target_pairs={{0,3},{1,0},{2,1},{3,2},{4,7},{5,4},{6,5},{7,6},{8,11},{9,8},{10,9... | collective-permute-start | bytes 294920 | tf_op jit(solution)/shard_map/ppermute | solution.py:660
  28.4 6.6 %collective-permute-start.5 = (f32[8,512]{1,0:T(8,128)S(1)}, f32[8,512]{1,0:T(8,128)S(1)}, u32[]{:S(2)}, u32[]{:S(2)}) collective-permute-start(f32[8,512]{1,0:T(8,128)S(1)} %get-tuple-element.38), channel_id=1, source_target_pairs={{0,4},{4,8},{8,12},{12,16},{16,20},{20,24},{24,28},{28,0},{1,5},{5... | collective-permute-start | bytes 49160 | tf_op jit(solution)/shard_map/ppermute | solution.py:660
  30.9 4.1 %collective-permute-start.6 = (f32[8,512]{1,0:T(8,128)S(1)}, f32[8,512]{1,0:T(8,128)S(1)}, u32[]{:S(2)}, u32[]{:S(2)}) collective-permute-start(f32[8,512]{1,0:T(8,128)S(1)} %get-tuple-element.39), channel_id=1, source_target_pairs={{0,28},{4,0},{8,4},{12,8},{16,12},{20,16},{24,20},{28,24},{1,29},{... | collective-permute-start | bytes 49160 | tf_op jit(solution)/shard_map/ppermute | solution.py:660
  35.0 3.3 %collective-permute-start.7 = (f32[48,128]{1,0:T(8,128)S(1)}, f32[48,128]{1,0:T(8,128)S(1)}, u32[]{:S(2)}, u32[]{:S(2)}) collective-permute-start(f32[48,128]{1,0:T(8,128)S(1)} %pad_maximum_fusion.6), channel_id=1, source_target_pairs={{0,1},{1,2},{2,3},{3,0},{4,5},{5,6},{6,7},{7,4},{8,9},{9,10},{10,1... | collective-permute-start | bytes 73736 | tf_op jit(solution)/shard_map/ppermute | solution.py:660
  35.1 3.2 %collective-permute-start.8 = (f32[48,128]{1,0:T(8,128)S(1)}, f32[48,128]{1,0:T(8,128)S(1)}, u32[]{:S(2)}, u32[]{:S(2)}) collective-permute-start(f32[48,128]{1,0:T(8,128)S(1)} %pad_maximum_fusion.7), channel_id=1, source_target_pairs={{0,3},{1,0},{2,1},{3,2},{4,7},{5,4},{6,5},{7,6},{8,11},{9,8},{10,9... | collective-permute-start | bytes 73736 | tf_op jit(solution)/shard_map/ppermute | solution.py:660
  51.6 6.6 %collective-permute-start.9 = (f32[8,512]{1,0:T(8,128)S(1)}, f32[8,512]{1,0:T(8,128)S(1)}, u32[]{:S(2)}, u32[]{:S(2)}) collective-permute-start(f32[8,512]{1,0:T(8,128)S(1)} %get-tuple-element.47), channel_id=1, source_target_pairs={{0,4},{4,8},{8,12},{12,16},{16,20},{20,24},{24,28},{28,0},{1,5},{5... | collective-permute-start | bytes 49160 | tf_op jit(solution)/shard_map/ppermute | solution.py:660
  56.2 3.7 %collective-permute-start.10 = (f32[8,512]{1,0:T(8,128)S(1)}, f32[8,512]{1,0:T(8,128)S(1)}, u32[]{:S(2)}, u32[]{:S(2)}) collective-permute-start(f32[8,512]{1,0:T(8,128)S(1)} %get-tuple-element.48), channel_id=1, source_target_pairs={{0,28},{4,0},{8,4},{12,8},{16,12},{20,16},{24,20},{28,24},{1,29},{... | collective-permute-start | bytes 49160 | tf_op jit(solution)/shard_map/ppermute | solution.py:660
  60.0 3.4 %collective-permute-start.11 = (f32[48,128]{1,0:T(8,128)S(1)}, f32[48,128]{1,0:T(8,128)S(1)}, u32[]{:S(2)}, u32[]{:S(2)}) collective-permute-start(f32[48,128]{1,0:T(8,128)S(1)} %pad_maximum_fusion.8), channel_id=1, source_target_pairs={{0,1},{1,2},{2,3},{3,0},{4,5},{5,6},{6,7},{7,4},{8,9},{9,10},{10,1... | collective-permute-start | bytes 73736 | tf_op jit(solution)/shard_map/ppermute | solution.py:660
  60.0 3.4 %collective-permute-start.12 = (f32[48,128]{1,0:T(8,128)S(1)}, f32[48,128]{1,0:T(8,128)S(1)}, u32[]{:S(2)}, u32[]{:S(2)}) collective-permute-start(f32[48,128]{1,0:T(8,128)S(1)} %pad_maximum_fusion.9), channel_id=1, source_target_pairs={{0,3},{1,0},{2,1},{3,2},{4,7},{5,4},{6,5},{7,6},{8,11},{9,8},{10,9... | collective-permute-start | bytes 73736 | tf_op jit(solution)/shard_map/ppermute | solution.py:660
  63.4 0.9 %copy-start.3 = (f32[96,512]{1,0:T(8,128)S(1)}, f32[96,512]{1,0:T(8,128)}, u32[]{:S(2)}) copy-start(f32[96,512]{1,0:T(8,128)} %get-tuple-element.51.refs_5_) | copy-start | bytes 589828
  64.3 22.6 %copy-start.2 = (f32[24,3,642]{2,0,1:T(8,128)S(1)}, f32[24,3,642]{2,0,1:T(8,128)}, u32[]{:S(2)}) copy-start(f32[24,3,642]{2,0,1:T(8,128)} %param.7) | copy-start | bytes 554692
  64.3 22.6 %copy-start.5 = (s32[24]{0:T(128)S(1)}, s32[24]{0:T(128)}, u32[]{:S(2)}) copy-start(s32[24]{0:T(128)} %home_ref.3) | copy-start | bytes 292
  71.0 3.5 %collective-permute-start.13 = (f32[3,4,2048]{2,1,0:T(4,128)S(1)}, f32[3,4,2048]{2,1,0:T(4,128)S(1)}, u32[]{:S(2)}, u32[]{:S(2)}) collective-permute-start(f32[3,4,2048]{2,1,0:T(4,128)S(1)} %get-tuple-element.56), channel_id=1, source_target_pairs={{0,3},{1,0},{2,1},{3,2},{4,7},{5,4},{6,5},{7,6},{8,11},{9,8},{10,9... | collective-permute-start | bytes 294920 | tf_op jit(solution)/shard_map/ppermute | solution.py:660
  71.7 6.7 %collective-permute-start.14 = (f32[3,4,2048]{2,1,0:T(4,128)S(1)}, f32[3,4,2048]{2,1,0:T(4,128)S(1)}, u32[]{:S(2)}, u32[]{:S(2)}) collective-permute-start(f32[3,4,2048]{2,1,0:T(4,128)S(1)} %get-tuple-element.57), channel_id=1, source_target_pairs={{0,2},{1,3},{2,0},{3,1},{4,6},{5,7},{6,4},{7,5},{8,10},{9,11},{10,... | collective-permute-start | bytes 294920 | tf_op jit(solution)/shard_map/ppermute | solution.py:660
  72.7 5.6 %collective-permute-start.15 = (f32[3,4,2048]{2,1,0:T(4,128)S(1)}, f32[3,4,2048]{2,1,0:T(4,128)S(1)}, u32[]{:S(2)}, u32[]{:S(2)}) collective-permute-start(f32[3,4,2048]{2,1,0:T(4,128)S(1)} %get-tuple-element.58), channel_id=1, source_target_pairs={{0,1},{1,2},{2,3},{3,0},{4,5},{5,6},{6,7},{7,4},{8,9},{9,10},{10,1... | collective-permute-start | bytes 294920 | tf_op jit(solution)/shard_map/ppermute | solution.py:660
  78.4 7.8 %collective-permute-start.16 = (f32[4,4,2048]{2,1,0:T(4,128)S(1)}, f32[4,4,2048]{2,1,0:T(4,128)S(1)}, u32[]{:S(2)}, u32[]{:S(2)}) collective-permute-start(f32[4,4,2048]{2,1,0:T(4,128)S(1)} %pad_maximum_fusion), channel_id=1, source_target_pairs={{0,4},{4,8},{8,12},{12,16},{16,20},{20,24},{24,28},{28,0},{1,5},{5... | collective-permute-start | bytes 393224 | tf_op jit(solution)/shard_map/ppermute | solution.py:660
  80.1 6.8 %collective-permute-start.17 = (f32[4,4,2048]{2,1,0:T(4,128)S(1)}, f32[4,4,2048]{2,1,0:T(4,128)S(1)}, u32[]{:S(2)}, u32[]{:S(2)}) collective-permute-start(f32[4,4,2048]{2,1,0:T(4,128)S(1)} %pad_maximum_fusion.1), channel_id=1, source_target_pairs={{0,28},{4,0},{8,4},{12,8},{16,12},{20,16},{24,20},{28,24},{1,29},{... | collective-permute-start | bytes 393224 | tf_op jit(solution)/shard_map/ppermute | solution.py:660

commit v2 on v1

--- a/solution.py
+++ b/solution.py
@@ -46,11 +46,12 @@
 FAST_AT = 2
 SLOW_AT = 64
 CODE_AT = 128
-LISTS = 256
+LISTS = 192
 F32 = jnp.float32
 BF16 = jnp.bfloat16
 SMEM = pltpu.SMEM
 VMEM = pltpu.VMEM
+HBM = pltpu.MemorySpace.HBM
 
 
 def spec(space):
@@ -91,6 +92,7 @@
         self.message = 3 * self.main + LANES
         self.groups = 3 * devices_y
         self.slots = 3 * devices_y * CAP
+        self.rows = self.slots + 8
         self.width_y = plane // CZ
 
 
@@ -105,7 +107,7 @@
         target_x = lax.div(home, z.devices_y)
         target_y = lax.rem(home, z.devices_y)
         side = lax.rem(target_x - own_x + 1 + z.devices_x, z.devices_x)
-        turn = lax.rem(target_y - own_y + z.devices_y, z.devices_y)
+        turn = lax.bitwise_xor(target_y, own_y)
         group = side * z.devices_y + turn
         rank = count_ref[group]
         count_ref[group] = rank + 1
@@ -113,8 +115,19 @@
     return found
 
 
-def pack_kernel(z, home_ref, stiff_ref, places_ref, left_ref, center_ref, right_ref, table_ref, count_ref):
+def pack_kernel(z, home_in, stiff_in, places_in, left_ref, center_ref, right_ref, *scratch):
+    home_ref, stiff_ref, places_ref, table_ref, count_ref, sem = scratch
+    copies = [
+        pltpu.make_async_copy(source, target, sem.at[k])
+        for k, (source, target) in enumerate(
+            [(home_in, home_ref), (stiff_in, stiff_ref), (places_in, places_ref)]
+        )
+    ]
+    for copy in copies:
+        copy.start()
     table_ref[...] = jnp.zeros_like(table_ref)
+    for copy in copies:
+        copy.wait()
     lane = lane_index((1, LANES))
     zeros = jnp.zeros((1, LANES - z.tail), F32)
     for n, (group, rank) in enumerate(cell_places(z, home_ref, count_ref)):
@@ -149,7 +162,16 @@
             out_ref[c, n : n + 1, :] = whole[:, : z.vertices] - places_ref[c, n : n + 1, :]
 
 
-def matrix_kernel(z, near_ref, shape_ref, link_ref, degree_ref, rest_ref, half_ref):
+def matrix_kernel(z, near_in, shape_in, after_in, link_ref, degree_ref, rest_ref, *scratch):
+    near_ref, shape_ref, half_ref, sem = scratch
+    copies = [
+        pltpu.make_async_copy(near_in, near_ref, sem.at[0]),
+        pltpu.make_async_copy(shape_in, shape_ref, sem.at[1]),
+    ]
+    for copy in copies:
+        copy.start()
+    for copy in copies:
+        copy.wait()
     near = near_ref[...]
     shape = shape_ref[...]
     rest_ref[...] = jnp.concatenate(
@@ -189,38 +211,40 @@
     lane = lane_index(ends.shape)
     for c in range(3):
         end = ends if c == 0 else pltpu.roll(ends, LANES - c * z.tail, 1)
-        places_ref[c, :, z.main :] = jnp.where(lane < z.tail, end, 0.0)
+        places_ref[c, : z.slots, z.main :] = jnp.where(lane < z.tail, end, 0.0)
+        places_ref[c, z.slots :, :] = jnp.zeros((8, z.full), F32)
     stiff_ref[...] = jnp.broadcast_to(ends[:, 3 * z.tail : 3 * z.tail + 1], ends.shape)
 
 
 def forces(z, places_ref, stiff_ref, shape_ref, link_ref, degree_ref, force_ref):
-    rows = places_ref.shape[1]
+    rows = z.slots
     lane = lane_index((rows, z.full))
     inside = lane < z.vertices
     parts = []
     for c in range(3):
-        x = places_ref[c]
+        x = places_ref[c, :rows, :]
         mean = jnp.sum(x, axis=1, keepdims=True) * (1.0 / z.vertices)
         parts.append(jnp.where(inside, x - mean - shape_ref[c : c + 1, :], 0.0))
     strain = jnp.concatenate(parts, axis=0)
     high = strain.astype(BF16)
     rest = strain - high.astype(F32)
     low = rest.astype(BF16)
-    link = link_ref[...]
-    linked = jnp.dot(high, link, preferred_element_type=F32) + jnp.dot(
-        low, link, preferred_element_type=F32
+    both = jnp.dot(
+        jnp.concatenate([high, low], axis=0), link_ref[...], preferred_element_type=F32
     )
+    linked = both[: 3 * rows] + both[3 * rows :]
     pulled = degree_ref[...] * (high.astype(F32) + low.astype(F32)) - linked
     stiff = stiff_ref[:, 0:1]
     for c in range(3):
-        force_ref[c] = -stiff * pulled[c * rows : (c + 1) * rows]
+        force_ref[c, :rows, :] = -stiff * pulled[c * rows : (c + 1) * rows]
+        force_ref[c, rows:, :] = jnp.zeros((8, z.full), F32)
 
 
 def list_slots(z, places_ref, stiff_ref, lists_ref):
     codes = None
     fits = None
     for c, width in ((0, z.width_x), (1, z.width_y)):
-        x = places_ref[c, :, : z.main]
+        x = places_ref[c, : z.slots, : z.main]
         low = jnp.maximum(jnp.floor(jnp.min(x, axis=1, keepdims=True)), 0.0)
         high = jnp.minimum(jnp.floor(jnp.max(x, axis=1, keepdims=True)) + 1.0, width - 1.0)
         block = jnp.minimum(jnp.floor(low * 0.125), (width - WINDOW) // 8 * 1.0)
@@ -229,46 +253,19 @@
         fits = fit if fits is None else fits & fit
     codes = jnp.where(fits, codes, SLOW * 1.0)
     codes = jnp.where(stiff_ref[:, 0:1] > 0.0, codes, -1.0).astype(jnp.int32)
+    fast, slow = jnp.int32(0), jnp.int32(0)
     for s in range(z.slots):
-        lists_ref[CODE_AT + s] = codes[s, 0]
-
-    def step(s, state):
-        fast, slow, empty = state
-        code = lists_ref[CODE_AT + s]
-        is_slow = code == SLOW
-        is_fast = (code >= 0) & (code < SLOW)
-
-        @pl.when(is_fast)
-        def _():
-            lists_ref[FAST_AT + fast] = s
-
-        @pl.when(is_slow)
-        def _():
-            lists_ref[SLOW_AT + slow] = s
-
-        @pl.when(code < 0)
-        def _():
-            lists_ref[CODE_AT + s] = 0
-
-        return (
-            jnp.where(is_fast, fast + 1, fast),
-            jnp.where(is_slow, slow + 1, slow),
-            jnp.where(code < 0, s, empty),
-        )
-
-    zero = jnp.int32(0)
-    fast, slow, empty = lax.fori_loop(0, z.slots, step, (zero, zero, zero))
-
-    @pl.when(lax.rem(fast, 2) == 1)
-    def _():
-        lists_ref[FAST_AT + fast] = empty
-
-    @pl.when(lax.rem(slow, 2) == 1)
-    def _():
-        lists_ref[SLOW_AT + slow] = empty
-
-    lists_ref[0] = lax.div(fast + 1, 2)
-    lists_ref[1] = lax.div(slow + 1, 2)
+        code = codes[s, 0]
+        lists_ref[CODE_AT + s] = code
+        lists_ref[FAST_AT + fast] = s
+        lists_ref[SLOW_AT + slow] = s
+        fast = fast + jnp.where((code >= 0) & (code < SLOW), 1, 0)
+        slow = slow + jnp.where(code == SLOW, 1, 0)
+    lists_ref[CODE_AT + z.slots] = 0
+    for k in range(6):
+        lists_ref[FAST_AT + fast + k] = z.slots
+    lists_ref[0] = lax.div(fast + 3, 4)
+    lists_ref[1] = slow
 
 
 def window_of(lists_ref, s):
@@ -277,7 +274,7 @@
 
 
 def tails_to_lanes(z, ref, c):
-    ends = ref[c, :, z.main :]
+    ends = ref[c, : z.slots, z.main :]
     lane = lane_index(ends.shape)
     row = row_index(ends.shape)
     picked = jnp.zeros_like(ends)
@@ -286,22 +283,40 @@
     return jnp.sum(picked, axis=0, keepdims=True)
 
 
-def hat_tables(x, y, depth, first_x, count_x, first_y, count_y, plane_ref, rows_at, at):
+def hat(gap):
+    return jnp.maximum(0.0, 1.0 - gap)
+
+
+def hat_depth(depth):
+    steps = row_index((CZ, depth.shape[1])).astype(F32)
+    wrapped = depth - CZ * jnp.floor(depth * (1.0 / CZ))
+    gap = jnp.abs(wrapped - steps)
+    return hat(jnp.minimum(gap, CZ - gap))
+
+
+def whole_tables(z, line, plane_ref):
+    x, y, depth = line
     width = x.shape[1]
-    steps_x = row_index((count_x, width)).astype(F32)
-    steps_y = row_index((count_y, width)).astype(F32)
-    if first_x is not None:
-        steps_x = steps_x + first_x
-        steps_y = steps_y + first_y
-    steps_z = row_index((CZ, width)).astype(F32)
-    hat_x = jnp.maximum(0.0, 1.0 - jnp.abs(x - steps_x))
-    hat_y = jnp.maximum(0.0, 1.0 - jnp.abs(y - steps_y))
-    wrapped = depth - CZ * jnp.floor(depth * (1.0 / CZ))
-    gap = jnp.abs(wrapped - steps_z)
-    hat_z = jnp.maximum(0.0, 1.0 - jnp.minimum(gap, CZ - gap))
-    for j in range(count_y):
-        rows = slice(rows_at + j * CZ, rows_at + (j + 1) * CZ)
-        plane_ref[rows, at : at + width] = (hat_y[j : j + 1] * hat_z).astype(BF16)
+    hat_x = hat(jnp.abs(x - row_index((z.width_x, width)).astype(F32)))
+    hat_y = hat(jnp.abs(y - row_index((z.width_y, width)).astype(F32)))
+    hat_z = hat_depth(depth)
+    for j in range(z.width_y):
+        plane_ref[j * CZ : (j + 1) * CZ, :width] = (hat_y[j : j + 1] * hat_z).astype(BF16)
+    return hat_x
+
+
+def window_tables(line, first, plane_ref, rows_at, rows_ref):
+    x, y, depth = line
+    steps = row_index((WINDOW, x.shape[1])).astype(F32)
+    hat_x = hat(jnp.abs(x - (steps + first[0].astype(F32))))
+    rows_ref[...] = hat(jnp.abs(y - (steps + first[1].astype(F32))))
+    hat_z = hat_depth(depth)
+    for j in range(WINDOW):
+        hat_y = rows_ref[pl.ds(j, 8, stride=0), :]
+        block = jnp.concatenate(
+            [hat_y * hat_z[k * 8 : (k + 1) * 8] for k in range(CZ // 8)], axis=0
+        )
+        plane_ref[rows_at + j * CZ : rows_at + (j + 1) * CZ, :] = block.astype(BF16)
     return hat_x
 
 
@@ -309,144 +324,135 @@
     return lax.dot_general(lift, plane, (((1,), (1,)), ((), ())), preferred_element_type=F32)
 
 
-def spread(z, places_ref, force_ref, lists_ref, grid_ref, plane_ref, lift_ref):
-    grid_ref[...] = jnp.zeros_like(grid_ref)
-
-    def fill(line, pull, firsts, counts, at, plane_row, lift_row):
-        hat_x = hat_tables(*line, firsts[0], counts[0], firsts[1], counts[1], plane_ref, plane_row, at)
-        width = line[0].shape[1]
+PLANE_ROWS = WINDOW * CZ
+LIFT_ROWS = 3 * WINDOW
+
+
+def fast_pairs(lists_ref, build, use):
+    def entry(pair, h):
+        s = lists_ref[FAST_AT + 2 * pair + h]
+        return s, window_of(lists_ref, s)
+
+    def pair(p):
+        return [entry(p, h) for h in range(2)]
+
+    def step(q, carry):
+        build(pair(2 * q + 1), 1)
+        use(pair(2 * q), 0)
+        build(pair(2 * q + 2), 0)
+        use(pair(2 * q + 1), 1)
+        return carry
+
+    build(pair(0), 0)
+    lax.fori_loop(0, lists_ref[0], step, 0)
+
+
+def spread(z, places_ref, force_ref, lists_ref, grid_ref, buffers):
+    planes, lifts, hats, _ = buffers
+
+    def lift_up(pull, hat_x, lift_ref, row):
+        count, width = hat_x.shape
         for c in range(3):
-            row = lift_row + c * counts[0]
-            lift_ref[row : row + counts[0], at : at + width] = (pull[c] * hat_x).astype(BF16)
+            rows = slice(row + c * count, row + (c + 1) * count)
+            lift_ref[rows, :width] = (pull[c] * hat_x).astype(BF16)
 
     def load(s):
         line = [places_ref[c, pl.ds(s, 1), : z.main] for c in range(3)]
         pull = [force_ref[c, pl.ds(s, 1), : z.main] for c in range(3)]
         return line, pull
 
-    whole = (z.width_x, z.width_y)
-    window = (WINDOW, WINDOW)
-    plane_rows = WINDOW * CZ
-    lift_rows = 3 * WINDOW
-
-    def fast(p, carry):
-        firsts = []
-        for h in range(2):
-            s = lists_ref[FAST_AT + 2 * p + h]
-            first = window_of(lists_ref, s)
-            firsts.append(first)
+    def build(pair, b):
+        for h, (s, first) in enumerate(pair):
             line, pull = load(s)
-            fill(
-                line, pull, [f.astype(F32) for f in first], window, 0, h * plane_rows, h * lift_rows
+            hat_x = window_tables(line, first, planes[b], h * PLANE_ROWS, hats[2 * b + h])
+            lift_up(pull, hat_x, lifts[b], h * LIFT_ROWS)
+
+    def use(pair, b):
+        for h, (_, first) in enumerate(pair):
+            part = contract(
+                lifts[b][h * LIFT_ROWS : (h + 1) * LIFT_ROWS, :],
+                planes[b][h * PLANE_ROWS : (h + 1) * PLANE_ROWS, :],
             )
-        for h in range(2):
-            part = contract(
-                lift_ref[h * lift_rows : (h + 1) * lift_rows, : z.main],
-                plane_ref[h * plane_rows : (h + 1) * plane_rows, : z.main],
-            )
-            lanes = pl.ds(pl.multiple_of(firsts[h][1] * CZ, LANES), plane_rows)
+            lanes = pl.ds(pl.multiple_of(first[1] * CZ, LANES), PLANE_ROWS)
             for c in range(3):
-                rows = pl.ds(pl.multiple_of(c * z.width_x + firsts[h][0], 8), WINDOW)
+                rows = pl.ds(pl.multiple_of(c * z.width_x + first[0], 8), WINDOW)
                 grid_ref[rows, lanes] += part[c * WINDOW : (c + 1) * WINDOW]
-        return carry
 
     def slow(p, carry):
-        for h in range(2):
-            line, pull = load(lists_ref[SLOW_AT + 2 * p + h])
-            fill(line, pull, (None, None), whole, h * z.main, 0, 0)
-        grid_ref[...] += contract(lift_ref[...], plane_ref[...])
+        line, pull = load(lists_ref[SLOW_AT + p])
+        lift_up(pull, whole_tables(z, line, planes[0]), lifts[0], 0)
+        grid_ref[...] += contract(lifts[0][...], planes[0][...])
         return carry
 
     line = [tails_to_lanes(z, places_ref, c) for c in range(3)]
     pull = [tails_to_lanes(z, force_ref, c) for c in range(3)]
-    fill(line, pull, (None, None), whole, 0, 0, 0)
-    grid_ref[...] = contract(lift_ref[:, :LANES], plane_ref[:, :LANES])
-    lax.fori_loop(0, lists_ref[0], fast, 0)
+    lift_up(pull, whole_tables(z, line, planes[1]), lifts[1], 0)
+    grid_ref[...] = contract(lifts[1][:, :LANES], planes[1][:, :LANES])
+    fast_pairs(lists_ref, build, use)
     lax.fori_loop(0, lists_ref[1], slow, 0)
 
 
-def sample(z, places_ref, flow_ref, lists_ref, plane_ref):
-    plane_rows = WINDOW * CZ
+def sample(z, places_ref, flow_ref, lists_ref, buffers):
+    planes, _, hats, hats_x = buffers
 
     def load(s):
         return [places_ref[c, pl.ds(s, 1), : z.main] for c in range(3)]
 
-    def move(s, line, picked, hat_x, count_x):
+    def move(s, picked, hat_x):
+        count = hat_x.shape[0]
         for c in range(3):
-            drift = jnp.sum(picked[c * count_x : (c + 1) * count_x] * hat_x, axis=0, keepdims=True)
-            places_ref[c, pl.ds(s, 1), : z.main] = line[c] + drift
-
-    def fast(p, carry):
-        slots = [lists_ref[FAST_AT + 2 * p + h] for h in range(2)]
-        firsts = [window_of(lists_ref, s) for s in slots]
-        lines = [load(s) for s in slots]
-        hats = [
-            hat_tables(
-                *lines[h],
-                firsts[h][0].astype(F32),
-                WINDOW,
-                firsts[h][1].astype(F32),
-                WINDOW,
-                plane_ref,
-                h * plane_rows,
-                0,
+            drift = jnp.sum(picked[c * count : (c + 1) * count] * hat_x, axis=0, keepdims=True)
+            places_ref[c, pl.ds(s, 1), : z.main] = places_ref[c, pl.ds(s, 1), : z.main] + drift
+
+    def build(pair, b):
+        for h, (s, first) in enumerate(pair):
+            hats_x[2 * b + h][...] = window_tables(
+                load(s), first, planes[b], h * PLANE_ROWS, hats[2 * b + h]
             )
-            for h in range(2)
-        ]
+
+    def use(pair, b):
         picked = []
-        for h in range(2):
-            lanes = pl.ds(pl.multiple_of(firsts[h][1] * CZ, LANES), plane_rows)
-            flow = jnp.concatenate(
-                [
-                    flow_ref[
-                        pl.ds(pl.multiple_of(c * z.width_x + firsts[h][0], 8), WINDOW), lanes
-                    ]
-                    for c in range(3)
-                ],
-                axis=0,
-            ).astype(BF16)
-            plane = plane_ref[h * plane_rows : (h + 1) * plane_rows, : z.main]
-            picked.append(jnp.dot(flow, plane, preferred_element_type=F32))
-        for h in range(2):
-            move(slots[h], lines[h], picked[h], hats[h], WINDOW)
+        for h, (_, first) in enumerate(pair):
+            lanes = pl.ds(pl.multiple_of(first[1] * CZ, LANES), PLANE_ROWS)
+            flow = [
+                flow_ref[pl.ds(pl.multiple_of(c * z.width_x + first[0], 8), WINDOW), lanes]
+                for c in range(3)
+            ]
+            picked.append(
+                jnp.dot(
+                    jnp.concatenate(flow, axis=0).astype(BF16),
+                    planes[b][h * PLANE_ROWS : (h + 1) * PLANE_ROWS, :],
+                    preferred_element_type=F32,
+                )
+            )
+        for h, (s, _) in enumerate(pair):
+            move(s, picked[h], hats_x[2 * b + h][...])
+
+    def slow(p, carry):
+        s = lists_ref[SLOW_AT + p]
+        hat_x = whole_tables(z, load(s), planes[0])
+        picked = jnp.dot(flow_ref[...].astype(BF16), planes[0][...], preferred_element_type=F32)
+        move(s, picked, hat_x)
         return carry
 
-    def slow(p, carry):
-        slots = [lists_ref[SLOW_AT + 2 * p + h] for h in range(2)]
-        lines = [load(s) for s in slots]
-        hats = [
-            hat_tables(
-                *lines[h], None, z.width_x, None, z.width_y, plane_ref, 0, h * z.main
-            )
-            for h in range(2)
-        ]
-        picked = jnp.dot(
-            flow_ref[...].astype(BF16), plane_ref[...], preferred_element_type=F32
-        )
-        for h in range(2):
-            move(
-                slots[h], lines[h], picked[:, h * z.main : (h + 1) * z.main], hats[h], z.width_x
-            )
-        return carry
-
     line = [tails_to_lanes(z, places_ref, c) for c in range(3)]
-    hat_x = hat_tables(*line, None, z.width_x, None, z.width_y, plane_ref, 0, 0)
+    hat_x = whole_tables(z, line, planes[1])
     picked = jnp.dot(
-        flow_ref[...].astype(BF16), plane_ref[:, :LANES], preferred_element_type=F32
+        flow_ref[...].astype(BF16), planes[1][:, :LANES], preferred_element_type=F32
     )
-    rows = places_ref.shape[1]
+    rows = z.slots
     lane = lane_index((rows, LANES))
     row = row_index((rows, LANES))
     for c in range(3):
         drift = jnp.sum(picked[c * z.width_x : (c + 1) * z.width_x] * hat_x, axis=0, keepdims=True)
-        ends = places_ref[c, :, z.main :]
+        ends = places_ref[c, :rows, z.main :]
         for t in range(z.tail):
             moved = jnp.sum(
                 jnp.where(lane == row * z.tail + t, drift, 0.0), axis=1, keepdims=True
             )
             ends = jnp.where(lane == t, ends + moved, ends)
-        places_ref[c, :, z.main :] = ends
-    lax.fori_loop(0, lists_ref[0], fast, 0)
+        places_ref[c, :rows, z.main :] = ends
+    fast_pairs(lists_ref, build, use)
     lax.fori_loop(0, lists_ref[1], slow, 0)
 
 
@@ -597,35 +603,64 @@
                 flow_ref[c * z.width_x + r * 8 : c * z.width_x + (r + 1) * 8, lanes] = sums[c]
 
 
+def buffer_types(z):
+    plane = VMEM((z.plane, z.main), BF16)
+    lift = VMEM((3 * z.width_x, z.main), BF16)
+    rows = VMEM((WINDOW, z.main), F32)
+    return [plane] * 2 + [lift] * 2 + [rows] * 8
+
+
+def split_buffers(refs):
+    return refs[:2], refs[2:4], refs[4:8], refs[8:12]
+
+
 def first_kernel(z, *refs):
     d = z.devices_y
     messages = refs[:d]
     shape_ref, link_ref, degree_ref, flow_ref = refs[d : d + 4]
     grid_ref, post_ref, right_ref, left_ref, up_ref, down_ref = refs[d + 4 : d + 10]
-    places_ref, stiff_ref, lists_ref = refs[d + 10 : d + 13]
-    ends, force, plane, lift = refs[d + 13 :]
+    places_ref, stiff_ref = refs[d + 10 : d + 12]
+    ends, force, lists = refs[d + 12 : d + 15]
+    buffers = split_buffers(refs[d + 15 :])
     for e in range(d):
         for h in range(3):
             split_message(z, messages[e][h], places_ref, ends, (3 * e + h) * CAP)
     place_tails(z, ends, places_ref, stiff_ref)
-    list_slots(z, places_ref, stiff_ref, lists_ref)
+    list_slots(z, places_ref, stiff_ref, lists)
     forces(z, places_ref, stiff_ref, shape_ref, link_ref, degree_ref, force)
-    spread(z, places_ref, force, lists_ref, grid_ref, plane, lift)
+    spread(z, places_ref, force, lists, grid_ref, buffers)
     collide(z, flow_ref, grid_ref, post_ref)
     write_edges(z, post_ref, right_ref, left_ref, up_ref, down_ref)
 
 
+def sort_edges(near_ref, far_ref, below_ref, above_ref):
+    even = lax.rem(lax.axis_index("gy"), 2) == 0
+
+    @pl.when(even)
+    def _():
+        above_ref[...] = near_ref[...]
+        below_ref[...] = far_ref[...]
+
+    @pl.when(jnp.logical_not(even))
+    def _():
+        below_ref[...] = near_ref[...]
+        above_ref[...] = far_ref[...]
+
+
 def middle_kernel(z, *refs):
-    post_ref, from_left, from_right, below, above = refs[:5]
-    old_grid, old_places, stiff_ref, old_lists, shape_ref, link_ref, degree_ref = refs[5:12]
-    grid_ref, next_ref, right_ref, left_ref, up_ref, down_ref, places_ref, lists_ref = refs[12:20]
-    moved, flow, force, plane, lift = refs[20:]
+    post_ref, from_left, from_right, near, far = refs[:5]
+    old_grid, old_places, stiff_ref, shape_ref, link_ref, degree_ref = refs[5:11]
+    grid_ref, next_ref, right_ref, left_ref, up_ref, down_ref, places_ref = refs[11:18]
+    moved, flow, below, above, force, lists = refs[18:24]
+    buffers = split_buffers(refs[24:])
+    sort_edges(near, far, below, above)
     places_ref[...] = old_places[...]
+    list_slots(z, places_ref, stiff_ref, lists)
     stream(z, post_ref, from_left, from_right, below, above, moved, old_grid, flow)
-    sample(z, places_ref, flow, old_lists, plane)
-    list_slots(z, places_ref, stiff_ref, lists_ref)
+    sample(z, places_ref, flow, lists, buffers)
+    list_slots(z, places_ref, stiff_ref, lists)
     forces(z, places_ref, stiff_ref, shape_ref, link_ref, degree_ref, force)
-    spread(z, places_ref, force, lists_ref, grid_ref, plane, lift)
+    spread(z, places_ref, force, lists, grid_ref, buffers)
     collide(z, moved, grid_ref, next_ref)
     write_edges(z, next_ref, right_ref, left_ref, up_ref, down_ref)
 
@@ -643,13 +678,17 @@
 
 def last_kernel(z, *refs):
     d = z.devices_y
-    post_ref, from_left, from_right, below, above, grid_ref, old_places, lists_ref = refs[:8]
-    moved_ref = refs[8]
-    message_refs = refs[9 : 9 + d]
-    flow, places, plane = refs[9 + d :]
+    post_ref, from_left, from_right, near, far, grid_ref, old_places, stiff_ref = refs[:8]
+    moved_ref, density_ref = refs[8:10]
+    message_refs = refs[10 : 10 + d]
+    flow, below, above, places, lists = refs[10 + d : 15 + d]
+    buffers = split_buffers(refs[15 + d :])
+    sort_edges(near, far, below, above)
+    density_ref[...] = grid_ref[...]
     places[...] = old_places[...]
+    list_slots(z, places, stiff_ref, lists)
     stream(z, post_ref, from_left, from_right, below, above, moved_ref, grid_ref, flow)
-    sample(z, places, flow, lists_ref, plane)
+    sample(z, places, flow, lists, buffers)
     for e in range(d):
         for h in range(3):
             join_message(z, places, (3 * e + h) * CAP, message_refs[e], h)
@@ -658,6 +697,18 @@
 def shift(value, axis, step):
     count = lax.axis_size(axis)
     return lax.ppermute(value, axis, [(i, (i + step) % count) for i in range(count)])
+
+
+def swap(value, axis, key):
+    count = lax.axis_size(axis)
+    return lax.ppermute(value, axis, [(i, i ^ key) for i in range(count)])
+
+
+def swap_across(value, axis):
+    count = lax.axis_size(axis)
+    return lax.ppermute(
+        value, axis, [(i, (i + 1) % count if i % 2 else (i - 1) % count) for i in range(count)]
+    )
 
 
 def trade_edges(z, right, left, up, down):
@@ -666,7 +717,10 @@
     far, near = slice(z.plane - LANES, z.plane), slice(0, LANES)
     up = jnp.concatenate([up, from_left[:, far], from_right[:, far]], axis=0)
     down = jnp.concatenate([down, from_left[:, near], from_right[:, near]], axis=0)
-    return from_left, from_right, shift(up, "gy", 1), shift(down, "gy", -1)
+    even = lax.rem(lax.axis_index("gy"), 2) == 0
+    across = swap_across(jnp.where(even, down, up), "gy")
+    beside = swap(jnp.where(even, up, down), "gy", 1)
+    return from_left, from_right, beside, across
 
 
 def local(populations, positions, stiffness, membrane_shape, neighbours, home_tile):
@@ -679,6 +733,7 @@
         lax.axis_size("gy"),
     )
     d = z.devices_y
+    turns = range(d - 1, 0, -1)
     run = functools.partial
     line = (CAP, z.message)
     table = VMEM((z.groups,) + line, F32)
@@ -687,13 +742,22 @@
     to_left, center, to_right = call(
         run(pack_kernel, z),
         [((d,) + line, F32, VMEM)] * 3,
-        [SMEM, SMEM, VMEM],
-        [table, counts],
+        [HBM] * 3,
+        [
+            SMEM(home_tile.shape, jnp.int32),
+            SMEM(stiffness.shape, F32),
+            VMEM(places_in.shape, F32),
+            table,
+            counts,
+            pltpu.SemaphoreType.DMA((3,)),
+        ],
     )(home_tile, stiffness, places_in)
     from_left = shift(to_right, "gx", 1)
     from_right = shift(to_left, "gx", -1)
-    messages = [jnp.stack([center[e], from_left[e], from_right[e]]) for e in range(d)]
-    messages = [messages[0]] + [shift(messages[e], "gy", e) for e in range(1, d)]
+    own = [jnp.stack([center[e], from_left[e], from_right[e]]) for e in range(d)]
+    messages = {e: swap(own[e], "gy", e) for e in turns}
+    messages = [own[0]] + [messages[e] for e in range(1, d)]
+    near = neighbours.T
     link, degree, shape = call(
         run(matrix_kernel, z),
         [
@@ -701,44 +765,48 @@
             ((1, z.full), F32, VMEM),
             ((3, z.full), F32, VMEM),
         ],
-        [VMEM, VMEM],
-        [VMEM((z.full, z.full), F32)],
+        [HBM, HBM, pl.ANY],
+        [
+            VMEM(near.shape, jnp.int32),
+            VMEM(membrane_shape.shape, F32),
+            VMEM((z.full, z.full), F32),
+            pltpu.SemaphoreType.DMA((2,)),
+        ],
         pl.CostEstimate(flops=2_000_000_000, bytes_accessed=4_000_000, transcendentals=0),
-    )(neighbours.T, membrane_shape)
+    )(near, membrane_shape, own[0])
 
     grid_type = ((3 * z.width_x, z.plane), F32, VMEM)
     post_type = ((19, z.width_x, z.plane), F32, VMEM)
-    plane_scratch = VMEM((z.plane, 2 * z.main), BF16)
-    lift_scratch = VMEM((3 * z.width_x, 2 * z.main), BF16)
     edge_types = [((8, z.plane), F32, VMEM)] * 2 + [((z.width_x, LANES), F32, VMEM)] * 2
-    places_type = ((3, z.slots, z.full), F32, VMEM)
-    lists_type = ((LISTS,), jnp.int32, SMEM)
+    places_type = ((3, z.rows, z.full), F32, VMEM)
+    lists = SMEM((LISTS,), jnp.int32)
     rows = VMEM(places_type[0], F32)
-
-    grid, post, right, left, up, down, places, stiff, lists = call(
+    flow = VMEM(grid_type[0], F32)
+    edge = VMEM((z.width_x + 16, LANES), F32)
+
+    grid, post, right, left, up, down, places, stiff = call(
         run(first_kernel, z),
-        [grid_type, post_type]
-        + edge_types
-        + [places_type, ((z.slots, LANES), F32, VMEM), lists_type],
+        [grid_type, post_type] + edge_types + [places_type, ((z.slots, LANES), F32, VMEM)],
         [VMEM] * (d + 4),
-        [VMEM((z.slots, LANES), F32), rows, plane_scratch, lift_scratch],
+        [VMEM((z.slots, LANES), F32), rows, lists] + buffer_types(z),
     )(*messages, shape, link, degree, populations)
     for _ in range(STEPS - 1):
         edges = trade_edges(z, right, left, up, down)
-        grid, post, right, left, up, down, places, lists = call(
+        grid, post, right, left, up, down, places = call(
             run(middle_kernel, z),
-            [grid_type, post_type] + edge_types + [places_type, lists_type],
-            [VMEM] * 8 + [SMEM] + [VMEM] * 3,
-            [VMEM(post_type[0], F32), VMEM(grid_type[0], F32), rows, plane_scratch, lift_scratch],
-        )(post, *edges, grid, places, stiff, lists, shape, link, degree)
+            [grid_type, post_type] + edge_types + [places_type],
+            [VMEM] * 11,
+            [VMEM(post_type[0], F32), flow, edge, edge, rows, lists] + buffer_types(z),
+        )(post, *edges, grid, places, stiff, shape, link, degree)
     edges = trade_edges(z, right, left, up, down)
-    moved, *messages = call(
+    moved, density, *messages = call(
         run(last_kernel, z),
-        [post_type] + [((3,) + line, F32, VMEM)] * d,
-        [VMEM] * 7 + [SMEM],
-        [VMEM(grid_type[0], F32), rows, plane_scratch],
-    )(post, *edges, grid, places, lists)
-    messages = [messages[0]] + [shift(messages[e], "gy", -e) for e in range(1, d)]
+        [post_type, grid_type] + [((3,) + line, F32, VMEM)] * d,
+        [VMEM] * 8,
+        [flow, edge, edge, rows, lists] + buffer_types(z),
+    )(post, *edges, grid, places, stiff)
+    back = {e: swap(messages[e], "gy", e) for e in turns}
+    messages = [messages[0]] + [back[e] for e in range(1, d)]
     right_part = shift(jnp.stack([m[1] for m in messages]), "gx", -1)
     left_part = shift(jnp.stack([m[2] for m in messages]), "gx", 1)
     (displacement,) = call(
@@ -747,7 +815,7 @@
         [SMEM] + [VMEM] * (3 + d),
         [table, counts],
     )(home_tile, places_in, left_part, right_part, *messages)
-    return moved, displacement.transpose(1, 0, 2), grid.reshape(3, z.width_x, z.plane)
+    return moved, displacement.transpose(1, 0, 2), density.reshape(3, z.width_x, z.plane)
 
 
 def solution(mesh):

time: 87.8 us -> 83.5 us (0.951); the launches traced: 88.5 us -> 83.3 us
  starting transfers between devices: 28.9 us -> 25.6 us
  waiting for transfers between devices: 22.3 us -> 25.2 us
  Pallas kernels: 31.7 us -> 29.1 us
  local copies, waits for them, and re-layouts: 4.68 us -> 2.32 us
    ppermute x0 -> x10, waiting for transfers between devices: none -> 13.3 us  [the longest x8 7.95 us: swap(): return lax.ppermute(value, axis, [(i, i ^ key) for i in range(count)])]
    ppermute x18 -> x8, waiting for transfers between devices: 22.3 us -> 11.9 us  [shift(): lax.ppermute(value, axis, [(i, (i + step) % count) for i in range(count)])]
    ppermute x18 -> x8, starting transfers between devices: 28.9 us -> 20.5 us  [shift(): lax.ppermute(value, axis, [(i, (i + step) % count) for i in range(count)])]
    ppermute x0 -> x10, starting transfers between devices: none -> 5.17 us  [the longest x8 5.03 us: swap(): return lax.ppermute(value, axis, [(i, i ^ key) for i in range(count)])]
    unnamed x18 -> x16, local copies, waits for them, and re-layouts: 4.62 us -> 2.26 us
    pallas_call x1, Pallas kernels: 13.2 us -> 11.8 us  [local(): call(run(middle_kernel, z), [grid_type, post_type] + edge_types + [places...]
    pallas_call x1, Pallas kernels: 7.45 us -> 6.53 us  [local(): call(run(first_kernel, z), [grid_type, post_type] + edge_types + [places_...]
  transfers between devices with their start and end apart: 18 -> 18, of which waited for: 14 -> 12; matrix products, arithmetic and copies ran while one was open for 0% -> 0% of each run, Pallas kernels for 2% -> 2%
where the time goes in v2:
time: 83.5 us; the launch traced here: 83.3 us
  Pallas kernels  29.1 us (35%)
  starting transfers between devices  25.6 us (31%)
  waiting for transfers between devices  25.2 us (30%)
  local copies, waits for them, and re-layouts  2.32 us (3%)
  between operations  0.85 us (1%)
    ppermute x8, starting transfers between devices, shift(): lax.ppermute(value, axis, [(i, (i + step) % count) for i in range(count)])  20.5 us
    ppermute x8, waiting for transfers between devices, shift(): lax.ppermute(value, axis, [(i, (i + step) % count) for i in range(count)])  11.9 us
    pallas_call x1, Pallas kernels, local(): call(run(middle_kernel, z), [grid_type, post_type] + edge_types + [places...  11.8 us
    ppermute x8, waiting for transfers between devices, swap(): return lax.ppermute(value, axis, [(i, i ^ key) for i in range(count)])  7.95 us
    pallas_call x1, Pallas kernels, local(): call(run(first_kernel, z), [grid_type, post_type] + edge_types + [places_...  6.53 us
    pallas_call x1, Pallas kernels, local(): call(run(last_kernel, z), [post_type, grid_type] + [((3,) + line, F32, VM...  6.48 us
    ppermute x2, waiting for transfers between devices, swap_across(): lax.ppermute(value, axis, [(i, (i + 1) % count if i % 2 else (i - 1) % co...  5.34 us
    ppermute x8, starting transfers between devices, swap(): return lax.ppermute(value, axis, [(i, i ^ key) for i in range(count)])  5.03 us
  transfers between devices with their start and end apart: 18, of which 12 were waited for; matrix products, arithmetic and copies ran while one was open for 0% of the time, Pallas kernels for 2%

profile of v2, /device:TPU:0, one launch (start us, length us, event | category | flops | bytes accessed | tf_op | source)
XLA Modules:
  0.0 83.3 jit_solution(13921922370011523707)
XLA Ops:
  0.6 0.0 copy-start.1
  0.6 0.9 %copy-done.1 = f32[24,3,642]{2,0,1:T(8,128)S(1)} copy-done((f32[24,3,642]{2,0,1:T(8,128)S(1)}, f32[24,3,642]{2,0,1:T(8,128)}, u32[]{:S(2)}) %copy-start.1) | copy-done | bytes 184920
  1.6 0.0 copy-start.3
  1.6 0.7 copy-done.3
  2.2 0.0 copy-start.5
  2.2 0.7 copy-done.5
  2.9 0.0 copy-start.6
  2.9 0.0 copy-start.7
  2.9 0.9 %shard_map.85 = (f32[4,4,2048]{2,1,0:T(4,128)S(1)}, f32[4,4,2048]{2,1,0:T(4,128)S(1)}, f32[4,4,2048]{2,1,0:T(4,128)S(1)}) custom-call(s32[24]{0:T(128)S(1)} %copy-done.3, f32[24]{0:T(128)S(1)} %copy-done.5, f32[3,24,642]{2,1,0:T(8,128)S(1)} %bitcast.4), custom_call_target="tpu_custom_call" | custom-call | tf_op jit(solution)/shard_map/pallas_call | solution.py:742
  3.8 3.0 %collective-permute-start = (f32[4,4,2048]{2,1,0:T(4,128)S(1)}, f32[4,4,2048]{2,1,0:T(4,128)S(1)}, u32[]{:S(2)}, u32[]{:S(2)}) collective-permute-start(f32[4,4,2048]{2,1,0:T(4,128)S(1)} %get-tuple-element.31), channel_id=1, source_target_pairs={{0,4},{4,8},{8,12},{12,16},{16,20},{20,24},{24,28},{28,0},{1,5},{5... | collective-permute-start | bytes 393224 | tf_op jit(solution)/shard_map/ppermute | solution.py:699
  6.8 3.1 %collective-permute-start.1 = (f32[4,4,2048]{2,1,0:T(4,128)S(1)}, f32[4,4,2048]{2,1,0:T(4,128)S(1)}, u32[]{:S(2)}, u32[]{:S(2)}) collective-permute-start(f32[4,4,2048]{2,1,0:T(4,128)S(1)} %get-tuple-element.32), channel_id=1, source_target_pairs={{0,28},{4,0},{8,4},{12,8},{16,12},{20,16},{24,20},{28,24},{1,29},{... | collective-permute-start | bytes 393224 | tf_op jit(solution)/shard_map/ppermute | solution.py:699
  10.0 3.5 %collective-permute-done = f32[4,4,2048]{2,1,0:T(4,128)S(1)} collective-permute-done((f32[4,4,2048]{2,1,0:T(4,128)S(1)}, f32[4,4,2048]{2,1,0:T(4,128)S(1)}, u32[]{:S(2)}, u32[]{:S(2)}) %collective-permute-start) | collective-permute-done | bytes 131104 | tf_op jit(solution)/shard_map/ppermute | solution.py:699
  13.5 1.1 %collective-permute-done.1 = f32[4,4,2048]{2,1,0:T(4,128)S(1)} collective-permute-done((f32[4,4,2048]{2,1,0:T(4,128)S(1)}, f32[4,4,2048]{2,1,0:T(4,128)S(1)}, u32[]{:S(2)}, u32[]{:S(2)}) %collective-permute-start.1) | collective-permute-done | bytes 131104 | tf_op jit(solution)/shard_map/ppermute | solution.py:699
  14.7 0.1 collective-permute-start.2
  14.8 1.6 %collective-permute-start.3 = (f32[3,4,2048]{2,1,0:T(4,128)S(1)}, f32[3,4,2048]{2,1,0:T(4,128)S(1)}, u32[]{:S(2)}, u32[]{:S(2)}) collective-permute-start(f32[3,4,2048]{2,1,0:T(4,128)S(1)} %pad_maximum_fusion.4), channel_id=1, source_target_pairs={{0,2},{1,3},{2,0},{3,1},{4,6},{5,7},{6,4},{7,5},{8,10},{9,11},{10,... | collective-permute-start | bytes 294920 | tf_op jit(solution)/shard_map/ppermute | solution.py:704
  16.4 0.4 collective-permute-start.4
  16.8 0.0 copy-done.6
  16.8 0.0 copy-done.7
  16.8 0.0 copy-start
  16.8 1.8 %shard_map.86 = (bf16[768,768]{1,0:T(8,128)(2,1)S(1)}, f32[1,768]{1,0:T(1,128)S(1)}, f32[3,768]{1,0:T(4,128)S(1)}) custom-call(s32[6,642]{1,0:T(8,128)S(1)} %bitcast.6, f32[3,642]{1,0:T(4,128)S(1)} %copy-done.7, f32[3,4,2048]{2,1,0:T(4,128)S(1)} %pad_maximum_fusion.2.after_in.refs_0_), custom_call_target="tpu_custom_call" | custom-call | flops 2000000000 | bytes 4000000 | tf_op jit(solution)/shard_map/pallas_call | solution.py:761
  18.6 0.0 collective-permute-done.2.refs_1_
  18.6 1.9 %collective-permute-done.3.refs_2_ = f32[3,4,2048]{2,1,0:T(4,128)S(1)} collective-permute-done((f32[3,4,2048]{2,1,0:T(4,128)S(1)}, f32[3,4,2048]{2,1,0:T(4,128)S(1)}, u32[]{:S(2)}, u32[]{:S(2)}) %collective-permute-start.3) | collective-permute-done | bytes 98336 | tf_op jit(solution)/shard_map/ppermute | solution.py:704
  20.5 1.1 %collective-permute-done.4.refs_3_ = f32[3,4,2048]{2,1,0:T(4,128)S(1)} collective-permute-done((f32[3,4,2048]{2,1,0:T(4,128)S(1)}, f32[3,4,2048]{2,1,0:T(4,128)S(1)}, u32[]{:S(2)}, u32[]{:S(2)}) %collective-permute-start.4) | collective-permute-done | bytes 98336 | tf_op jit(solution)/shard_map/ppermute | solution.py:704
  21.7 0.0 copy-done
  21.7 6.5 %shard_map.87 = (f32[96,512]{1,0:T(8,128)S(1)}, f32[19,32,512]{2,1,0:T(8,128)S(1)}, f32[8,512]{1,0:T(8,128)S(1)}, f32[8,512]{1,0:T(8,128)S(1)}, f32[32,128]{1,0:...) custom-call(f32[3,4,2048]{2,1,0:T(4,128)S(1)} %pad_maximum_fusion.2.after_in.refs_0_, ...), custom_call_target="tpu_custom_call" | custom-call | tf_op jit(solution)/shard_map/pallas_call | solution.py:787
  28.2 0.1 collective-permute-start.5
  28.3 4.7 %collective-permute-start.6 = (f32[8,512]{1,0:T(8,128)S(1)}, f32[8,512]{1,0:T(8,128)S(1)}, u32[]{:S(2)}, u32[]{:S(2)}) collective-permute-start(f32[8,512]{1,0:T(8,128)S(1)} %get-tuple-element.38), channel_id=1, source_target_pairs={{0,28},{4,0},{8,4},{12,8},{16,12},{20,16},{24,20},{28,24},{1,29},{... | collective-permute-start | bytes 49160 | tf_op jit(solution)/shard_map/ppermute | solution.py:699
  33.0 1.7 %collective-permute-done.5.refs_1_ = f32[8,512]{1,0:T(8,128)S(1)} collective-permute-done((f32[8,512]{1,0:T(8,128)S(1)}, f32[8,512]{1,0:T(8,128)S(1)}, u32[]{:S(2)}, u32[]{:S(2)}) %collective-permute-start.5) | collective-permute-done | bytes 16416 | tf_op jit(solution)/shard_map/ppermute | solution.py:699
  34.7 0.0 collective-permute-done.6.refs_2_
  34.7 0.1 collective-permute-start.8
  34.8 1.1 %collective-permute-start.7 = (f32[48,128]{1,0:T(8,128)S(1)}, f32[48,128]{1,0:T(8,128)S(1)}, u32[]{:S(2)}, u32[]{:S(2)}) collective-permute-start(f32[48,128]{1,0:T(8,128)S(1)} %get-tuple-element.80), channel_id=1, source_target_pairs={{0,1},{1,0},{2,3},{3,2},{4,5},{5,4},{6,7},{7,6},{8,9},{9,8},{10,11... | collective-permute-start | bytes 73736 | tf_op jit(solution)/shard_map/ppermute | solution.py:704
  35.9 2.2 %collective-permute-done.8.refs_4_ = f32[48,128]{1,0:T(8,128)S(1)} collective-permute-done((f32[48,128]{1,0:T(8,128)S(1)}, f32[48,128]{1,0:T(8,128)S(1)}, u32[]{:S(2)}, u32[]{:S(2)}) %collective-permute-start.8) | collective-permute-done | bytes 24608 | tf_op jit(solution)/shard_map/ppermute | solution.py:709
  38.0 0.0 collective-permute-done.7.refs_3_
  38.0 11.8 %shard_map.88 = (f32[96,512]{1,0:T(8,128)S(1)}, f32[19,32,512]{2,1,0:T(8,128)S(1)}, f32[8,512]{1,0:T(8,128)S(1)}, f32[8,512]{1,0:T(8,128)S(1)}, f32[32,128]{1,0:...) custom-call(f32[19,32,512]{2,1,0:T(8,128)S(1)} %get-tuple-element.36.refs_0_, ...), custom_call_target="tpu_custom_call" | custom-call | tf_op jit(solution)/shard_map/pallas_call | solution.py:795
  49.8 0.1 collective-permute-start.9
  49.9 4.7 %collective-permute-start.10 = (f32[8,512]{1,0:T(8,128)S(1)}, f32[8,512]{1,0:T(8,128)S(1)}, u32[]{:S(2)}, u32[]{:S(2)}) collective-permute-start(f32[8,512]{1,0:T(8,128)S(1)} %get-tuple-element.46), channel_id=1, source_target_pairs={{0,28},{4,0},{8,4},{12,8},{16,12},{20,16},{24,20},{28,24},{1,29},{... | collective-permute-start | bytes 49160 | tf_op jit(solution)/shard_map/ppermute | solution.py:699
  54.6 1.7 %collective-permute-done.9.refs_1_ = f32[8,512]{1,0:T(8,128)S(1)} collective-permute-done((f32[8,512]{1,0:T(8,128)S(1)}, f32[8,512]{1,0:T(8,128)S(1)}, u32[]{:S(2)}, u32[]{:S(2)}) %collective-permute-start.9) | collective-permute-done | bytes 16416 | tf_op jit(solution)/shard_map/ppermute | solution.py:699
  56.3 0.0 collective-permute-done.10.refs_2_
  56.3 0.1 collective-permute-start.12
  56.4 0.1 collective-permute-start.11
  56.5 3.2 %collective-permute-done.12.refs_4_ = f32[48,128]{1,0:T(8,128)S(1)} collective-permute-done((f32[48,128]{1,0:T(8,128)S(1)}, f32[48,128]{1,0:T(8,128)S(1)}, u32[]{:S(2)}, u32[]{:S(2)}) %collective-permute-start.12) | collective-permute-done | bytes 24608 | tf_op jit(solution)/shard_map/ppermute | solution.py:709
  59.6 0.0 collective-permute-done.11.refs_3_
  59.7 0.0 copy-start.2
  59.7 0.0 copy-start.4
  59.7 6.5 %shard_map.89 = (f32[19,32,512]{2,1,0:T(8,128)}, f32[96,512]{1,0:T(8,128)}, f32[3,4,2048]{2,1,0:T(4,128)S(1)}, f32[3,4,2048]{2,1,0:T(4,128)S(1)}, f32[3,4,2048]{2,1,0:T(4,128)S(1)}, /*index=5*/f32[3,4,2048]{2,1,0:T(4,128)S(1)}) custom-call(f32[19,32,512]{2,1,0:T(8,128)S(1)} %get-tuple-element.44.refs_0_, f32[8,512]{1,0:T(8,128)S(1)} %collective-permute-done.9.refs_1_, ...), custom_call_target="tpu_custom_call" | custom-call | tf_op jit(solution)/shard_map/pallas_call | solution.py:802
  66.1 0.0 collective-permute-start.13
  66.1 0.1 collective-permute-start.14
  66.2 1.8 %collective-permute-start.15 = (f32[3,4,2048]{2,1,0:T(4,128)S(1)}, f32[3,4,2048]{2,1,0:T(4,128)S(1)}, u32[]{:S(2)}, u32[]{:S(2)}) collective-permute-start(f32[3,4,2048]{2,1,0:T(4,128)S(1)} %get-tuple-element.55), channel_id=1, source_target_pairs={{0,3},{1,2},{2,1},{3,0},{4,7},{5,6},{6,5},{7,4},{8,11},{9,10},{10,... | collective-permute-start | bytes 294920 | tf_op jit(solution)/shard_map/ppermute | solution.py:704
  68.0 0.0 collective-permute-done.13.rest_1_
  68.0 3.9 %collective-permute-done.14.rest_2_ = f32[3,4,2048]{2,1,0:T(4,128)S(1)} collective-permute-done((f32[3,4,2048]{2,1,0:T(4,128)S(1)}, f32[3,4,2048]{2,1,0:T(4,128)S(1)}, u32[]{:S(2)}, u32[]{:S(2)}) %collective-permute-start.14) | collective-permute-done | bytes 98336 | tf_op jit(solution)/shard_map/ppermute | solution.py:704
  71.9 1.0 %collective-permute-done.15.rest_3_ = f32[3,4,2048]{2,1,0:T(4,128)S(1)} collective-permute-done((f32[3,4,2048]{2,1,0:T(4,128)S(1)}, f32[3,4,2048]{2,1,0:T(4,128)S(1)}, u32[]{:S(2)}, u32[]{:S(2)}) %collective-permute-start.15) | collective-permute-done | bytes 98336 | tf_op jit(solution)/shard_map/ppermute | solution.py:704
  73.0 0.1 collective-permute-start.16
  73.1 4.8 %collective-permute-start.17 = (f32[4,4,2048]{2,1,0:T(4,128)S(1)}, f32[4,4,2048]{2,1,0:T(4,128)S(1)}, u32[]{:S(2)}, u32[]{:S(2)}) collective-permute-start(f32[4,4,2048]{2,1,0:T(4,128)S(1)} %pad_maximum_fusion.1), channel_id=1, source_target_pairs={{0,28},{4,0},{8,4},{12,8},{16,12},{20,16},{24,20},{28,24},{1,29},{... | collective-permute-start | bytes 393224 | tf_op jit(solution)/shard_map/ppermute | solution.py:699
  77.8 3.7 %collective-permute-done.16.left_ref = f32[4,4,2048]{2,1,0:T(4,128)S(1)} collective-permute-done((f32[4,4,2048]{2,1,0:T(4,128)S(1)}, f32[4,4,2048]{2,1,0:T(4,128)S(1)}, u32[]{:S(2)}, u32[]{:S(2)}) %collective-permute-start.16) | collective-permute-done | bytes 131104 | tf_op jit(solution)/shard_map/ppermute | solution.py:699
  81.6 0.1 collective-permute-done.17.right_ref
  81.7 0.0 copy-done.2
  81.7 0.0 copy-done.4
  81.7 1.6 %shard_map.90 = f32[3,24,642]{2,1,0:T(8,128)} custom-call(s32[24]{0:T(128)S(1)} %copy-done.4, f32[3,24,642]{2,1,0:T(8,128)S(1)} %bitcast.5, f32[4,4,2048]{2,1,0:T(4,128)S(1)} %collective-permute-done.16.left_ref, f32[4,4,2048]{2,1,0:T(4,128)S(1)} %collective-permute-done.17.right_ref, f32[3,4,2048]{2,1,0:T(4,128)S(1)} %get-tuple-element.52.rest_0_, ...), custom_call_target="tpu_custom_call" | custom-call | tf_op jit(solution)/shard_map/pallas_call | solution.py:812
  (19 shorter events, 0.2 us)
Async XLA Ops:
  0.6 0.9 %copy-start.1 = (f32[24,3,642]{2,0,1:T(8,128)S(1)}, f32[24,3,642]{2,0,1:T(8,128)}, u32[]{:S(2)}) copy-start(f32[24,3,642]{2,0,1:T(8,128)} %param.7) | copy-start | bytes 554692
  1.6 0.7 copy-start.3
  2.2 0.7 copy-start.5
  2.9 13.9 %copy-start.6 = (s32[642,6]{0,1:T(8,128)S(1)}, s32[642,6]{0,1:T(8,128)}, u32[]{:S(2)}) copy-start(s32[642,6]{0,1:T(8,128)} %param.10) | copy-start | bytes 46228
  2.9 13.9 %copy-start.7 = (f32[3,642]{1,0:T(4,128)S(1)}, f32[3,642]{1,0:T(4,128)}, u32[]{:S(2)}) copy-start(f32[3,642]{1,0:T(4,128)} %shape_in.1) | copy-start | bytes 23116
  3.8 9.7 %collective-permute-start = (f32[4,4,2048]{2,1,0:T(4,128)S(1)}, f32[4,4,2048]{2,1,0:T(4,128)S(1)}, u32[]{:S(2)}, u32[]{:S(2)}) collective-permute-start(f32[4,4,2048]{2,1,0:T(4,128)S(1)} %get-tuple-element.31), channel_id=1, source_target_pairs={{0,4},{4,8},{8,12},{12,16},{16,20},{20,24},{24,28},{28,0},{1,5},{5... | collective-permute-start | bytes 393224 | tf_op jit(solution)/shard_map/ppermute | solution.py:699
  6.8 7.8 %collective-permute-start.1 = (f32[4,4,2048]{2,1,0:T(4,128)S(1)}, f32[4,4,2048]{2,1,0:T(4,128)S(1)}, u32[]{:S(2)}, u32[]{:S(2)}) collective-permute-start(f32[4,4,2048]{2,1,0:T(4,128)S(1)} %get-tuple-element.32), channel_id=1, source_target_pairs={{0,28},{4,0},{8,4},{12,8},{16,12},{20,16},{24,20},{28,24},{1,29},{... | collective-permute-start | bytes 393224 | tf_op jit(solution)/shard_map/ppermute | solution.py:699
  14.7 4.0 %collective-permute-start.2 = (f32[3,4,2048]{2,1,0:T(4,128)S(1)}, f32[3,4,2048]{2,1,0:T(4,128)S(1)}, u32[]{:S(2)}, u32[]{:S(2)}) collective-permute-start(f32[3,4,2048]{2,1,0:T(4,128)S(1)} %pad_maximum_fusion.3), channel_id=1, source_target_pairs={{0,1},{1,0},{2,3},{3,2},{4,5},{5,4},{6,7},{7,6},{8,9},{9,8},{10,11... | collective-permute-start | bytes 294920 | tf_op jit(solution)/shard_map/ppermute | solution.py:704
  14.8 5.7 %collective-permute-start.3 = (f32[3,4,2048]{2,1,0:T(4,128)S(1)}, f32[3,4,2048]{2,1,0:T(4,128)S(1)}, u32[]{:S(2)}, u32[]{:S(2)}) collective-permute-start(f32[3,4,2048]{2,1,0:T(4,128)S(1)} %pad_maximum_fusion.4), channel_id=1, source_target_pairs={{0,2},{1,3},{2,0},{3,1},{4,6},{5,7},{6,4},{7,5},{8,10},{9,11},{10,... | collective-permute-start | bytes 294920 | tf_op jit(solution)/shard_map/ppermute | solution.py:704
  16.4 5.3 %collective-permute-start.4 = (f32[3,4,2048]{2,1,0:T(4,128)S(1)}, f32[3,4,2048]{2,1,0:T(4,128)S(1)}, u32[]{:S(2)}, u32[]{:S(2)}) collective-permute-start(f32[3,4,2048]{2,1,0:T(4,128)S(1)} %pad_maximum_fusion.5), channel_id=1, source_target_pairs={{0,3},{1,2},{2,1},{3,0},{4,7},{5,6},{6,5},{7,4},{8,11},{9,10},{10,... | collective-permute-start | bytes 294920 | tf_op jit(solution)/shard_map/ppermute | solution.py:704
  16.8 4.8 %copy-start = (f32[19,32,512]{2,1,0:T(8,128)S(1)}, f32[19,32,512]{2,1,0:T(8,128)}, u32[]{:S(2)}) copy-start(f32[19,32,512]{2,1,0:T(8,128)} %refs_7_.1) | copy-start | bytes 3735556
  28.2 6.5 %collective-permute-start.5 = (f32[8,512]{1,0:T(8,128)S(1)}, f32[8,512]{1,0:T(8,128)S(1)}, u32[]{:S(2)}, u32[]{:S(2)}) collective-permute-start(f32[8,512]{1,0:T(8,128)S(1)} %get-tuple-element.37), channel_id=1, source_target_pairs={{0,4},{4,8},{8,12},{12,16},{16,20},{20,24},{24,28},{28,0},{1,5},{5... | collective-permute-start | bytes 49160 | tf_op jit(solution)/shard_map/ppermute | solution.py:699
  28.3 6.4 %collective-permute-start.6 = (f32[8,512]{1,0:T(8,128)S(1)}, f32[8,512]{1,0:T(8,128)S(1)}, u32[]{:S(2)}, u32[]{:S(2)}) collective-permute-start(f32[8,512]{1,0:T(8,128)S(1)} %get-tuple-element.38), channel_id=1, source_target_pairs={{0,28},{4,0},{8,4},{12,8},{16,12},{20,16},{24,20},{28,24},{1,29},{... | collective-permute-start | bytes 49160 | tf_op jit(solution)/shard_map/ppermute | solution.py:699
  34.7 3.3 %collective-permute-start.8 = (f32[48,128]{1,0:T(8,128)S(1)}, f32[48,128]{1,0:T(8,128)S(1)}, u32[]{:S(2)}, u32[]{:S(2)}) collective-permute-start(f32[48,128]{1,0:T(8,128)S(1)} %get-tuple-element.79), channel_id=1, source_target_pairs={{0,3},{1,2},{2,1},{3,0},{4,7},{5,6},{6,5},{7,4},{8,11},{9,10},{10,... | collective-permute-start | bytes 73736 | tf_op jit(solution)/shard_map/ppermute | solution.py:709
  34.8 3.2 %collective-permute-start.7 = (f32[48,128]{1,0:T(8,128)S(1)}, f32[48,128]{1,0:T(8,128)S(1)}, u32[]{:S(2)}, u32[]{:S(2)}) collective-permute-start(f32[48,128]{1,0:T(8,128)S(1)} %get-tuple-element.80), channel_id=1, source_target_pairs={{0,1},{1,0},{2,3},{3,2},{4,5},{5,4},{6,7},{7,6},{8,9},{9,8},{10,11... | collective-permute-start | bytes 73736 | tf_op jit(solution)/shard_map/ppermute | solution.py:704
  49.8 6.5 %collective-permute-start.9 = (f32[8,512]{1,0:T(8,128)S(1)}, f32[8,512]{1,0:T(8,128)S(1)}, u32[]{:S(2)}, u32[]{:S(2)}) collective-permute-start(f32[8,512]{1,0:T(8,128)S(1)} %get-tuple-element.45), channel_id=1, source_target_pairs={{0,4},{4,8},{8,12},{12,16},{16,20},{20,24},{24,28},{28,0},{1,5},{5... | collective-permute-start | bytes 49160 | tf_op jit(solution)/shard_map/ppermute | solution.py:699
  49.9 6.4 %collective-permute-start.10 = (f32[8,512]{1,0:T(8,128)S(1)}, f32[8,512]{1,0:T(8,128)S(1)}, u32[]{:S(2)}, u32[]{:S(2)}) collective-permute-start(f32[8,512]{1,0:T(8,128)S(1)} %get-tuple-element.46), channel_id=1, source_target_pairs={{0,28},{4,0},{8,4},{12,8},{16,12},{20,16},{24,20},{28,24},{1,29},{... | collective-permute-start | bytes 49160 | tf_op jit(solution)/shard_map/ppermute | solution.py:699
  56.3 3.3 %collective-permute-start.12 = (f32[48,128]{1,0:T(8,128)S(1)}, f32[48,128]{1,0:T(8,128)S(1)}, u32[]{:S(2)}, u32[]{:S(2)}) collective-permute-start(f32[48,128]{1,0:T(8,128)S(1)} %get-tuple-element.77), channel_id=1, source_target_pairs={{0,3},{1,2},{2,1},{3,0},{4,7},{5,6},{6,5},{7,4},{8,11},{9,10},{10,... | collective-permute-start | bytes 73736 | tf_op jit(solution)/shard_map/ppermute | solution.py:709
  56.4 3.2 %collective-permute-start.11 = (f32[48,128]{1,0:T(8,128)S(1)}, f32[48,128]{1,0:T(8,128)S(1)}, u32[]{:S(2)}, u32[]{:S(2)}) collective-permute-start(f32[48,128]{1,0:T(8,128)S(1)} %get-tuple-element.78), channel_id=1, source_target_pairs={{0,1},{1,0},{2,3},{3,2},{4,5},{5,4},{6,7},{7,6},{8,9},{9,8},{10,11... | collective-permute-start | bytes 73736 | tf_op jit(solution)/shard_map/ppermute | solution.py:704
  59.7 22.0 %copy-start.2 = (f32[24,3,642]{2,0,1:T(8,128)S(1)}, f32[24,3,642]{2,0,1:T(8,128)}, u32[]{:S(2)}) copy-start(f32[24,3,642]{2,0,1:T(8,128)} %param.7) | copy-start | bytes 554692
  59.7 22.0 %copy-start.4 = (s32[24]{0:T(128)S(1)}, s32[24]{0:T(128)}, u32[]{:S(2)}) copy-start(s32[24]{0:T(128)} %home_ref.1) | copy-start | bytes 292
  66.1 1.9 %collective-permute-start.13 = (f32[3,4,2048]{2,1,0:T(4,128)S(1)}, f32[3,4,2048]{2,1,0:T(4,128)S(1)}, u32[]{:S(2)}, u32[]{:S(2)}) collective-permute-start(f32[3,4,2048]{2,1,0:T(4,128)S(1)} %get-tuple-element.53), channel_id=1, source_target_pairs={{0,1},{1,0},{2,3},{3,2},{4,5},{5,4},{6,7},{7,6},{8,9},{9,8},{10,11... | collective-permute-start | bytes 294920 | tf_op jit(solution)/shard_map/ppermute | solution.py:704
  66.1 5.7 %collective-permute-start.14 = (f32[3,4,2048]{2,1,0:T(4,128)S(1)}, f32[3,4,2048]{2,1,0:T(4,128)S(1)}, u32[]{:S(2)}, u32[]{:S(2)}) collective-permute-start(f32[3,4,2048]{2,1,0:T(4,128)S(1)} %get-tuple-element.54), channel_id=1, source_target_pairs={{0,2},{1,3},{2,0},{3,1},{4,6},{5,7},{6,4},{7,5},{8,10},{9,11},{10,... | collective-permute-start | bytes 294920 | tf_op jit(solution)/shard_map/ppermute | solution.py:704
  66.2 6.7 %collective-permute-start.15 = (f32[3,4,2048]{2,1,0:T(4,128)S(1)}, f32[3,4,2048]{2,1,0:T(4,128)S(1)}, u32[]{:S(2)}, u32[]{:S(2)}) collective-permute-start(f32[3,4,2048]{2,1,0:T(4,128)S(1)} %get-tuple-element.55), channel_id=1, source_target_pairs={{0,3},{1,2},{2,1},{3,0},{4,7},{5,6},{6,5},{7,4},{8,11},{9,10},{10,... | collective-permute-start | bytes 294920 | tf_op jit(solution)/shard_map/ppermute | solution.py:704
  73.0 8.6 %collective-permute-start.16 = (f32[4,4,2048]{2,1,0:T(4,128)S(1)}, f32[4,4,2048]{2,1,0:T(4,128)S(1)}, u32[]{:S(2)}, u32[]{:S(2)}) collective-permute-start(f32[4,4,2048]{2,1,0:T(4,128)S(1)} %pad_maximum_fusion), channel_id=1, source_target_pairs={{0,4},{4,8},{8,12},{12,16},{16,20},{20,24},{24,28},{28,0},{1,5},{5... | collective-permute-start | bytes 393224 | tf_op jit(solution)/shard_map/ppermute | solution.py:699
  73.1 8.6 %collective-permute-start.17 = (f32[4,4,2048]{2,1,0:T(4,128)S(1)}, f32[4,4,2048]{2,1,0:T(4,128)S(1)}, u32[]{:S(2)}, u32[]{:S(2)}) collective-permute-start(f32[4,4,2048]{2,1,0:T(4,128)S(1)} %pad_maximum_fusion.1), channel_id=1, source_target_pairs={{0,28},{4,0},{8,4},{12,8},{16,12},{20,16},{24,20},{28,24},{1,29},{... | collective-permute-start | bytes 393224 | tf_op jit(solution)/shard_map/ppermute | solution.py:699
